TPU v7x, 256 devices: a whole 4x4x8 slice. The times are simulated.
256 devices in a mesh: gx: 4 (over y), gy: 32 (over x, z), layer: 2 (over core).
Axes of the slice: x: 4, y: 4, z: 8, core: 2. Of those that a mesh axis runs over, the one named last changes fastest.
Arguments:
- profiles: bfloat16 [2, 4, 524288, 256], P('layer', 'gx', 'gy'), may hold values from 0.049804688 to 2
- time_weight: bfloat16 [256], replicated, may hold values from 0 to 0.029907227
- slot_cell: int32 [2, 4, 524288], P('layer', 'gx', 'gy'), may hold values from 0 to 65535
- inst_count: int32 [2, 4, 32], P('layer', 'gx', 'gy'), may hold values from 1 to 16384, as said below
- metal: float32 [6, 512, 16384], P('layer', 'gx', 'gy'), may hold values from 0.5 to 4
- via_density: float32 [512, 16384], P('gx', 'gy'), may hold values from 0.5 to 4
- pad: float32 [512, 16384], P('gx', 'gy'), may hold values from 0.05 to 0.5
- start_drop: float32 [6, 512, 16384], P('layer', 'gx', 'gy'), may hold values from 0 to 1
Outputs:
- drop: float32 [6, 512, 16384], P('layer', 'gx', 'gy')
- residual: float32 [6, 512, 16384], P('layer', 'gx', 'gy')
Inputs may be any that keep to these rules, and one draw needn't show every extreme that they name: The first inst_count slots of a device are live, the rest are padding; and one device is full in every draw. `slot_cell`: row-major cell index within the tile of 128 x 512 cells.
All inputs are finite; a program needn't handle non-finite values.
Results may differ from a plain program's by a relative error of at most 0.0018.
Values sent between devices are 32-bit elements; how exact they have to be, the bound alone decides.
No kernel may reach another device: no remote copies, remote signals or barrier semaphores. Data moves between devices by JAX's collectives and lax.ppermute only.
A program may use at most 64 MiB of HBM per device.

v0:
```python
import jax
import jax.numpy as jnp
from jax import lax
from jax.sharding import Mesh
from jax.sharding import PartitionSpec as P

BLOCK = 512
ITERS = 3
GX_GY_LAYER = ("gx", "gy_0", "gy_1", "layer")
GY = ("gy_0", "gy_1")


def over_axes(shard, axes):
    for axis in axes:
        shard = lax.psum(shard, axis)
    return shard


def from_behind(value, axis, steps):
    count = lax.axis_size(axis)
    first, last = (max(0, -steps), min(count, count - steps))
    return lax.ppermute(value, axis, [(source, source + steps) for source in range(first, last)])


def padded(shard, sides, width):
    edges = {}
    for axis, dim in sides:
        devices, length = (lax.axis_size(axis), shard.shape[dim])
        up = [(i, (i + 1) % devices) for i in range(devices - 1)]
        last = lax.slice_in_dim(shard, length - width, length, axis=dim)
        first = lax.slice_in_dim(shard, 0, width, axis=dim)
        edges[dim] = (
            lax.ppermute(last, axis, up),
            lax.ppermute(first, axis, [(b, a) for a, b in up]),
        )
    done = []
    for _, dim in sides:
        low, high = edges[dim]
        around = [(width, width) if d in done else (0, 0) for d in range(shard.ndim)]
        shard = jnp.concatenate([jnp.pad(low, around), shard, jnp.pad(high, around)], axis=dim)
        done.append(dim)
    return shard


def harmonic(values, beside):
    return 2.0 * values * beside / (values + beside)


def links(extended, via_column):
    middle = extended[1:-1, 1:-1, 1:-1]
    east_link = harmonic(middle, extended[1:-1, 2:, 1:-1])
    west_link = harmonic(middle, extended[1:-1, :-2, 1:-1])
    north_link = harmonic(middle, extended[1:-1, 1:-1, 2:])
    south_link = harmonic(middle, extended[1:-1, 1:-1, :-2])
    upper_link = via_column * harmonic(middle, extended[2:, 1:-1, 1:-1])
    lower_link = via_column * harmonic(middle, extended[:-2, 1:-1, 1:-1])
    return (east_link, west_link, north_link, south_link, upper_link, lower_link)


def diagonal_of(conduct):
    east_link, west_link, north_link, south_link, upper_link, lower_link = conduct
    return east_link + west_link + north_link + south_link + upper_link + lower_link


def operate(field, extended, conduct, diagonal):
    east_link, west_link, north_link, south_link, upper_link, lower_link = conduct
    result = (
        diagonal * field
        - east_link * extended[1:-1, 2:, 1:-1]
        - west_link * extended[1:-1, :-2, 1:-1]
    )
    result = result - north_link * extended[1:-1, 1:-1, 2:] - south_link * extended[1:-1, 1:-1, :-2]
    return result - upper_link * extended[2:, 1:-1, 1:-1] - lower_link * extended[:-2, 1:-1, 1:-1]


def both_sums(residual, scaled, image):
    return (
        over_axes(jnp.sum(residual * scaled), GX_GY_LAYER),
        over_axes(jnp.sum(scaled * image), GX_GY_LAYER),
    )


def solve(apply, diagonal, rhs, start):
    solution = start
    residual = rhs - apply(start)
    scaled = residual / diagonal
    image = apply(scaled)
    energy, curvature = both_sums(residual, scaled, image)
    step_size = energy / curvature
    direction, along = (scaled, image)
    for iteration in range(ITERS):
        solution = solution + step_size * direction
        residual = residual - step_size * along
        if iteration + 1 < ITERS:
            scaled = residual / diagonal
            image = apply(scaled)
            energy_next, curvature = both_sums(residual, scaled, image)
            momentum = energy_next / energy
            step_size = energy_next / (curvature - momentum * energy_next / step_size)
            direction = scaled + momentum * direction
            along = image + momentum * along
            energy = energy_next
    return (solution, residual)


def per_device(profiles, time_weight, slot_cell, inst_count, metal, via_density, pad, start_drop):
    tile_rows, tile_cols = (metal.shape[1], metal.shape[2])
    slot_current = jnp.dot(
        profiles.reshape(-1, profiles.shape[-1]), time_weight, preferred_element_type=jnp.float32
    )
    slot_cells = slot_cell.reshape(-1)
    live_count = inst_count.reshape(())
    positions = jnp.arange(slot_cells.shape[0], dtype=jnp.int32)
    slot_current = jnp.where(positions < live_count, slot_current, 0.0)
    block_rows = min(BLOCK, slot_cells.shape[0])
    blocks_live = (live_count + block_rows - 1) // block_rows
    row_ids = jnp.arange(tile_rows, dtype=jnp.int32)
    col_ids = jnp.arange(tile_cols, dtype=jnp.int32)

    def add_block(block_index, total):
        first = block_index * block_rows
        cells = lax.dynamic_slice_in_dim(slot_cells, first, block_rows)
        amounts = lax.dynamic_slice_in_dim(slot_current, first, block_rows)
        left = jnp.where(cells[:, None] // tile_cols == row_ids[None, :], amounts[:, None], 0.0)
        left_high = left.astype(jnp.bfloat16)
        left_low = (left - left_high.astype(jnp.float32)).astype(jnp.bfloat16)
        right = (cells[:, None] % tile_cols == col_ids[None, :]).astype(jnp.bfloat16)
        dims = (((0,), (0,)), ((), ()))
        upper_part = lax.dot_general(left_high, right, dims, preferred_element_type=jnp.float32)
        lower_part = lax.dot_general(left_low, right, dims, preferred_element_type=jnp.float32)
        return total + (upper_part + lower_part)

    partial_value = lax.fori_loop(
        0, blocks_live, add_block, jnp.zeros((tile_rows, tile_cols), jnp.float32)
    )
    others = from_behind(partial_value, "layer", -1)
    bottom = lax.axis_index("layer") == 0
    current = jnp.where(bottom, partial_value + others, 0.0)
    rhs = jnp.zeros_like(metal).at[0].set(current)
    extended = padded(metal, (("gx", 1), (GY, 2), ("layer", 0)), 1)
    conduct = links(extended, via_density[None])
    top = lax.axis_index("layer") == lax.axis_size("layer") - 1
    diagonal = diagonal_of(conduct).at[-1].add(jnp.where(top, pad, 0.0))

    def apply(field):
        rims = padded(field, (("gx", 1), (GY, 2), ("layer", 0)), 1)
        return operate(field, rims, conduct, diagonal)

    solution, residual = solve(apply, diagonal, rhs, start_drop)
    return (solution, residual)


def solution(mesh):
    split = Mesh(
        mesh.devices.reshape(mesh.shape["gx"], 4, 8, mesh.shape["layer"]),
        ("gx", "gy_0", "gy_1", "layer"),
    )
    return jax.shard_map(
        per_device,
        mesh=split,
        in_specs=(
            P("layer", "gx", GY, None),
            P(),
            P("layer", "gx", GY),
            P("layer", "gx", GY),
            P("layer", "gx", GY),
            P("gx", GY),
            P("gx", GY),
            P("layer", "gx", GY),
        ),
        out_specs=(P("layer", "gx", GY), P("layer", "gx", GY)),
        check_vma=False,
    )
```

profile of v0, /device:TPU:1, one launch (start us, length us, event | category | flops | bytes accessed | tf_op | source)
XLA Modules:
  0.0 361.7 jit_solution(13540631876954959527)
XLA Ops:
  2.5 4.4 %collective-permute-start.10 = (f32[3,128,1]{2,1,0:T(8,128)}, f32[3,128,1]{2,1,0:T(8,128)S(1)}, u32[]{:S(2)}, u32[]{:S(2)}) collective-permute-start(f32[3,128,1]{2,1,0:T(8,128)} %get-tuple-element.210), channel_id=1, source_target_pairs={{0,2},{2,4},{4,6},{6,8},{8,10},{10,12},{12,14},{14,16},{16,18},{18... | collective-permute-start | bytes 4616 | tf_op jit(solution)/shard_map/ppermute | solution.py:33
  9.3 4.2 %collective-permute-start.4 = (f32[3,128,1]{2,1,0:T(8,128)S(1)}, f32[3,128,1]{2,1,0:T(8,128)S(1)}, u32[]{:S(2)}, u32[]{:S(2)}) collective-permute-start(f32[3,128,1]{2,1,0:T(8,128)S(1)} %get-tuple-element.216), channel_id=1, source_target_pairs={{0,2},{2,4},{4,6},{6,8},{8,10},{10,12},{12,14},{14,16},{16,18},{18... | collective-permute-start | bytes 4616 | tf_op jit(solution)/shard_map/ppermute | solution.py:33
  15.8 3.3 collective-permute-start.5
  22.3 5.7 %fusion.19 = f32[1,16384]{1,0:T(1,128)S(1)} fusion(bf16[256,1]{0,1:T(2,128)(2,1)S(1)} %reshape.111, bf16[1,1,16384,256]{3,2,1,0:T(8,128)(2,1)} %param.14), kind=kOutput, calls=%fused_computation.28 | convolution fusion | flops 8388608 | bytes 8454656 | tf_op jit(solution)/shard_map/dot_general | solution.py:108
  28.1 10.6 %while.15 = (s32[]{:T(128)}, f32[128,512]{1,0:T(8,128)S(1)}, s32[]{:T(128)}, s32[16384]{0:T(1024)}, f32[16384]{0:T(1024)S(1)}, /*index=5*/s32[]{:T(128)}, s32[]{:T(128)}, s32[]{:T(128)}, s32[]{:T(128)}) while((s32[]{:T(128)}, f32[128,512]{1,0:T(8,128)S(1)}, s32[]{:T(128)}, s32[16384]{0:T(1024)}, f32[16384]{0:T(1024)S(1)}, ...), condition=%wide.region_1.2_spmd.clone, body=%wide.region_0.1_spmd.clone.sunk | while | flops 135407104 | bytes 1071251 | solution.py:133
  38.7 5.3 %collective-permute-start.2 = (f32[3,1,512]{2,1,0:T(1,128)S(1)}, f32[3,1,512]{2,1,0:T(1,128)S(1)}, u32[]{:S(2)}, u32[]{:S(2)}) collective-permute-start(f32[3,1,512]{2,1,0:T(1,128)S(1)} %get-tuple-element.218), channel_id=1, source_target_pairs={{0,64},{64,128},{128,192},{1,65},{65,129},{129,193},{2,66},{66,130... | collective-permute-start | bytes 18440 | tf_op jit(solution)/shard_map/ppermute | solution.py:33
  47.6 6.4 %collective-permute-done.3 = f32[3,128,1]{2,1,0:T(8,128)S(1)} collective-permute-done((f32[3,128,1]{2,1,0:T(8,128)S(1)}, f32[3,128,1]{2,1,0:T(8,128)S(1)}, u32[]{:S(2)}, u32[]{:S(2)}) %collective-permute-start.3) | collective-permute-done | bytes 1568 | tf_op jit(solution)/shard_map/ppermute | solution.py:34
  54.0 4.2 %collective-permute-start.8 = (f32[3,1,512]{2,1,0:T(1,128)S(1)}, f32[3,1,512]{2,1,0:T(1,128)S(1)}, u32[]{:S(2)}, u32[]{:S(2)}) collective-permute-start(f32[3,1,512]{2,1,0:T(1,128)S(1)} %get-tuple-element.212), channel_id=1, source_target_pairs={{0,64},{64,128},{128,192},{1,65},{65,129},{129,193},{2,66},{66,130... | collective-permute-start | bytes 18440 | tf_op jit(solution)/shard_map/ppermute | solution.py:33
  65.6 3.4 add_add_fusion
  70.2 5.7 %fusion.93 = (f32[3,128,512]{2,1,0:T(8,128)S(1)}, f32[3,128,512]{2,1,0:T(8,128)S(1)}) fusion(f32[3,128,512]{2,1,0:T(8,128)S(1)} %fusion.86, f32[3,128,512]{2,1,0:T(8,128)S(1)} %get-tuple-element.187, f32[3,130,1]{2,1,0:T(8,128)S(1)} %pad.71, f32[3,1,512]{2,1,0:T(1,128)S(1)} %collective-permute-done.7, f32[3,128,512]{2,1,0:T(8,128)} %param.21, ...), kind=kLoop, calls=%fused_computation.210 | loop fusion | flops 11796480 | bytes 6322272 | tf_op jit(solution)/shard_map/div | solution.py:86
  79.4 4.3 %collective-permute-start.14 = (f32[3,1,512]{2,1,0:T(1,128)S(1)}, f32[3,1,512]{2,1,0:T(1,128)S(1)}, u32[]{:S(2)}, u32[]{:S(2)}) collective-permute-start(f32[3,1,512]{2,1,0:T(1,128)S(1)} %get-tuple-element.206), channel_id=1, source_target_pairs={{0,64},{64,128},{128,192},{1,65},{65,129},{129,193},{2,66},{66,130... | collective-permute-start | bytes 18440 | tf_op jit(solution)/shard_map/ppermute | solution.py:33
  85.1 6.8 %collective-permute-start.16 = (f32[3,128,1]{2,1,0:T(8,128)S(1)}, f32[3,128,1]{2,1,0:T(8,128)S(1)}, u32[]{:S(2)}, u32[]{:S(2)}) collective-permute-start(f32[3,128,1]{2,1,0:T(8,128)S(1)} %get-tuple-element.204), channel_id=1, source_target_pairs={{0,2},{2,4},{4,6},{6,8},{8,10},{10,12},{12,14},{14,16},{16,18},{18... | collective-permute-start | bytes 4616 | tf_op jit(solution)/shard_map/ppermute | solution.py:33
  95.8 8.7 %collective-permute-done.15 = f32[3,128,1]{2,1,0:T(8,128)S(1)} collective-permute-done((f32[3,128,1]{2,1,0:T(8,128)S(1)}, f32[3,128,1]{2,1,0:T(8,128)S(1)}, u32[]{:S(2)}, u32[]{:S(2)}) %collective-permute-start.15) | collective-permute-done | bytes 1568 | tf_op jit(solution)/shard_map/ppermute | solution.py:34
  104.6 4.9 %multiply_reduce_fusion.4 = (f32[]{:T(128)}, f32[]{:T(128)}, f32[3,128,512]{2,1,0:T(8,128)}) fusion(f32[3,128,512]{2,1,0:T(8,128)S(1)} %get-tuple-element.183, f32[3,128,512]{2,1,0:T(8,128)S(1)} %get-tuple-element.184, f32[3,128,512]{2,1,0:T(8,128)S(1)} %get-tuple-element.187, f32[3,130,1]{2,1,0:T(8,128)S(1)} %pad.75, ...), kind=kLoop, calls=%fused_computation.196 | loop fusion | flops 12189694 | bytes 6060136 | tf_op jit(solution)/shard_map/reduce_sum | solution.py:79
  109.4 8.6 %all-reduce.29 = (f32[]{:T(128)}, f32[]{:T(128)}) all-reduce(f32[]{:T(128)} %get-tuple-element.141, f32[]{:T(128)} %get-tuple-element.140), channel_id=1, replica_groups=mesh['gx'=4,'gy_0'=4,'gy_1'=8,'layer'=2] {'gx'}, use_global_device_ids=true, to_apply=%region_3.4 | all-reduce | flops 2 | bytes 16 | tf_op jit(solution)/shard_map/psum | solution.py:15
  118.1 51.7 %all-reduce.26 = (f32[]{:T(128)}, f32[]{:T(128)}) all-reduce(f32[]{:T(128)} %get-tuple-element.168, f32[]{:T(128)} %get-tuple-element.169), channel_id=1, replica_groups=mesh['gx'=4,'gy_0'=4,'gy_1'=8,'layer'=2] {'gy_0'}, use_global_device_ids=true, to_apply=%region_4.5 | all-reduce | flops 2 | bytes 16 | tf_op jit(solution)/shard_map/psum | solution.py:15
  169.8 19.4 %all-reduce.23 = (f32[]{:T(128)}, f32[]{:T(128)}) all-reduce(f32[]{:T(128)} %get-tuple-element.162, f32[]{:T(128)} %get-tuple-element.163), channel_id=1, replica_groups=mesh['gx'=4,'gy_0'=4,'gy_1'=8,'layer'=2] {'gy_1'}, use_global_device_ids=true, to_apply=%region_5.6 | all-reduce | flops 2 | bytes 16 | tf_op jit(solution)/shard_map/psum | solution.py:15
  189.2 13.8 %all-reduce.32 = (f32[]{:T(128)}, f32[]{:T(128)}) all-reduce(f32[]{:T(128)} %get-tuple-element.156, f32[]{:T(128)} %get-tuple-element.157), channel_id=1, replica_groups=mesh['gx'=4,'gy_0'=4,'gy_1'=8,'layer'=2] {'layer'}, use_global_device_ids=true, to_apply=%region_6.7 | all-reduce | flops 2 | bytes 16 | tf_op jit(solution)/shard_map/psum | solution.py:15
  213.4 2.9 collective-permute-start.22
  220.4 5.8 %collective-permute-done.21 = f32[3,128,1]{2,1,0:T(8,128)S(1)} collective-permute-done((f32[3,128,1]{2,1,0:T(8,128)S(1)}, f32[3,128,1]{2,1,0:T(8,128)S(1)}, u32[]{:S(2)}, u32[]{:S(2)}) %collective-permute-start.21) | collective-permute-done | bytes 1568 | tf_op jit(solution)/shard_map/ppermute | solution.py:34
  226.3 5.8 %multiply_reduce_fusion.2 = (f32[]{:T(128)}, f32[]{:T(128)}, f32[3,128,512]{2,1,0:T(8,128)}) fusion(f32[3,128,512]{2,1,0:T(8,128)S(1)} %get-tuple-element.180, f32[3,128,512]{2,1,0:T(8,128)S(1)} %get-tuple-element.181, f32[3,128,512]{2,1,0:T(8,128)S(1)} %get-tuple-element.187, f32[3,130,1]{2,1,0:T(8,128)S(1)} %pad.79, ...), kind=kLoop, calls=%fused_computation.193 | loop fusion | flops 12189694 | bytes 6060136 | tf_op jit(solution)/shard_map/reduce_sum | solution.py:79
  232.0 8.3 %all-reduce.28 = (f32[]{:T(128)}, f32[]{:T(128)}) all-reduce(f32[]{:T(128)} %get-tuple-element.139, f32[]{:T(128)} %get-tuple-element.138), channel_id=1, replica_groups=mesh['gx'=4,'gy_0'=4,'gy_1'=8,'layer'=2] {'gx'}, use_global_device_ids=true, to_apply=%region_13.14 | all-reduce | flops 2 | bytes 16 | tf_op jit(solution)/shard_map/psum | solution.py:15
  240.3 8.7 %all-reduce.25 = (f32[]{:T(128)}, f32[]{:T(128)}) all-reduce(f32[]{:T(128)} %get-tuple-element.166, f32[]{:T(128)} %get-tuple-element.167), channel_id=1, replica_groups=mesh['gx'=4,'gy_0'=4,'gy_1'=8,'layer'=2] {'gy_0'}, use_global_device_ids=true, to_apply=%region_14.15 | all-reduce | flops 2 | bytes 16 | tf_op jit(solution)/shard_map/psum | solution.py:15
  249.0 13.1 %all-reduce.22 = (f32[]{:T(128)}, f32[]{:T(128)}) all-reduce(f32[]{:T(128)} %get-tuple-element.160, f32[]{:T(128)} %get-tuple-element.161), channel_id=1, replica_groups=mesh['gx'=4,'gy_0'=4,'gy_1'=8,'layer'=2] {'gy_1'}, use_global_device_ids=true, to_apply=%region_15.16 | all-reduce | flops 2 | bytes 16 | tf_op jit(solution)/shard_map/psum | solution.py:15
  262.1 14.3 %all-reduce.31 = (f32[]{:T(128)}, f32[]{:T(128)}) all-reduce(f32[]{:T(128)} %get-tuple-element.154, f32[]{:T(128)} %get-tuple-element.155), channel_id=1, replica_groups=mesh['gx'=4,'gy_0'=4,'gy_1'=8,'layer'=2] {'layer'}, use_global_device_ids=true, to_apply=%region_16.17 | all-reduce | flops 2 | bytes 16 | tf_op jit(solution)/shard_map/psum | solution.py:15
  294.8 6.0 %collective-permute-done.27 = f32[3,128,1]{2,1,0:T(8,128)S(1)} collective-permute-done((f32[3,128,1]{2,1,0:T(8,128)S(1)}, f32[3,128,1]{2,1,0:T(8,128)S(1)}, u32[]{:S(2)}, u32[]{:S(2)}) %collective-permute-start.27) | collective-permute-done | bytes 1568 | tf_op jit(solution)/shard_map/ppermute | solution.py:34
  300.9 5.7 %multiply_reduce_fusion = (f32[]{:T(128)}, f32[]{:T(128)}, f32[3,128,512]{2,1,0:T(8,128)}) fusion(f32[3,128,512]{2,1,0:T(8,128)S(1)} %get-tuple-element.177, f32[3,128,512]{2,1,0:T(8,128)S(1)} %get-tuple-element.178, f32[3,128,512]{2,1,0:T(8,128)S(1)} %get-tuple-element.187, f32[3,130,1]{2,1,0:T(8,128)S(1)} %pad.83, ...), kind=kLoop, calls=%fused_computation.189 | loop fusion | flops 12189694 | bytes 6060136 | tf_op jit(solution)/shard_map/reduce_sum | solution.py:79
  306.7 8.2 %all-reduce.27 = (f32[]{:T(128)}, f32[]{:T(128)}) all-reduce(f32[]{:T(128)} %get-tuple-element.137, f32[]{:T(128)} %get-tuple-element.136), channel_id=1, replica_groups=mesh['gx'=4,'gy_0'=4,'gy_1'=8,'layer'=2] {'gx'}, use_global_device_ids=true, to_apply=%region_23.24 | all-reduce | flops 2 | bytes 16 | tf_op jit(solution)/shard_map/psum | solution.py:15
  314.9 11.8 %all-reduce.24 = (f32[]{:T(128)}, f32[]{:T(128)}) all-reduce(f32[]{:T(128)} %get-tuple-element.164, f32[]{:T(128)} %get-tuple-element.165), channel_id=1, replica_groups=mesh['gx'=4,'gy_0'=4,'gy_1'=8,'layer'=2] {'gy_0'}, use_global_device_ids=true, to_apply=%region_24.25 | all-reduce | flops 2 | bytes 16 | tf_op jit(solution)/shard_map/psum | solution.py:15
  326.7 12.3 %all-reduce.21 = (f32[]{:T(128)}, f32[]{:T(128)}) all-reduce(f32[]{:T(128)} %get-tuple-element.158, f32[]{:T(128)} %get-tuple-element.159), channel_id=1, replica_groups=mesh['gx'=4,'gy_0'=4,'gy_1'=8,'layer'=2] {'gy_1'}, use_global_device_ids=true, to_apply=%region_25.26 | all-reduce | flops 2 | bytes 16 | tf_op jit(solution)/shard_map/psum | solution.py:15
  339.0 14.0 %all-reduce.30 = (f32[]{:T(128)}, f32[]{:T(128)}) all-reduce(f32[]{:T(128)} %get-tuple-element.152, f32[]{:T(128)} %get-tuple-element.153), channel_id=1, replica_groups=mesh['gx'=4,'gy_0'=4,'gy_1'=8,'layer'=2] {'layer'}, use_global_device_ids=true, to_apply=%region_26.27 | all-reduce | flops 2 | bytes 16 | tf_op jit(solution)/shard_map/psum | solution.py:15
  357.0 4.7 %multiply_subtract_fusion = (f32[3,128,512]{2,1,0:T(8,128)}, f32[3,128,512]{2,1,0:T(8,128)}) fusion(f32[3,128,512]{2,1,0:T(8,128)} %copy-done.7, f32[3,128,512]{2,1,0:T(8,128)} %get-tuple-element.176, f32[]{:T(128)S(6)} %div.84, f32[]{:T(128)S(6)} %div.86, f32[3,128,512]{2,1,0:T(8,128)} %get-tuple-element.179, f32[3,128,512]{2,1,0:T(8,128)} %get-tuple-element.182, ...), kind=kLoop, calls=%fused_computation.187 | loop fusion | flops 3145728 | bytes 7864340 | tf_op jit(solution)/shard_map/sub | solution.py:93
  (126 shorter events, 67.6 us)
Async XLA Ops:
  2.5 36.3 %collective-permute-start.10 = (f32[3,128,1]{2,1,0:T(8,128)}, f32[3,128,1]{2,1,0:T(8,128)S(1)}, u32[]{:S(2)}, u32[]{:S(2)}) collective-permute-start(f32[3,128,1]{2,1,0:T(8,128)} %get-tuple-element.210), channel_id=1, source_target_pairs={{0,2},{2,4},{4,6},{6,8},{8,10},{10,12},{12,14},{14,16},{16,18},{18... | collective-permute-start | bytes 4616 | tf_op jit(solution)/shard_map/ppermute | solution.py:33
  6.8 37.2 %collective-permute-start.9 = (f32[3,128,1]{2,1,0:T(8,128)S(1)}, f32[3,128,1]{2,1,0:T(8,128)S(1)}, u32[]{:S(2)}, u32[]{:S(2)}) collective-permute-start(f32[3,128,1]{2,1,0:T(8,128)S(1)} %get-tuple-element.211), channel_id=1, source_target_pairs={{2,0},{4,2},{6,4},{8,6},{10,8},{12,10},{14,12},{16,14},{18,16},{20... | collective-permute-start | bytes 4616 | tf_op jit(solution)/shard_map/ppermute | solution.py:34
  9.3 36.1 %collective-permute-start.4 = (f32[3,128,1]{2,1,0:T(8,128)S(1)}, f32[3,128,1]{2,1,0:T(8,128)S(1)}, u32[]{:S(2)}, u32[]{:S(2)}) collective-permute-start(f32[3,128,1]{2,1,0:T(8,128)S(1)} %get-tuple-element.216), channel_id=1, source_target_pairs={{0,2},{2,4},{4,6},{6,8},{8,10},{10,12},{12,14},{14,16},{16,18},{18... | collective-permute-start | bytes 4616 | tf_op jit(solution)/shard_map/ppermute | solution.py:33
  14.5 47.8 %collective-permute-start.6 = (f32[1,128,512]{2,1,0:T(8,128)S(1)}, f32[1,128,512]{2,1,0:T(8,128)S(1)}, u32[]{:S(2)}, u32[]{:S(2)}) collective-permute-start(f32[1,128,512]{2,1,0:T(8,128)S(1)} %get-tuple-element.214), channel_id=1, source_target_pairs={{0,1},{2,3},{4,5},{6,7},{8,9},{10,11},{12,13},{14,15},{16,17},{18,... | collective-permute-start | bytes 786440 | tf_op jit(solution)/shard_map/ppermute | solution.py:33
  15.8 47.8 %collective-permute-start.5 = (f32[1,128,512]{2,1,0:T(8,128)S(1)}, f32[1,128,512]{2,1,0:T(8,128)S(1)}, u32[]{:S(2)}, u32[]{:S(2)}) collective-permute-start(f32[1,128,512]{2,1,0:T(8,128)S(1)} %get-tuple-element.215), channel_id=1, source_target_pairs={{1,0},{3,2},{5,4},{7,6},{9,8},{11,10},{13,12},{15,14},{17,16},{19,... | collective-permute-start | bytes 786440 | tf_op jit(solution)/shard_map/ppermute | solution.py:34
  38.7 19.5 %collective-permute-start.2 = (f32[3,1,512]{2,1,0:T(1,128)S(1)}, f32[3,1,512]{2,1,0:T(1,128)S(1)}, u32[]{:S(2)}, u32[]{:S(2)}) collective-permute-start(f32[3,1,512]{2,1,0:T(1,128)S(1)} %get-tuple-element.218), channel_id=1, source_target_pairs={{0,64},{64,128},{128,192},{1,65},{65,129},{129,193},{2,66},{66,130... | collective-permute-start | bytes 18440 | tf_op jit(solution)/shard_map/ppermute | solution.py:33
  44.1 15.5 %collective-permute-start.1 = (f32[3,1,512]{2,1,0:T(1,128)S(1)}, f32[3,1,512]{2,1,0:T(1,128)S(1)}, u32[]{:S(2)}, u32[]{:S(2)}) collective-permute-start(f32[3,1,512]{2,1,0:T(1,128)S(1)} %get-tuple-element.219), channel_id=1, source_target_pairs={{64,0},{128,64},{192,128},{65,1},{129,65},{193,129},{66,2},{130,66... | collective-permute-start | bytes 18440 | tf_op jit(solution)/shard_map/ppermute | solution.py:34
  45.4 8.7 %collective-permute-start.3 = (f32[3,128,1]{2,1,0:T(8,128)S(1)}, f32[3,128,1]{2,1,0:T(8,128)S(1)}, u32[]{:S(2)}, u32[]{:S(2)}) collective-permute-start(f32[3,128,1]{2,1,0:T(8,128)S(1)} %get-tuple-element.217), channel_id=1, source_target_pairs={{2,0},{4,2},{6,4},{8,6},{10,8},{12,10},{14,12},{16,14},{18,16},{20... | collective-permute-start | bytes 4616 | tf_op jit(solution)/shard_map/ppermute | solution.py:34
  54.0 16.1 %collective-permute-start.8 = (f32[3,1,512]{2,1,0:T(1,128)S(1)}, f32[3,1,512]{2,1,0:T(1,128)S(1)}, u32[]{:S(2)}, u32[]{:S(2)}) collective-permute-start(f32[3,1,512]{2,1,0:T(1,128)S(1)} %get-tuple-element.212), channel_id=1, source_target_pairs={{0,64},{64,128},{128,192},{1,65},{65,129},{129,193},{2,66},{66,130... | collective-permute-start | bytes 18440 | tf_op jit(solution)/shard_map/ppermute | solution.py:33
  58.3 11.9 %collective-permute-start.7 = (f32[3,1,512]{2,1,0:T(1,128)S(1)}, f32[3,1,512]{2,1,0:T(1,128)S(1)}, u32[]{:S(2)}, u32[]{:S(2)}) collective-permute-start(f32[3,1,512]{2,1,0:T(1,128)S(1)} %get-tuple-element.213), channel_id=1, source_target_pairs={{64,0},{128,64},{192,128},{65,1},{129,65},{193,129},{66,2},{130,66... | collective-permute-start | bytes 18440 | tf_op jit(solution)/shard_map/ppermute | solution.py:34
  59.6 10.5 %collective-permute-start = (f32[128,512]{1,0:T(8,128)S(1)}, f32[128,512]{1,0:T(8,128)S(1)}, u32[]{:S(2)}, u32[]{:S(2)}) collective-permute-start(f32[128,512]{1,0:T(8,128)S(1)} %get-tuple-element.121), channel_id=1, source_target_pairs={{1,0},{3,2},{5,4},{7,6},{9,8},{11,10},{13,12},{15,14},{17,16},{19,... | collective-permute-start | bytes 786440 | tf_op jit(solution)/shard_map/ppermute | solution.py:22
  62.3 7.8 %collective-permute-start.11 = (f32[1,128,512]{2,1,0:T(8,128)}, f32[1,128,512]{2,1,0:T(8,128)S(1)}, u32[]{:S(2)}, u32[]{:S(2)}) collective-permute-start(f32[1,128,512]{2,1,0:T(8,128)} %get-tuple-element.208), channel_id=1, source_target_pairs={{1,0},{3,2},{5,4},{7,6},{9,8},{11,10},{13,12},{15,14},{17,16},{19,... | collective-permute-start | bytes 786440 | tf_op jit(solution)/shard_map/ppermute | solution.py:34
  64.4 5.8 %collective-permute-start.12 = (f32[1,128,512]{2,1,0:T(8,128)}, f32[1,128,512]{2,1,0:T(8,128)S(1)}, u32[]{:S(2)}, u32[]{:S(2)}) collective-permute-start(f32[1,128,512]{2,1,0:T(8,128)} %get-tuple-element.209), channel_id=1, source_target_pairs={{0,1},{2,3},{4,5},{6,7},{8,9},{10,11},{12,13},{14,15},{16,17},{18,... | collective-permute-start | bytes 786440 | tf_op jit(solution)/shard_map/ppermute | solution.py:33
  76.0 28.6 %collective-permute-start.17 = (f32[1,128,512]{2,1,0:T(8,128)S(1)}, f32[1,128,512]{2,1,0:T(8,128)S(1)}, u32[]{:S(2)}, u32[]{:S(2)}) collective-permute-start(f32[1,128,512]{2,1,0:T(8,128)S(1)} %get-tuple-element.202), channel_id=1, source_target_pairs={{1,0},{3,2},{5,4},{7,6},{9,8},{11,10},{13,12},{15,14},{17,16},{19,... | collective-permute-start | bytes 786440 | tf_op jit(solution)/shard_map/ppermute | solution.py:34
  78.1 26.5 %collective-permute-start.18 = (f32[1,128,512]{2,1,0:T(8,128)S(1)}, f32[1,128,512]{2,1,0:T(8,128)S(1)}, u32[]{:S(2)}, u32[]{:S(2)}) collective-permute-start(f32[1,128,512]{2,1,0:T(8,128)S(1)} %get-tuple-element.203), channel_id=1, source_target_pairs={{0,1},{2,3},{4,5},{6,7},{8,9},{10,11},{12,13},{14,15},{16,17},{18,... | collective-permute-start | bytes 786440 | tf_op jit(solution)/shard_map/ppermute | solution.py:33
  79.4 25.1 %collective-permute-start.14 = (f32[3,1,512]{2,1,0:T(1,128)S(1)}, f32[3,1,512]{2,1,0:T(1,128)S(1)}, u32[]{:S(2)}, u32[]{:S(2)}) collective-permute-start(f32[3,1,512]{2,1,0:T(1,128)S(1)} %get-tuple-element.206), channel_id=1, source_target_pairs={{0,64},{64,128},{128,192},{1,65},{65,129},{129,193},{2,66},{66,130... | collective-permute-start | bytes 18440 | tf_op jit(solution)/shard_map/ppermute | solution.py:33
  83.7 20.9 %collective-permute-start.13 = (f32[3,1,512]{2,1,0:T(1,128)S(1)}, f32[3,1,512]{2,1,0:T(1,128)S(1)}, u32[]{:S(2)}, u32[]{:S(2)}) collective-permute-start(f32[3,1,512]{2,1,0:T(1,128)S(1)} %get-tuple-element.207), channel_id=1, source_target_pairs={{64,0},{128,64},{192,128},{65,1},{129,65},{193,129},{66,2},{130,66... | collective-permute-start | bytes 18440 | tf_op jit(solution)/shard_map/ppermute | solution.py:34
  85.1 9.4 %collective-permute-start.16 = (f32[3,128,1]{2,1,0:T(8,128)S(1)}, f32[3,128,1]{2,1,0:T(8,128)S(1)}, u32[]{:S(2)}, u32[]{:S(2)}) collective-permute-start(f32[3,128,1]{2,1,0:T(8,128)S(1)} %get-tuple-element.204), channel_id=1, source_target_pairs={{0,2},{2,4},{4,6},{6,8},{8,10},{10,12},{12,14},{14,16},{16,18},{18... | collective-permute-start | bytes 4616 | tf_op jit(solution)/shard_map/ppermute | solution.py:33
  94.5 10.0 %collective-permute-start.15 = (f32[3,128,1]{2,1,0:T(8,128)S(1)}, f32[3,128,1]{2,1,0:T(8,128)S(1)}, u32[]{:S(2)}, u32[]{:S(2)}) collective-permute-start(f32[3,128,1]{2,1,0:T(8,128)S(1)} %get-tuple-element.205), channel_id=1, source_target_pairs={{2,0},{4,2},{6,4},{8,6},{10,8},{12,10},{14,12},{16,14},{18,16},{20... | collective-permute-start | bytes 4616 | tf_op jit(solution)/shard_map/ppermute | solution.py:34
  206.0 95.0 %copy-start.5 = (f32[3,130,1]{2,1,0:T(8,128)S(1)}, f32[3,130,1]{2,1,0:T(8,128)}, u32[]{:S(2)}) copy-start(f32[3,130,1]{2,1,0:T(8,128)} %copy-done.4) | copy-start | bytes 4684
  206.0 20.2 %collective-permute-start.23 = (f32[1,128,512]{2,1,0:T(8,128)S(1)}, f32[1,128,512]{2,1,0:T(8,128)S(1)}, u32[]{:S(2)}, u32[]{:S(2)}) collective-permute-start(f32[1,128,512]{2,1,0:T(8,128)S(1)} %get-tuple-element.196), channel_id=1, source_target_pairs={{1,0},{3,2},{5,4},{7,6},{9,8},{11,10},{13,12},{15,14},{17,16},{19,... | collective-permute-start | bytes 786440 | tf_op jit(solution)/shard_map/ppermute | solution.py:34
  208.4 17.8 %collective-permute-start.24 = (f32[1,128,512]{2,1,0:T(8,128)S(1)}, f32[1,128,512]{2,1,0:T(8,128)S(1)}, u32[]{:S(2)}, u32[]{:S(2)}) collective-permute-start(f32[1,128,512]{2,1,0:T(8,128)S(1)} %get-tuple-element.197), channel_id=1, source_target_pairs={{0,1},{2,3},{4,5},{6,7},{8,9},{10,11},{12,13},{14,15},{16,17},{18,... | collective-permute-start | bytes 786440 | tf_op jit(solution)/shard_map/ppermute | solution.py:33
  209.7 16.5 %collective-permute-start.20 = (f32[3,1,512]{2,1,0:T(1,128)S(1)}, f32[3,1,512]{2,1,0:T(1,128)S(1)}, u32[]{:S(2)}, u32[]{:S(2)}) collective-permute-start(f32[3,1,512]{2,1,0:T(1,128)S(1)} %get-tuple-element.200), channel_id=1, source_target_pairs={{0,64},{64,128},{128,192},{1,65},{65,129},{129,193},{2,66},{66,130... | collective-permute-start | bytes 18440 | tf_op jit(solution)/shard_map/ppermute | solution.py:33
  212.0 14.3 %collective-permute-start.19 = (f32[3,1,512]{2,1,0:T(1,128)S(1)}, f32[3,1,512]{2,1,0:T(1,128)S(1)}, u32[]{:S(2)}, u32[]{:S(2)}) collective-permute-start(f32[3,1,512]{2,1,0:T(1,128)S(1)} %get-tuple-element.201), channel_id=1, source_target_pairs={{64,0},{128,64},{192,128},{65,1},{129,65},{193,129},{66,2},{130,66... | collective-permute-start | bytes 18440 | tf_op jit(solution)/shard_map/ppermute | solution.py:34
  213.4 5.5 %collective-permute-start.22 = (f32[3,128,1]{2,1,0:T(8,128)S(1)}, f32[3,128,1]{2,1,0:T(8,128)S(1)}, u32[]{:S(2)}, u32[]{:S(2)}) collective-permute-start(f32[3,128,1]{2,1,0:T(8,128)S(1)} %get-tuple-element.198), channel_id=1, source_target_pairs={{0,2},{2,4},{4,6},{6,8},{8,10},{10,12},{12,14},{14,16},{16,18},{18... | collective-permute-start | bytes 4616 | tf_op jit(solution)/shard_map/ppermute | solution.py:33
  218.9 7.3 %collective-permute-start.21 = (f32[3,128,1]{2,1,0:T(8,128)S(1)}, f32[3,128,1]{2,1,0:T(8,128)S(1)}, u32[]{:S(2)}, u32[]{:S(2)}) collective-permute-start(f32[3,128,1]{2,1,0:T(8,128)S(1)} %get-tuple-element.199), channel_id=1, source_target_pairs={{2,0},{4,2},{6,4},{8,6},{10,8},{12,10},{14,12},{16,14},{18,16},{20... | collective-permute-start | bytes 4616 | tf_op jit(solution)/shard_map/ppermute | solution.py:34
  282.7 18.2 %collective-permute-start.29 = (f32[1,128,512]{2,1,0:T(8,128)S(1)}, f32[1,128,512]{2,1,0:T(8,128)S(1)}, u32[]{:S(2)}, u32[]{:S(2)}) collective-permute-start(f32[1,128,512]{2,1,0:T(8,128)S(1)} %get-tuple-element.190), channel_id=1, source_target_pairs={{1,0},{3,2},{5,4},{7,6},{9,8},{11,10},{13,12},{15,14},{17,16},{19,... | collective-permute-start | bytes 786440 | tf_op jit(solution)/shard_map/ppermute | solution.py:34
  284.9 16.0 %collective-permute-start.30 = (f32[1,128,512]{2,1,0:T(8,128)S(1)}, f32[1,128,512]{2,1,0:T(8,128)S(1)}, u32[]{:S(2)}, u32[]{:S(2)}) collective-permute-start(f32[1,128,512]{2,1,0:T(8,128)S(1)} %get-tuple-element.191), channel_id=1, source_target_pairs={{0,1},{2,3},{4,5},{6,7},{8,9},{10,11},{12,13},{14,15},{16,17},{18,... | collective-permute-start | bytes 786440 | tf_op jit(solution)/shard_map/ppermute | solution.py:33
  286.3 14.6 %collective-permute-start.26 = (f32[3,1,512]{2,1,0:T(1,128)S(1)}, f32[3,1,512]{2,1,0:T(1,128)S(1)}, u32[]{:S(2)}, u32[]{:S(2)}) collective-permute-start(f32[3,1,512]{2,1,0:T(1,128)S(1)} %get-tuple-element.194), channel_id=1, source_target_pairs={{0,64},{64,128},{128,192},{1,65},{65,129},{129,193},{2,66},{66,130... | collective-permute-start | bytes 18440 | tf_op jit(solution)/shard_map/ppermute | solution.py:33
  287.6 13.3 %collective-permute-start.25 = (f32[3,1,512]{2,1,0:T(1,128)S(1)}, f32[3,1,512]{2,1,0:T(1,128)S(1)}, u32[]{:S(2)}, u32[]{:S(2)}) collective-permute-start(f32[3,1,512]{2,1,0:T(1,128)S(1)} %get-tuple-element.195), channel_id=1, source_target_pairs={{64,0},{128,64},{192,128},{65,1},{129,65},{193,129},{66,2},{130,66... | collective-permute-start | bytes 18440 | tf_op jit(solution)/shard_map/ppermute | solution.py:34
  289.0 4.5 %collective-permute-start.28 = (f32[3,128,1]{2,1,0:T(8,128)S(1)}, f32[3,128,1]{2,1,0:T(8,128)S(1)}, u32[]{:S(2)}, u32[]{:S(2)}) collective-permute-start(f32[3,128,1]{2,1,0:T(8,128)S(1)} %get-tuple-element.192), channel_id=1, source_target_pairs={{0,2},{2,4},{4,6},{6,8},{8,10},{10,12},{12,14},{14,16},{16,18},{18... | collective-permute-start | bytes 4616 | tf_op jit(solution)/shard_map/ppermute | solution.py:33
  293.5 7.3 %collective-permute-start.27 = (f32[3,128,1]{2,1,0:T(8,128)S(1)}, f32[3,128,1]{2,1,0:T(8,128)S(1)}, u32[]{:S(2)}, u32[]{:S(2)}) collective-permute-start(f32[3,128,1]{2,1,0:T(8,128)S(1)} %get-tuple-element.193), channel_id=1, source_target_pairs={{2,0},{4,2},{6,4},{8,6},{10,8},{12,10},{14,12},{16,14},{18,16},{20... | collective-permute-start | bytes 4616 | tf_op jit(solution)/shard_map/ppermute | solution.py:34
  (11 other events, 288.2 us)
where the time goes:
time: 364 us; the launch traced here: 362 us
  blocking collectives  184 us (51%)
  starting transfers between devices  71 us (20%)
  other arithmetic  38.7 us (11%)
  waiting for transfers between devices  34.7 us (10%)
  matrix products  11.9 us (3%)
  between operations  11.6 us (3%)
  local copies, waits for them, and re-layouts  9.3 us (3%)
    psum x12, blocking collectives, over_axes(): shard = lax.psum(shard, axis)  184 us
    ppermute x15, starting transfers between devices, padded(): lax.ppermute(last, axis, up)  43.9 us
    ppermute x15, waiting for transfers between devices, padded(): lax.ppermute(first, axis, [(b, a) for a, b in up])  26.9 us
    ppermute x15, starting transfers between devices, padded(): lax.ppermute(first, axis, [(b, a) for a, b in up])  24.4 us
    reduce_sum x3, other arithmetic, both_sums(): jnp.sum(scaled * image)  16.4 us
    div x3, other arithmetic, solve(): scaled = residual / diagonal  9.34 us
    ppermute x15, waiting for transfers between devices, padded(): lax.ppermute(last, axis, up)  7.79 us
  transfers between devices with their start and end apart: 31, of which 7 were waited for; matrix products, arithmetic and copies ran while one was open for 7% of the time, Pallas kernels for 0%

commit v1 on v0

v1 whole, which is shorter than its diff:
```python
import jax
import jax.numpy as jnp
from jax import lax
from jax.experimental import pallas as pl
from jax.experimental.pallas import tpu as pltpu
from jax.sharding import Mesh
from jax.sharding import PartitionSpec as P

ALL = ("gx", "gy_0", "gy_1", "layer")
GY = ("gy_0", "gy_1")
HALO = 4
LANES = 128
SIDE = 256
SLOTS = 2048
CHUNK = 512
TINY = 1e-30
MOMENTS = 6

VMEM = pl.BlockSpec(memory_space=pltpu.VMEM)
SMEM = pl.BlockSpec(memory_space=pltpu.SMEM)


def params(mebibytes):
    return pltpu.CompilerParams(vmem_limit_bytes=mebibytes << 20)


def scatter_kernel(count_ref, weight_ref, profile_ref, cell_ref, out_ref, total_ref):
    step = pl.program_id(0)

    @pl.when(step == 0)
    def _():
        total_ref[...] = jnp.zeros_like(total_ref)

    @pl.when(step * SLOTS < count_ref[0])
    def _():
        half = out_ref.shape[0]
        for first in range(0, SLOTS, CHUNK):
            amount = lax.dot_general(
                weight_ref[...],
                profile_ref[first : first + CHUNK, :],
                (((1,), (1,)), ((), ())),
                preferred_element_type=jnp.float32,
            )[:1]
            position = step * SLOTS + first + lax.broadcasted_iota(jnp.int32, (1, CHUNK), 1)
            amount = jnp.where(position < count_ref[0], amount, 0.0)
            high = amount.astype(jnp.bfloat16).astype(jnp.float32)
            low = amount - high
            cell = cell_ref[:, first : first + CHUNK]
            row = (cell >> 9) + ((cell >> 8) & 1) * half
            col = cell & (SIDE - 1)
            ids = lax.broadcasted_iota(jnp.int32, (SIDE, CHUNK), 0)
            here = ids == row
            left = jnp.concatenate(
                [
                    jnp.where(here, high, 0.0).astype(jnp.bfloat16),
                    jnp.where(here, low, 0.0).astype(jnp.bfloat16),
                ],
                axis=0,
            )
            right = jnp.where(ids == col, 1.0, 0.0).astype(jnp.bfloat16)
            total_ref[...] += lax.dot_general(
                left, right, (((1,), (1,)), ((), ())), preferred_element_type=jnp.float32
            )

    @pl.when(step == pl.num_programs(0) - 1)
    def _():
        half = out_ref.shape[0]
        both = total_ref[:SIDE, :] + total_ref[SIDE:, :]
        out_ref[:, :SIDE] = both[:half]
        out_ref[:, SIDE:] = both[half:]


def scatter(profiles, time_weight, slot_cell, inst_count, tile):
    slots, times = profiles.shape[-2:]
    return pl.pallas_call(
        scatter_kernel,
        out_shape=jax.ShapeDtypeStruct(tile, jnp.float32),
        grid=(slots // SLOTS,),
        in_specs=[
            SMEM,
            pl.BlockSpec((16, times), lambda i: (0, 0)),
            pl.BlockSpec((SLOTS, times), lambda i: (i, 0)),
            pl.BlockSpec((1, SLOTS), lambda i: (0, i)),
        ],
        out_specs=pl.BlockSpec(tile, lambda i: (0, 0)),
        scratch_shapes=[pltpu.VMEM((2 * SIDE, SIDE), jnp.float32)],
        compiler_params=params(24),
        cost_estimate=pl.CostEstimate(
            flops=6 * slots * SIDE * SIDE, bytes_accessed=2 * slots * times, transcendentals=0
        ),
        name="scatter",
    )(
        inst_count.reshape(1),
        jnp.broadcast_to(time_weight[None], (16, times)),
        profiles.reshape(slots, times),
        slot_cell.reshape(1, slots),
    )


def plane_readers(metal, other_metal, start, other_start, via, pad, mine, theirs, flip):
    readers = []
    for own, other in ((metal, other_metal), (start, other_start)):
        for ref in (own, other):
            for k in range(3):
                index = jnp.where(flip == 1, 2 - k, k)
                readers.append(lambda rows, cols, ref=ref, index=index: ref[index, rows, cols])
    readers.append(lambda rows, cols: via[rows, cols])
    readers.append(lambda rows, cols: pad[rows, cols])
    readers.append(lambda rows, cols: mine[rows, cols] + theirs[rows, cols])
    return readers


def rows_kernel(flag, m, om, s, os, via, pad, mine, theirs, first_ref, last_ref):
    rows = m.shape[1]
    readers = plane_readers(m, om, s, os, via, pad, mine, theirs, flag[0])
    low = lax.broadcasted_iota(jnp.int32, (8, m.shape[2]), 0) < HALO
    for ref, start in ((first_ref, 0), (last_ref, rows - 8)):
        span = slice(start, start + 8)
        for pair in range(0, len(readers), 2):
            one = readers[pair](span, slice(None))
            two = one
            if pair + 1 < len(readers):
                two = pltpu.roll(readers[pair + 1](span, slice(None)), HALO, 0)
            packed = jnp.where(low, one, two) if start == 0 else jnp.where(low, two, one)
            ref[pair * HALO : pair * HALO + 8, :] = packed


def row_halo(after, before, plane, cols, flag):
    span = slice(plane // 2 * 8, plane // 2 * 8 + 8)
    tail = jnp.where(flag[2] == 1, after[span, cols], 0.0)
    head = jnp.where(flag[1] == 1, before[span, cols], 0.0)
    low = lax.broadcasted_iota(jnp.int32, tail.shape, 0) < HALO
    if plane % 2 == 0:
        return jnp.where(low, tail, head)
    return pltpu.roll(jnp.where(low, head, tail), HALO, 0)


def cols_kernel(flag, m, om, s, os, via, pad, mine, theirs, after, before, first_ref, last_ref):
    rows, cols = m.shape[1], m.shape[2]
    readers = plane_readers(m, om, s, os, via, pad, mine, theirs, flag[0])
    for ref, start in ((first_ref, 0), (last_ref, cols - LANES)):
        span = slice(start, start + LANES)
        lane = lax.broadcasted_iota(jnp.int32, (rows + 8, LANES), 1)
        packed = jnp.zeros((rows + 8, LANES), jnp.float32)
        for plane, read in enumerate(readers):
            values = jnp.concatenate(
                [read(slice(None), span), row_halo(after, before, plane, span, flag)], axis=0
            )
            where = HALO * plane if start == 0 else (LANES - HALO + HALO * plane) % LANES
            turned = pltpu.roll(values, HALO * plane, 1) if plane else values
            packed = jnp.where((lane >= where) & (lane < where + HALO), turned, packed)
        ref[...] = packed


def col_halo(right, left, plane, flag):
    lane = lax.broadcasted_iota(jnp.int32, right.shape, 1)
    where = HALO * plane
    back = (LANES - HALO + where) % LANES
    tail = (lane >= where) & (lane < where + HALO) & (flag[4] == 1)
    head = (lane >= back) & (lane < back + HALO) & (flag[3] == 1)
    values = jnp.where(tail, right[...], jnp.where(head, left[...], 0.0))
    return pltpu.roll(values, (LANES - where) % LANES, 1) if plane else values


def strip_call(kernel, shape, name, *operands):
    return pl.pallas_call(
        kernel,
        out_shape=(jax.ShapeDtypeStruct(shape, jnp.float32),) * 2,
        in_specs=[SMEM] + [VMEM] * (len(operands) - 1),
        out_specs=(VMEM, VMEM),
        compiler_params=params(24),
        name=name,
    )(*operands)


def after_row(values):
    return pltpu.roll(values, values.shape[0] - 1, 0)


def before_row(values):
    return pltpu.roll(values, 1, 0)


def after_col(values):
    return pltpu.roll(values, values.shape[1] - 1, 1)


def before_col(values):
    return pltpu.roll(values, 1, 1)


def harmonic(values, beside):
    return 2.0 * values * beside / jnp.maximum(values + beside, TINY)


def basis_kernel(
    flag, m, om, s, os, via, pad, mine, theirs, after, before, right, left,
    diag_out, z0_out, z1_out, z2_out, w2_out, moments_ref,
    metal_ref, start_ref, column_ref, row_link, col_link, up_link, diag_ref, inv_ref, r_ref, z_ref, v_ref,
):
    rows, cols = m.shape[1], m.shape[2]
    flip = flag[0]
    readers = plane_readers(m, om, s, os, via, pad, mine, theirs, flip)
    places = [metal_ref.at[k] for k in range(6)] + [start_ref.at[k] for k in range(6)]
    places += [column_ref.at[k] for k in range(3)]
    every = slice(None)
    for plane, (read, place) in enumerate(zip(readers, places)):
        place[:rows, :cols] = read(every, every)
        place[rows:, :cols] = row_halo(after, before, plane, every, flag)
        place[:, cols:] = col_halo(right, left, plane, flag)

    up_link[0] = jnp.zeros_like(up_link[0])
    up_link[6] = jnp.zeros_like(up_link[0])

    def link(k, _):
        metal = metal_ref[k]
        row_link[k] = harmonic(metal, after_row(metal))
        col_link[k] = harmonic(metal, after_col(metal))
        return 0

    lax.fori_loop(0, 6, link, 0)

    def climb(k, _):
        up_link[k + 1] = column_ref[0] * harmonic(metal_ref[k], metal_ref[k + 1])
        return 0

    lax.fori_loop(0, 5, climb, 0)

    padded_layer = jnp.where(flip == 1, 0, 5)
    fed_layer = 5 - padded_layer

    def operate(field, k):
        v = field[k]
        row, col = row_link[k], col_link[k]
        result = diag_ref[k] * v - row * after_row(v) - before_row(row * v)
        result = result - col * after_col(v) - before_col(col * v)
        above, below = jnp.minimum(k + 1, 5), jnp.maximum(k - 1, 0)
        return result - up_link[k + 1] * field[above] - up_link[k] * field[below]

    def diagonal(k, _):
        row, col = row_link[k], col_link[k]
        total = row + before_row(row) + col + before_col(col) + up_link[k + 1] + up_link[k]
        total = total + jnp.where(k == padded_layer, column_ref[1], 0.0)
        diag_ref[k] = total
        inv_ref[k] = 1.0 / jnp.maximum(total, TINY)
        return 0

    lax.fori_loop(0, 6, diagonal, 0)

    def own(values):
        return values[:rows, :cols]

    def first(k, _):
        r = jnp.where(k == fed_layer, column_ref[2], 0.0) - operate(start_ref, k)
        r_ref[k] = r
        z_ref[k] = r * inv_ref[k]
        return 0

    lax.fori_loop(0, 6, first, 0)

    def second(k, _):
        r = r_ref[k] - operate(z_ref, k)
        v_ref[k] = r * inv_ref[k]
        return 0

    lax.fori_loop(0, 5, second, 0)

    def keep(k, sums):
        z0, z1, r0 = own(z_ref[k]), own(v_ref[k]), own(r_ref[k])
        z0_out[k] = z0
        z1_out[k] = z1
        diag_out[k] = own(diag_ref[k])
        return sums[0] + fold(z0 * r0), sums[1] + fold(z1 * r0)

    def fold(values):
        return values.reshape(rows // 8, 8, cols // LANES, LANES).sum(axis=(0, 2))

    zero = jnp.zeros((8, LANES), jnp.float32)
    sums = lax.fori_loop(0, 3, keep, (zero, zero))

    def third(k, sums):
        r = diag_ref[k] * v_ref[k] - operate(v_ref, k)
        z_ref[k] = r * inv_ref[k]
        return 0

    lax.fori_loop(0, 4, third, 0)

    def fourth(k, sums):
        z1, z2, d = own(v_ref[k]), own(z_ref[k]), own(diag_ref[k])
        w2 = own(operate(z_ref, k))
        z2_out[k] = z2
        w2_out[k] = w2
        d2 = d * z2
        terms = (d * z1 * z1, z1 * d2, z2 * d2, z2 * (d2 - w2))
        return tuple(total + fold(term) for total, term in zip(sums, terms))

    sums = sums + lax.fori_loop(0, 3, fourth, (zero,) * 4)
    lane = lax.broadcasted_iota(jnp.int32, (8, LANES), 1)
    packed = zero
    for k, total in enumerate(sums):
        packed = jnp.where(lane == k, jnp.sum(total, keepdims=True), packed)
    moments_ref[...] = jnp.broadcast_to(packed[:1], moments_ref.shape)


def basis(devices, *operands):
    own = operands[1].shape
    full = (own[1] + 8, own[2] + LANES)
    layers = pltpu.VMEM((6,) + full, jnp.float32)
    return pl.pallas_call(
        basis_kernel,
        out_shape=(jax.ShapeDtypeStruct(own, jnp.float32),) * 5
        + (jax.ShapeDtypeStruct((devices, LANES), jnp.float32),),
        in_specs=[SMEM] + [VMEM] * (len(operands) - 1),
        out_specs=(VMEM,) * 6,
        scratch_shapes=[
            layers,
            layers,
            pltpu.VMEM((3,) + full, jnp.float32),
            layers,
            layers,
            pltpu.VMEM((7,) + full, jnp.float32),
            layers,
            layers,
            layers,
            layers,
            layers,
        ],
        compiler_params=params(50),
        name="basis",
    )(*operands)


def product(one, two, moments):
    total = 0.0
    for i, a in enumerate(one):
        for j, b in enumerate(two):
            total = total + a * b * moments[i + j]
    return total


def coefficients(moments, iterations):
    drops = [moments[i] - moments[i + 1] for i in range(MOMENTS - 1)]
    one = jnp.ones_like(moments[0])
    residual, direction, iterate = [one], [one], [0.0 * one] * iterations
    energy = moments[0]
    for iteration in range(iterations):
        step = energy / product(direction, direction, drops)
        iterate = [x + step * (direction[i] if i < len(direction) else 0.0) for i, x in enumerate(iterate)]
        image = [a - b for a, b in zip(direction + [0.0], [0.0] + direction)]
        residual = [a - step * b for a, b in zip(residual + [0.0], image)]
        if iteration + 1 < iterations:
            after = product(residual, residual, moments)
            ratio = after / energy
            direction = [a + ratio * b for a, b in zip(residual, direction + [0.0])]
            energy = after
    return iterate, residual


def update_kernel(flag, sums, start, diag, z0_ref, z1_ref, z2_ref, w2_ref, drop_ref, residual_ref):
    sums = jnp.sum(sums[...], axis=0, keepdims=True)
    lane = lax.broadcasted_iota(jnp.int32, sums.shape, 1)
    moments = [
        jnp.sum(jnp.where(lane == k, sums, 0.0), axis=1, keepdims=True) for k in range(MOMENTS)
    ]
    x, r = coefficients(moments, 3)
    for k in range(3):
        index = jnp.where(flag[0] == 1, 2 - k, k)
        z0, z1, z2 = z0_ref[k], z1_ref[k], z2_ref[k]
        drop_ref[index] = start[index] + (x[0] * z0 + x[1] * z1 + x[2] * z2)
        inner = r[0] * z0 + r[1] * z1 + (r[2] + r[3]) * z2
        residual_ref[index] = diag[k] * inner - r[3] * w2_ref[k]


def update(*operands):
    shape = jax.ShapeDtypeStruct(operands[2].shape, jnp.float32)
    return pl.pallas_call(
        update_kernel,
        out_shape=(shape, shape),
        in_specs=[SMEM] + [VMEM] * (len(operands) - 1),
        out_specs=(VMEM, VMEM),
        compiler_params=params(24),
        name="update",
    )(*operands)


def ring(value, axes, shift):
    count = lax.axis_size(axes)
    return lax.ppermute(value, axes, [(i, (i + shift) % count) for i in range(count)])


def per_device(profiles, time_weight, slot_cell, inst_count, metal, via_density, pad, start_drop):
    rows, cols = metal.shape[1], metal.shape[2]
    gx, gy, layer = lax.axis_index("gx"), lax.axis_index(GY), lax.axis_index("layer")
    flag = jnp.stack(
        [
            layer,
            gx > 0,
            gx < lax.axis_size("gx") - 1,
            gy > 0,
            gy < lax.axis_size(GY) - 1,
        ]
    ).astype(jnp.int32)
    other_metal = ring(metal, "layer", 1)
    other_start = ring(start_drop, "layer", 1)
    mine = scatter(profiles, time_weight, slot_cell, inst_count, (rows, cols))
    theirs = ring(mine, "layer", 1)
    planes = (flag, metal, other_metal, start_drop, other_start, via_density, pad, mine, theirs)
    first, last = strip_call(rows_kernel, (64, cols), "rows", *planes)
    after, before = ring(first, "gx", -1), ring(last, "gx", 1)
    first, last = strip_call(cols_kernel, (rows + 8, LANES), "cols", *planes, after, before)
    right, left = ring(first, GY, -1), ring(last, GY, 1)
    devices = lax.axis_size(ALL)
    diag, z0, z1, z2, w2, moments = basis(devices, *planes, after, before, right, left)
    sums = lax.all_to_all(moments, ALL, 0, 0, tiled=True)
    return update(flag, sums, start_drop, diag, z0, z1, z2, w2)


def solution(mesh):
    split = Mesh(
        mesh.devices.reshape(mesh.shape["gx"], 4, 8, mesh.shape["layer"]),
        ("gx", "gy_0", "gy_1", "layer"),
    )
    grid = P("layer", "gx", GY)
    return jax.shard_map(
        per_device,
        mesh=split,
        in_specs=(P("layer", "gx", GY, None), P(), grid, grid, grid, P("gx", GY), P("gx", GY), grid),
        out_specs=(grid, grid),
        check_vma=False,
    )
```

time: 364 us -> 91.2 us (0.25)
  blocking collectives: 184 us -> 20.4 us
  starting transfers between devices: 71 us -> 21.1 us
  other arithmetic: 38.7 us -> 0 us
  Pallas kernels: 0 us -> 25.8 us
  waiting for transfers between devices: 34.7 us -> 13 us
  matrix products: 11.9 us -> 0 us
  between operations: 11.6 us -> 1.34 us
    psum x12 -> x0, blocking collectives: 184 us -> none  [over_axes(): shard = lax.psum(shard, axis)]
    ppermute x31 -> x7, starting transfers between devices: 71 us -> 21.1 us  [ring(): lax.ppermute(value, axes, [(i, (i + shift) % count) for i in range(count)])]
    pallas_call x0 -> x5, Pallas kernels: none -> 25.8 us  [the longest x1 16.1 us: basis(): pl.pallas_call(basis_kernel, out_shape=(jax.ShapeDtypeStruct(own, jnp.flo...]
    ppermute x31 -> x7, waiting for transfers between devices: 34.7 us -> 13 us  [ring(): lax.ppermute(value, axes, [(i, (i + shift) % count) for i in range(count)])]
    all_to_all x0 -> x1, blocking collectives: none -> 20.4 us  [per_device(): sums = lax.all_to_all(moments, ALL, 0, 0, tiled=True)]
    reduce_sum x3 -> x0, other arithmetic: 16.4 us -> none  [both_sums(): jnp.sum(scaled * image)]
    dot_general x11 -> x0, matrix products: 11.9 us -> none  [the longest x1 5.71 us: per_device(): jnp.dot(profiles.reshape(-1, profiles.shape[-1]), time_weight, preferred_...]
    div x3 -> x0, other arithmetic: 9.34 us -> none  [solve(): scaled = residual / diagonal]
  transfers between devices with their start and end apart: 31 -> 7, of which waited for: 7 -> 5; matrix products, arithmetic and copies ran while one was open for 7% -> 1% of each run, Pallas kernels for 0% -> 4%
where the time goes in v1:
time: 91.2 us; the launch traced here: 90 us
  Pallas kernels  25.8 us (28%)
  starting transfers between devices  21.1 us (23%)
  blocking collectives  20.4 us (22%)
  waiting for transfers between devices  13 us (14%)
  local copies, waits for them, and re-layouts  8.4 us (9%)
  between operations  1.34 us (1%)
    ppermute x7, starting transfers between devices, ring(): lax.ppermute(value, axes, [(i, (i + shift) % count) for i in range(count)])  21.1 us
    all_to_all x1, blocking collectives, per_device(): sums = lax.all_to_all(moments, ALL, 0, 0, tiled=True)  20.4 us
    pallas_call x1, Pallas kernels, basis(): pl.pallas_call(basis_kernel, out_shape=(jax.ShapeDtypeStruct(own, jnp.flo...  16.1 us
    ppermute x7, waiting for transfers between devices, ring(): lax.ppermute(value, axes, [(i, (i + shift) % count) for i in range(count)])  13 us
    unnamed x22, local copies, waits for them, and re-layouts  7.65 us
    pallas_call x1, Pallas kernels, scatter(): pl.pallas_call(scatter_kernel, out_shape=jax.ShapeDtypeStruct(tile, jnp.f...  4.03 us
    pallas_call x2, Pallas kernels, strip_call(): pl.pallas_call(kernel, out_shape=(jax.ShapeDtypeStruct(shape, jnp.float32...  3.2 us
    pallas_call x1, Pallas kernels, update(): pl.pallas_call(update_kernel, out_shape=(shape, shape), in_specs=[SMEM] +...  2.47 us
  transfers between devices with their start and end apart: 7, of which 5 were waited for; matrix products, arithmetic and copies ran while one was open for 1% of the time, Pallas kernels for 4%

profile of v1, /device:TPU:1, one launch (start us, length us, event | category | flops | bytes accessed | tf_op | source)
XLA Modules:
  0.0 90.0 jit_solution(2287629475413861171)
XLA Ops:
  0.6 3.3 %collective-permute-start = (f32[3,128,512]{2,1,0:T(8,128)}, f32[3,128,512]{2,1,0:T(8,128)S(1)}, u32[]{:S(2)}, u32[]{:S(2)}) collective-permute-start(f32[3,128,512]{2,1,0:T(8,128)} %m.5), channel_id=1, source_target_pairs={{0,1},{1,0},{2,3},{3,2},{4,5},{5,4},{6,7},{7,6},{8,9},{9,8},{10,11... | collective-permute-start | bytes 2359304 | tf_op jit(solution)/shard_map/ppermute | solution.py:388
  4.0 0.1 collective-permute-start.1
  4.7 0.7 broadcast_in_dim.2.weight_ref
  5.4 3.4 %copy-done.9 = bf16[1,1,16384,256]{3,2,1,0:T(8,128)(2,1)S(1)} copy-done((bf16[1,1,16384,256]{3,2,1,0:T(8,128)(2,1)S(1)}, bf16[1,1,16384,256]{3,2,1,0:T(8,128)(2,1)}, u32[]{:S(2)}) %copy-start.9) | copy-done | bytes 8388632
  8.8 0.8 copy-done.10
  9.6 4.0 %scatter.1.mine = f32[128,512]{1,0:T(8,128)} custom-call(s32[1]{0:T(128)} %bitcast.12.count_ref, bf16[16,256]{1,0:T(8,128)(2,1)S(1)} %broadcast_in_dim.2.weight_ref, bf16[16384,256]{1,0:T(8,128)(2,1)S(1)} %bitcast.15, s32[1,16384]{1,0:T(1,128)S(1)} %bitcast.16), custom_call_target="tpu_custom_call" | custom-call | flops 6442450944 | bytes 8388608 | tf_op jit(solution)/shard_map/scatter/pallas_call | solution.py:75
  13.6 0.4 collective-permute-start.2
  14.0 0.1 stack.39.flag
  14.1 1.4 %collective-permute-done.2.theirs = f32[128,512]{1,0:T(8,128)} collective-permute-done((f32[128,512]{1,0:T(8,128)}, f32[128,512]{1,0:T(8,128)}, u32[]{:S(2)}, u32[]{:S(2)}) %collective-permute-start.2) | collective-permute-done | bytes 262176 | tf_op jit(solution)/shard_map/ppermute | solution.py:388
  15.5 0.0 collective-permute-done.om
  15.6 0.0 collective-permute-done.1.os
  15.6 0.0 copy-done
  15.6 0.0 copy-done.2
  15.6 0.0 copy-done.4
  15.6 0.0 copy-start.5
  15.6 1.1 %copy-done.5 = f32[128,512]{1,0:T(8,128)S(1)} copy-done((f32[128,512]{1,0:T(8,128)S(1)}, f32[128,512]{1,0:T(8,128)}, u32[]{:S(2)}) %copy-start.5) | copy-done | bytes 262168
  16.7 1.3 %rows.1 = (f32[64,512]{1,0:T(8,128)S(1)}, f32[64,512]{1,0:T(8,128)S(1)}) custom-call(s32[5]{0:T(128)S(1)} %stack.39.flag, f32[3,128,512]{2,1,0:T(8,128)S(1)} %copy-done.2, f32[3,128,512]{2,1,0:T(8,128)S(1)} %collective-permute-done.om, f32[3,128,512]{2,1,0:T(8,128)S(1)} %copy-done, f32[3,128,512]{2,1,0:T(8,128)} %collective-permute-done.1.os, ...), custom_call_target="tpu_custom_call" | custom-call | tf_op jit(solution)/shard_map/rows/pallas_call | solution.py:166
  18.1 1.1 %collective-permute-start.3 = (f32[64,512]{1,0:T(8,128)S(1)}, f32[64,512]{1,0:T(8,128)S(1)}, u32[]{:S(2)}, u32[]{:S(2)}) collective-permute-start(f32[64,512]{1,0:T(8,128)S(1)} %get-tuple-element.12), channel_id=1, source_target_pairs={{0,192},{64,0},{128,64},{192,128},{1,193},{65,1},{129,65},{193,129... | collective-permute-start | bytes 393224 | tf_op jit(solution)/shard_map/ppermute | solution.py:388
  19.2 0.5 collective-permute-start.4
  19.6 3.2 %collective-permute-done.3.after = f32[64,512]{1,0:T(8,128)S(1)} collective-permute-done((f32[64,512]{1,0:T(8,128)S(1)}, f32[64,512]{1,0:T(8,128)S(1)}, u32[]{:S(2)}, u32[]{:S(2)}) %collective-permute-start.3) | collective-permute-done | bytes 131104 | tf_op jit(solution)/shard_map/ppermute | solution.py:388
  22.9 1.9 %collective-permute-done.4.before = f32[64,512]{1,0:T(8,128)S(1)} collective-permute-done((f32[64,512]{1,0:T(8,128)S(1)}, f32[64,512]{1,0:T(8,128)S(1)}, u32[]{:S(2)}, u32[]{:S(2)}) %collective-permute-start.4) | collective-permute-done | bytes 131104 | tf_op jit(solution)/shard_map/ppermute | solution.py:388
  24.8 1.9 %cols.1 = (f32[136,128]{1,0:T(8,128)S(1)}, f32[136,128]{1,0:T(8,128)S(1)}) custom-call(s32[5]{0:T(128)S(1)} %stack.39.flag, f32[3,128,512]{2,1,0:T(8,128)S(1)} %copy-done.2, f32[3,128,512]{2,1,0:T(8,128)S(1)} %collective-permute-done.om, f32[3,128,512]{2,1,0:T(8,128)S(1)} %copy-done, f32[3,128,512]{2,1,0:T(8,128)} %collective-permute-done.1.os, ...), custom_call_target="tpu_custom_call" | custom-call | tf_op jit(solution)/shard_map/cols/pallas_call | solution.py:166
  26.6 15.7 %collective-permute-start.5 = (f32[136,128]{1,0:T(8,128)S(1)}, f32[136,128]{1,0:T(8,128)S(1)}, u32[]{:S(2)}, u32[]{:S(2)}) collective-permute-start(f32[136,128]{1,0:T(8,128)S(1)} %get-tuple-element.14), channel_id=1, source_target_pairs={{0,62},{2,0},{4,2},{6,4},{8,6},{10,8},{12,10},{14,12},{16,14},{18,... | collective-permute-start | bytes 208904 | tf_op jit(solution)/shard_map/ppermute | solution.py:388
  42.3 0.0 collective-permute-start.6
  42.3 1.4 %collective-permute-done.5.right = f32[136,128]{1,0:T(8,128)S(1)} collective-permute-done((f32[136,128]{1,0:T(8,128)S(1)}, f32[136,128]{1,0:T(8,128)S(1)}, u32[]{:S(2)}, u32[]{:S(2)}) %collective-permute-start.5) | collective-permute-done | bytes 69664 | tf_op jit(solution)/shard_map/ppermute | solution.py:388
  43.7 5.1 %collective-permute-done.6.left = f32[136,128]{1,0:T(8,128)S(1)} collective-permute-done((f32[136,128]{1,0:T(8,128)S(1)}, f32[136,128]{1,0:T(8,128)S(1)}, u32[]{:S(2)}, u32[]{:S(2)}) %collective-permute-start.6) | collective-permute-done | bytes 69664 | tf_op jit(solution)/shard_map/ppermute | solution.py:388
  48.8 0.0 copy-done.3
  48.8 16.1 %basis.1 = (f32[3,128,512]{2,1,0:T(8,128)S(1)}, f32[3,128,512]{2,1,0:T(8,128)S(1)}, f32[3,128,512]{2,1,0:T(8,128)S(1)}, f32[3,128,512]{2,1,0:T(8,128)}, f32[3,128,512]{2,1,0:T(8,128)}, /*index=5*/f32[256,128]{1,0:T(8,128)S(1)}) custom-call(s32[5]{0:T(128)S(1)} %stack.39.flag, f32[3,128,512]{2,1,0:T(8,128)} %m.5, f32[3,128,512]{2,1,0:T(8,128)} %copy-done.3, ...), custom_call_target="tpu_custom_call" | custom-call | tf_op jit(solution)/shard_map/basis/pallas_call | solution.py:309
  64.9 20.4 %all_to_all.11 = f32[256,1,128]{2,1,0:T(1,128)S(1)} all-to-all(f32[256,1,128]{2,1,0:T(1,128)S(1)} %bitcast.14), channel_id=1, replica_groups=mesh['gx'=4,'gy_0'=4,'gy_1'=8,'layer'=2] {'gx','gy_0','gy_1','layer'}, dimensions={0} | all-to-all | bytes 262144 | tf_op jit(solution)/shard_map/all_to_all | solution.py:414
  85.3 1.1 %copy-done.7 = f32[3,128,512]{2,1,0:T(8,128)S(1)} copy-done((f32[3,128,512]{2,1,0:T(8,128)S(1)}, f32[3,128,512]{2,1,0:T(8,128)}, u32[]{:S(2)}) %copy-start.7) | copy-done | bytes 786456
  86.4 1.1 %copy-done.8 = f32[3,128,512]{2,1,0:T(8,128)S(1)} copy-done((f32[3,128,512]{2,1,0:T(8,128)S(1)}, f32[3,128,512]{2,1,0:T(8,128)}, u32[]{:S(2)}) %copy-start.8) | copy-done | bytes 786456
  87.6 2.5 %update.1 = (f32[3,128,512]{2,1,0:T(8,128)}, f32[3,128,512]{2,1,0:T(8,128)}) custom-call(s32[5]{0:T(128)S(1)} %stack.39.flag, f32[256,128]{1,0:T(8,128)S(1)} %bitcast.13, f32[3,128,512]{2,1,0:T(8,128)S(1)} %copy-done.1, f32[3,128,512]{2,1,0:T(8,128)S(1)} %get-tuple-element.17.diag, f32[3,128,512]{2,1,0:T(8,128)S(1)} %get-tuple-element.18.z0_ref, ...), custom_call_target="tpu_custom_call" | custom-call | tf_op jit(solution)/shard_map/update/pallas_call | solution.py:376
  (12 shorter events, 0.0 us)
Async XLA Ops:
  0.6 14.9 %collective-permute-start = (f32[3,128,512]{2,1,0:T(8,128)}, f32[3,128,512]{2,1,0:T(8,128)S(1)}, u32[]{:S(2)}, u32[]{:S(2)}) collective-permute-start(f32[3,128,512]{2,1,0:T(8,128)} %m.5), channel_id=1, source_target_pairs={{0,1},{1,0},{2,3},{3,2},{4,5},{5,4},{6,7},{7,6},{8,9},{9,8},{10,11... | collective-permute-start | bytes 2359304 | tf_op jit(solution)/shard_map/ppermute | solution.py:388
  4.0 11.6 %collective-permute-start.1 = (f32[3,128,512]{2,1,0:T(8,128)}, f32[3,128,512]{2,1,0:T(8,128)}, u32[]{:S(2)}, u32[]{:S(2)}) collective-permute-start(f32[3,128,512]{2,1,0:T(8,128)} %start.1), channel_id=1, source_target_pairs={{0,1},{1,0},{2,3},{3,2},{4,5},{5,4},{6,7},{7,6},{8,9},{9,8},{10,11... | collective-permute-start | bytes 2359304 | tf_op jit(solution)/shard_map/ppermute | solution.py:388
  5.4 3.4 %copy-start.9 = (bf16[1,1,16384,256]{3,2,1,0:T(8,128)(2,1)S(1)}, bf16[1,1,16384,256]{3,2,1,0:T(8,128)(2,1)}, u32[]{:S(2)}) copy-start(bf16[1,1,16384,256]{3,2,1,0:T(8,128)(2,1)} %param.8) | copy-start | bytes 25165828
  8.8 0.8 copy-start.10
  9.6 6.0 %copy-start = (f32[3,128,512]{2,1,0:T(8,128)S(1)}, f32[3,128,512]{2,1,0:T(8,128)}, u32[]{:S(2)}) copy-start(f32[3,128,512]{2,1,0:T(8,128)} %start.1) | copy-start | bytes 2359300
  9.6 6.0 %copy-start.2 = (f32[3,128,512]{2,1,0:T(8,128)S(1)}, f32[3,128,512]{2,1,0:T(8,128)}, u32[]{:S(2)}) copy-start(f32[3,128,512]{2,1,0:T(8,128)} %m.5) | copy-start | bytes 2359300
  9.6 6.0 %copy-start.4 = (f32[128,512]{1,0:T(8,128)S(1)}, f32[128,512]{1,0:T(8,128)}, u32[]{:S(2)}) copy-start(f32[128,512]{1,0:T(8,128)} %via.5) | copy-start | bytes 786436
  13.6 71.7 %copy-start.1 = (f32[3,128,512]{2,1,0:T(8,128)S(1)}, f32[3,128,512]{2,1,0:T(8,128)}, u32[]{:S(2)}) copy-start(f32[3,128,512]{2,1,0:T(8,128)} %start.1) | copy-start | bytes 2359300
  13.6 1.9 %collective-permute-start.2 = (f32[128,512]{1,0:T(8,128)}, f32[128,512]{1,0:T(8,128)}, u32[]{:S(2)}, u32[]{:S(2)}) collective-permute-start(f32[128,512]{1,0:T(8,128)} %scatter.1.mine), channel_id=1, source_target_pairs={{0,1},{1,0},{2,3},{3,2},{4,5},{5,4},{6,7},{7,6},{8,9},{9,8},{10,11... | collective-permute-start | bytes 786440 | tf_op jit(solution)/shard_map/ppermute | solution.py:388
  15.5 33.2 %copy-start.3 = (f32[3,128,512]{2,1,0:T(8,128)}, f32[3,128,512]{2,1,0:T(8,128)S(1)}, u32[]{:S(2)}) copy-start(f32[3,128,512]{2,1,0:T(8,128)S(1)} %collective-permute-done.om) | copy-start | bytes 2359300
  15.6 1.2 %copy-start.5 = (f32[128,512]{1,0:T(8,128)S(1)}, f32[128,512]{1,0:T(8,128)}, u32[]{:S(2)}) copy-start(f32[128,512]{1,0:T(8,128)} %pad.5) | copy-start | bytes 786436
  16.7 32.1 %copy-start.6 = (f32[128,512]{1,0:T(8,128)S(1)}, f32[128,512]{1,0:T(8,128)}, u32[]{:S(2)}) copy-start(f32[128,512]{1,0:T(8,128)} %pad.5) | copy-start | bytes 786436
  18.1 4.8 %collective-permute-start.3 = (f32[64,512]{1,0:T(8,128)S(1)}, f32[64,512]{1,0:T(8,128)S(1)}, u32[]{:S(2)}, u32[]{:S(2)}) collective-permute-start(f32[64,512]{1,0:T(8,128)S(1)} %get-tuple-element.12), channel_id=1, source_target_pairs={{0,192},{64,0},{128,64},{192,128},{1,193},{65,1},{129,65},{193,129... | collective-permute-start | bytes 393224 | tf_op jit(solution)/shard_map/ppermute | solution.py:388
  19.2 5.6 %collective-permute-start.4 = (f32[64,512]{1,0:T(8,128)S(1)}, f32[64,512]{1,0:T(8,128)S(1)}, u32[]{:S(2)}, u32[]{:S(2)}) collective-permute-start(f32[64,512]{1,0:T(8,128)S(1)} %get-tuple-element.13), channel_id=1, source_target_pairs={{0,64},{64,128},{128,192},{192,0},{1,65},{65,129},{129,193},{193,1... | collective-permute-start | bytes 393224 | tf_op jit(solution)/shard_map/ppermute | solution.py:388
  26.6 17.1 %collective-permute-start.5 = (f32[136,128]{1,0:T(8,128)S(1)}, f32[136,128]{1,0:T(8,128)S(1)}, u32[]{:S(2)}, u32[]{:S(2)}) collective-permute-start(f32[136,128]{1,0:T(8,128)S(1)} %get-tuple-element.14), channel_id=1, source_target_pairs={{0,62},{2,0},{4,2},{6,4},{8,6},{10,8},{12,10},{14,12},{16,14},{18,... | collective-permute-start | bytes 208904 | tf_op jit(solution)/shard_map/ppermute | solution.py:388
  42.3 6.5 %collective-permute-start.6 = (f32[136,128]{1,0:T(8,128)S(1)}, f32[136,128]{1,0:T(8,128)S(1)}, u32[]{:S(2)}, u32[]{:S(2)}) collective-permute-start(f32[136,128]{1,0:T(8,128)S(1)} %get-tuple-element.15), channel_id=1, source_target_pairs={{0,2},{2,4},{4,6},{6,8},{8,10},{10,12},{12,14},{14,16},{16,18},{18... | collective-permute-start | bytes 208904 | tf_op jit(solution)/shard_map/ppermute | solution.py:388
  85.3 1.1 %copy-start.7 = (f32[3,128,512]{2,1,0:T(8,128)S(1)}, f32[3,128,512]{2,1,0:T(8,128)}, u32[]{:S(2)}) copy-start(f32[3,128,512]{2,1,0:T(8,128)} %get-tuple-element.20.z2_ref) | copy-start | bytes 2359300
  86.4 1.1 %copy-start.8 = (f32[3,128,512]{2,1,0:T(8,128)S(1)}, f32[3,128,512]{2,1,0:T(8,128)}, u32[]{:S(2)}) copy-start(f32[3,128,512]{2,1,0:T(8,128)} %get-tuple-element.21.w2_ref) | copy-start | bytes 2359300

commit v2 on v1

v2 whole, which is shorter than its diff:
```python
import jax
import jax.numpy as jnp
from jax import lax
from jax.experimental import pallas as pl
from jax.experimental.pallas import tpu as pltpu
from jax.sharding import Mesh
from jax.sharding import PartitionSpec as P

ALL = ("gx", "gy_0", "gy_1", "layer")
GY = ("gy_0", "gy_1")
HALO = 4
LANES = 128
SIDE = 256
CHUNK = 4096
TINY = 1e-30
MOMENTS = 6

VMEM = pl.BlockSpec(memory_space=pltpu.VMEM)
HBM = pl.BlockSpec(memory_space=pltpu.HBM)
SMEM = pl.BlockSpec(memory_space=pltpu.SMEM)


def params(mebibytes):
    return pltpu.CompilerParams(vmem_limit_bytes=mebibytes << 20)


def scatter_kernel(count_ref, weight_ref, profile_hbm, cell_hbm, out_ref, profile_ref, cell_ref, total_ref, sems):
    half = out_ref.shape[0]
    blocks = profile_ref.shape[0] // CHUNK
    fetches = [pltpu.make_async_copy(cell_hbm, cell_ref, sems.at[blocks])]
    for block in range(blocks):
        span = pl.ds(block * CHUNK, CHUNK)
        fetches.append(
            pltpu.make_async_copy(profile_hbm.at[span], profile_ref.at[span], sems.at[block])
        )
    for fetch in fetches:
        fetch.start()
    total_ref[...] = jnp.zeros_like(total_ref)
    weight = jnp.broadcast_to(weight_ref[...], (16, weight_ref.shape[1]))
    ids = lax.broadcasted_iota(jnp.int32, (SIDE, CHUNK), 0).astype(jnp.float32).astype(jnp.bfloat16)
    zero, one = jnp.bfloat16(0), jnp.bfloat16(1)
    fetches[0].wait()

    def add_block(block, _):
        first = pl.multiple_of(block * CHUNK, CHUNK)
        span = pl.ds(first, CHUNK)
        pltpu.make_async_copy(profile_hbm.at[span], profile_ref.at[span], sems.at[block]).wait()
        amount = lax.dot_general(
            weight,
            profile_ref[span, :],
            (((1,), (1,)), ((), ())),
            preferred_element_type=jnp.float32,
        )[:1]
        position = first + lax.broadcasted_iota(jnp.int32, (1, CHUNK), 1)
        amount = jnp.where(position < count_ref[0], amount, 0.0)
        high = amount.astype(jnp.bfloat16)
        low = (amount - high.astype(jnp.float32)).astype(jnp.bfloat16)
        cell = cell_ref[:, span]
        row = ((cell >> 9) + ((cell >> 8) & 1) * half).astype(jnp.float32).astype(jnp.bfloat16)
        col = (cell & (SIDE - 1)).astype(jnp.float32).astype(jnp.bfloat16)
        here = ids == row
        left = jnp.concatenate([jnp.where(here, high, zero), jnp.where(here, low, zero)], axis=0)
        right = jnp.where(ids == col, one, zero)
        total_ref[...] += lax.dot_general(
            left, right, (((1,), (1,)), ((), ())), preferred_element_type=jnp.float32
        )
        return 0

    lax.fori_loop(0, blocks, add_block, 0)
    both = total_ref[:SIDE, :] + total_ref[SIDE:, :]
    out_ref[:, :SIDE] = both[:half]
    out_ref[:, SIDE:] = both[half:]


def scatter(profiles, time_weight, slot_cell, inst_count, tile):
    slots, times = profiles.shape[-2:]
    return pl.pallas_call(
        scatter_kernel,
        out_shape=jax.ShapeDtypeStruct(tile, jnp.float32),
        in_specs=[SMEM, VMEM, HBM, HBM],
        out_specs=VMEM,
        scratch_shapes=[
            pltpu.VMEM((slots, times), jnp.bfloat16),
            pltpu.VMEM((1, slots), jnp.int32),
            pltpu.VMEM((2 * SIDE, SIDE), jnp.float32),
            pltpu.SemaphoreType.DMA((slots // CHUNK + 1,)),
        ],
        compiler_params=params(24),
        cost_estimate=pl.CostEstimate(
            flops=6 * slots * SIDE * SIDE, bytes_accessed=2 * slots * times, transcendentals=0
        ),
        name="scatter",
    )(
        inst_count.reshape(1),
        time_weight.reshape(1, times),
        pltpu.with_memory_space_constraint(profiles.reshape(slots, times), pltpu.HBM),
        pltpu.with_memory_space_constraint(slot_cell.reshape(1, slots), pltpu.HBM),
    )


def plane_readers(metal, other_metal, start, other_start, via, pad, mine, theirs, flip):
    readers = []
    for own, other in ((metal, other_metal), (start, other_start)):
        for ref in (own, other):
            for k in range(3):
                index = jnp.where(flip == 1, 2 - k, k)
                readers.append(lambda rows, cols, ref=ref, index=index: ref[index, rows, cols])
    readers.append(lambda rows, cols: via[rows, cols])
    readers.append(lambda rows, cols: pad[rows, cols])
    readers.append(lambda rows, cols: mine[rows, cols] + theirs[rows, cols])
    return readers


def rows_kernel(flag, m, om, s, os, via, pad, mine, theirs, first_ref, last_ref):
    rows = m.shape[1]
    readers = plane_readers(m, om, s, os, via, pad, mine, theirs, flag[0])
    low = lax.broadcasted_iota(jnp.int32, (8, m.shape[2]), 0) < HALO
    for ref, start in ((first_ref, 0), (last_ref, rows - 8)):
        span = slice(start, start + 8)
        for pair in range(0, len(readers), 2):
            one = readers[pair](span, slice(None))
            two = one
            if pair + 1 < len(readers):
                two = pltpu.roll(readers[pair + 1](span, slice(None)), HALO, 0)
            packed = jnp.where(low, one, two) if start == 0 else jnp.where(low, two, one)
            ref[pair * HALO : pair * HALO + 8, :] = packed


def row_halo(ref, plane, cols, inside):
    values = jnp.where(inside == 1, ref[plane // 2 * 8 : plane // 2 * 8 + 8, cols], 0.0)
    return pltpu.roll(values, HALO, 0) if plane % 2 else values


def cols_kernel(flag, m, om, s, os, via, pad, mine, theirs, after, before, first_ref, last_ref):
    rows, cols = m.shape[1], m.shape[2]
    readers = plane_readers(m, om, s, os, via, pad, mine, theirs, flag[0])
    for ref, start in ((first_ref, 0), (last_ref, cols - LANES)):
        span = slice(start, start + LANES)
        lane = lax.broadcasted_iota(jnp.int32, (rows + 16, LANES), 1)
        packed = jnp.zeros((rows + 16, LANES), jnp.float32)
        for plane, read in enumerate(readers):
            values = jnp.concatenate(
                [
                    row_halo(before, plane, span, flag[1]),
                    read(slice(None), span),
                    row_halo(after, plane, span, flag[2]),
                ],
                axis=0,
            )
            where = HALO * plane if start == 0 else (LANES - HALO + HALO * plane) % LANES
            turned = pltpu.roll(values, HALO * plane, 1) if plane else values
            packed = jnp.where((lane >= where) & (lane < where + HALO), turned, packed)
        ref[...] = packed


def col_halo(right, left, plane, flag):
    lane = lax.broadcasted_iota(jnp.int32, right.shape, 1)
    where = HALO * plane
    back = (LANES - HALO + where) % LANES
    tail = (lane >= where) & (lane < where + HALO) & (flag[4] == 1)
    head = (lane >= back) & (lane < back + HALO) & (flag[3] == 1)
    values = jnp.where(tail, right[...], jnp.where(head, left[...], 0.0))
    return pltpu.roll(values, (LANES - where) % LANES, 1) if plane else values


def strip_call(kernel, shape, name, *operands):
    return pl.pallas_call(
        kernel,
        out_shape=(jax.ShapeDtypeStruct(shape, jnp.float32),) * 2,
        in_specs=[SMEM] + [VMEM] * (len(operands) - 1),
        out_specs=(VMEM, VMEM),
        compiler_params=params(24),
        name=name,
    )(*operands)


OWN = 16


def harmonic(values, beside):
    return 2.0 * values * beside / jnp.maximum(values + beside, TINY)


def basis_kernel(
    flag, m, om, s, os, via, pad, mine, theirs, after, before, right, left,
    inv_out, r0_out, s1_out, s2_out, s3_out, moments_ref,
    metal_ref, start_ref, column_ref, row_link, col_link, up_link, inv_ref, z0_ref, z1_ref, z2_ref,
):
    rows, cols = m.shape[1], m.shape[2]
    tiles, strips = cols // LANES, rows // 8
    flip = flag[0]
    readers = plane_readers(m, om, s, os, via, pad, mine, theirs, flip)
    places = [(metal_ref, k) for k in range(6)] + [(start_ref, k) for k in range(6)]
    places += [(column_ref, k) for k in range(3)]
    for plane, (read, (ref, k)) in enumerate(zip(readers, places)):
        for j in range(tiles):
            span = slice(j * LANES, j * LANES + LANES)
            ref[k, j, OWN - 8 : OWN, :] = row_halo(before, plane, span, flag[1])
            ref[k, j, OWN : OWN + rows, :] = read(slice(None), span)
            ref[k, j, OWN + rows : OWN + rows + 8, :] = row_halo(after, plane, span, flag[2])
        ref[k, tiles, OWN - 8 : OWN + rows + 8, :] = col_halo(right, left, plane, flag)

    lane = lax.broadcasted_iota(jnp.int32, (tiles + 1, 8, LANES), 2)

    def after_col(values):
        turned = pltpu.roll(values, LANES - 1, 2)
        return jnp.where(lane == LANES - 1, jnp.concatenate([turned[1:], turned[:1]], 0), turned)

    def before_col(values):
        turned = pltpu.roll(values, 1, 2)
        return jnp.where(lane == 0, jnp.concatenate([turned[-1:], turned[:-1]], 0), turned)

    def put(ref, k, i, values):
        ref[k, :, pl.ds(OWN + 8 * i, 8), :] = values

    def put_own(ref, k, i, values):
        for j in range(tiles):
            ref[k, pl.ds(8 * i, 8), j * LANES : j * LANES + LANES] = values[j]

    def fold(values):
        return jnp.sum(values[:tiles], axis=0)

    def sweep(body, count):
        body(-1, None)
        zero = jnp.zeros((8, LANES), jnp.float32)
        sums = lax.fori_loop(0, strips, body, (zero,) * count)
        body(strips, None)
        return sums

    weight = jnp.where(flip == 1, 1.0, 0.0)

    def first(i, sums):
        def get(ref, k, off=0):
            return ref[k, :, pl.ds(OWN + 8 * i + off, 8), :]

        energy = None if sums is None else sums[0]
        up_before = None
        for k in range(6):
            metal, x = get(metal_ref, k), get(start_ref, k)
            row = harmonic(metal, get(metal_ref, k, 1))
            put(row_link, k, i, row)
            row_before = get(row_link, k, -1)
            col = harmonic(metal, after_col(metal))
            put(col_link, k, i, col)
            total = row + row_before + col + before_col(col)
            near = row * get(start_ref, k, 1) + row_before * get(start_ref, k, -1)
            near = near + col * after_col(x) + before_col(col * x)
            if k < 5:
                up = get(column_ref, 0) * harmonic(metal, get(metal_ref, k + 1))
                put(up_link, k, i, up)
                total = total + up
                near = near + up * get(start_ref, k + 1)
            if k > 0:
                total = total + up_before
                near = near + up_before * get(start_ref, k - 1)
            up_before = up
            if k == 0:
                total = total + weight * get(column_ref, 1)
                near = near + (1.0 - weight) * get(column_ref, 2)
            if k == 5:
                total = total + (1.0 - weight) * get(column_ref, 1)
                near = near + weight * get(column_ref, 2)
            inv = 1.0 / jnp.maximum(total, TINY)
            r = near - total * x
            z = r * inv
            put(inv_ref, k, i, inv)
            put(z0_ref, k, i, z)
            if sums is not None and k < 3:
                put_own(inv_out, k, i, inv)
                put_own(r0_out, k, i, r)
                energy = energy + fold(z * r)
        return None if sums is None else (energy,)

    def step(source, target, out, planes):
        def body(i, sums):
            def get(ref, k, off=0):
                return ref[k, :, pl.ds(OWN + 8 * i + off, 8), :]

            totals = sums
            up_before, z_before = None, None
            z = get(source, 0)
            for k in range(planes):
                col = get(col_link, k)
                near = get(row_link, k) * get(source, k, 1) + get(row_link, k, -1) * get(source, k, -1)
                near = near + col * after_col(z) + before_col(col * z)
                if k < 5:
                    up, z_after = get(up_link, k), get(source, k + 1)
                    near = near + up * z_after
                if k > 0:
                    near = near + up_before * z_before
                if target is not None:
                    fresh = near * get(inv_ref, k)
                    put(target, k, i, fresh)
                if sums is not None and k < 3:
                    put_own(out, k, i, near)
                    terms = (z * near,) if target is None else (z * near, fresh * near)
                    totals = tuple(a + fold(b) for a, b in zip(totals, terms))
                up_before, z_before, z = up, z, z_after
            return totals

        return body

    sums = sweep(first, 1)
    sums += sweep(step(z0_ref, z1_ref, s1_out, 5), 2)
    sums += sweep(step(z1_ref, z2_ref, s2_out, 4), 2)
    zero = jnp.zeros((8, LANES), jnp.float32)
    sums += lax.fori_loop(0, strips, step(z2_ref, None, s3_out, 3), (zero,))
    lane = lax.broadcasted_iota(jnp.int32, (8, LANES), 1)
    packed = zero
    for k, total in enumerate(sums):
        packed = jnp.where(lane == k, jnp.sum(total, keepdims=True), packed)
    moments_ref[...] = jnp.broadcast_to(packed[:1], moments_ref.shape)


def basis(devices, *operands):
    own = operands[1].shape
    shape = (own[2] // LANES + 1, own[1] + 2 * OWN, LANES)
    planes = (6, 6, 3, 6, 6, 5, 6, 6, 5, 4)
    return pl.pallas_call(
        basis_kernel,
        out_shape=(jax.ShapeDtypeStruct(own, jnp.float32),) * 5
        + (jax.ShapeDtypeStruct((devices, LANES), jnp.float32),),
        in_specs=[SMEM] + [VMEM] * (len(operands) - 1),
        out_specs=(VMEM,) * 6,
        scratch_shapes=[pltpu.VMEM((count,) + shape, jnp.float32) for count in planes],
        compiler_params=params(32),
        name="basis",
    )(*operands)


def product(one, two, moments):
    total = 0.0
    for i, a in enumerate(one):
        for j, b in enumerate(two):
            total = total + a * b * moments[i + j]
    return total


def coefficients(moments, iterations):
    drops = [moments[i] - moments[i + 1] for i in range(MOMENTS - 1)]
    one = jnp.ones_like(moments[0])
    residual, direction, iterate = [one], [one], [0.0 * one] * iterations
    energy = moments[0]
    for iteration in range(iterations):
        step = energy / product(direction, direction, drops)
        iterate = [x + step * (direction[i] if i < len(direction) else 0.0) for i, x in enumerate(iterate)]
        image = [a - b for a, b in zip(direction + [0.0], [0.0] + direction)]
        residual = [a - step * b for a, b in zip(residual + [0.0], image)]
        if iteration + 1 < iterations:
            after = product(residual, residual, moments)
            ratio = after / energy
            direction = [a + ratio * b for a, b in zip(residual, direction + [0.0])]
            energy = after
    return iterate, residual


def update_kernel(flag, sums, start, inv, r0_ref, s1_ref, s2_ref, s3_ref, drop_ref, residual_ref):
    sums = jnp.sum(sums[...], axis=0, keepdims=True)
    lane = lax.broadcasted_iota(jnp.int32, sums.shape, 1)
    moments = [
        jnp.sum(jnp.where(lane == k, sums, 0.0), axis=1, keepdims=True) for k in range(MOMENTS)
    ]
    x, r = coefficients(moments, 3)
    for k in range(3):
        index = jnp.where(flag[0] == 1, 2 - k, k)
        r0, s1, s2 = r0_ref[k], s1_ref[k], s2_ref[k]
        drop_ref[index] = start[index] + inv[k] * (x[0] * r0 + x[1] * s1 + x[2] * s2)
        residual_ref[index] = r[0] * r0 + r[1] * s1 + r[2] * s2 + r[3] * s3_ref[k]


def update(*operands):
    shape = jax.ShapeDtypeStruct(operands[2].shape, jnp.float32)
    return pl.pallas_call(
        update_kernel,
        out_shape=(shape, shape),
        in_specs=[SMEM] + [VMEM] * (len(operands) - 1),
        out_specs=(VMEM, VMEM),
        compiler_params=params(24),
        name="update",
    )(*operands)


def ring(value, axes, shift):
    count = lax.axis_size(axes)
    return lax.ppermute(value, axes, [(i, (i + shift) % count) for i in range(count)])


def per_device(profiles, time_weight, slot_cell, inst_count, metal, via_density, pad, start_drop):
    rows, cols = metal.shape[1], metal.shape[2]
    gx, gy, layer = lax.axis_index("gx"), lax.axis_index(GY), lax.axis_index("layer")
    flag = jnp.stack(
        [
            layer,
            gx > 0,
            gx < lax.axis_size("gx") - 1,
            gy > 0,
            gy < lax.axis_size(GY) - 1,
        ]
    ).astype(jnp.int32)
    other_metal = ring(metal, "layer", 1)
    other_start = ring(start_drop, "layer", 1)
    mine = scatter(profiles, time_weight, slot_cell, inst_count, (rows, cols))
    theirs = ring(mine, "layer", 1)
    planes = (flag, metal, other_metal, start_drop, other_start, via_density, pad, mine, theirs)
    first, last = strip_call(rows_kernel, (64, cols), "rows", *planes)
    after, before = ring(first, "gx", -1), ring(last, "gx", 1)
    first, last = strip_call(cols_kernel, (rows + 16, LANES), "cols", *planes, after, before)
    right, left = ring(first, GY, -1), ring(last, GY, 1)
    devices = lax.axis_size(ALL)
    inv, r0, s1, s2, s3, moments = basis(devices, *planes, after, before, right, left)
    sums = lax.all_to_all(moments, ALL, 0, 0, tiled=True)
    return update(flag, sums, start_drop, inv, r0, s1, s2, s3)


def solution(mesh):
    split = Mesh(
        mesh.devices.reshape(mesh.shape["gx"], 4, 8, mesh.shape["layer"]),
        ("gx", "gy_0", "gy_1", "layer"),
    )
    grid = P("layer", "gx", GY)
    return jax.shard_map(
        per_device,
        mesh=split,
        in_specs=(P("layer", "gx", GY, None), P(), grid, grid, grid, P("gx", GY), P("gx", GY), grid),
        out_specs=(grid, grid),
        check_vma=False,
    )
```

time: 91.2 us -> 79.9 us (0.88); the launches traced: 90 us -> 79.6 us
  starting transfers between devices: 21.1 us -> 13.3 us
  local copies, waits for them, and re-layouts: 8.4 us -> 1.7 us
  Pallas kernels: 25.8 us -> 29.5 us
    ppermute x7, starting transfers between devices: 21.1 us -> 13.3 us  [ring(): lax.ppermute(value, axes, [(i, (i + shift) % count) for i in range(count)])]
    unnamed x22 -> x10, local copies, waits for them, and re-layouts: 7.65 us -> 0.96 us
    pallas_call x1, Pallas kernels: 4.03 us -> 9.95 us  [scatter(): pl.pallas_call(scatter_kernel, out_shape=jax.ShapeDtypeStruct(tile, jnp.f...]
    pallas_call x1, Pallas kernels: 16.1 us -> 14.3 us  [basis(): pl.pallas_call(basis_kernel, out_shape=(jax.ShapeDtypeStruct(own, jnp.flo...]
  transfers between devices with their start and end apart: 7 -> 7, of which waited for: 5 -> 5; matrix products, arithmetic and copies ran while one was open for 1% -> 1% of each run, Pallas kernels for 4% -> 12%
where the time goes in v2:
time: 79.9 us; the launch traced here: 79.6 us
  Pallas kernels  29.5 us (37%)
  blocking collectives  20.7 us (26%)
  starting transfers between devices  13.3 us (17%)
  waiting for transfers between devices  13.1 us (16%)
  local copies, waits for them, and re-layouts  1.7 us (2%)
  between operations  1.35 us (2%)
    all_to_all x1, blocking collectives, per_device(): sums = lax.all_to_all(moments, ALL, 0, 0, tiled=True)  20.7 us
    pallas_call x1, Pallas kernels, basis(): pl.pallas_call(basis_kernel, out_shape=(jax.ShapeDtypeStruct(own, jnp.flo...  14.3 us
    ppermute x7, starting transfers between devices, ring(): lax.ppermute(value, axes, [(i, (i + shift) % count) for i in range(count)])  13.3 us
    ppermute x7, waiting for transfers between devices, ring(): lax.ppermute(value, axes, [(i, (i + shift) % count) for i in range(count)])  13.1 us
    pallas_call x1, Pallas kernels, scatter(): pl.pallas_call(scatter_kernel, out_shape=jax.ShapeDtypeStruct(tile, jnp.f...  9.95 us
    pallas_call x2, Pallas kernels, strip_call(): pl.pallas_call(kernel, out_shape=(jax.ShapeDtypeStruct(shape, jnp.float32...  2.76 us
    pallas_call x1, Pallas kernels, update(): pl.pallas_call(update_kernel, out_shape=(shape, shape), in_specs=[SMEM] +...  2.48 us
  transfers between devices with their start and end apart: 7, of which 5 were waited for; matrix products, arithmetic and copies ran while one was open for 1% of the time, Pallas kernels for 12%

profile of v2, /device:TPU:1, one launch (start us, length us, event | category | flops | bytes accessed | tf_op | source)
XLA Modules:
  0.0 79.6 jit_solution(8176886514071652215)
XLA Ops:
  0.6 3.3 %collective-permute-start = (f32[3,128,512]{2,1,0:T(8,128)}, f32[3,128,512]{2,1,0:T(8,128)S(1)}, u32[]{:S(2)}, u32[]{:S(2)}) collective-permute-start(f32[3,128,512]{2,1,0:T(8,128)} %m.5), channel_id=1, source_target_pairs={{0,1},{1,0},{2,3},{3,2},{4,5},{5,4},{6,7},{7,6},{8,9},{9,8},{10,11... | collective-permute-start | bytes 2359304 | tf_op jit(solution)/shard_map/ppermute | solution.py:385
  4.0 0.1 collective-permute-start.1
  4.7 0.7 reshape.19.weight_ref
  5.4 0.0 copy-start
  5.4 0.0 copy-start.1
  5.4 0.0 copy-start.2
  5.4 9.9 %scatter.1.mine = f32[128,512]{1,0:T(8,128)} custom-call(s32[1]{0:T(128)} %bitcast.12.count_ref, bf16[1,256]{1,0:T(2,128)(2,1)S(1)} %reshape.19.weight_ref, bf16[16384,256]{1,0:T(8,128)(2,1)} %bitcast.15, s32[1,16384]{1,0:T(1,128)} %bitcast.16), custom_call_target="tpu_custom_call" | custom-call | flops 6442450944 | bytes 8388608 | tf_op jit(solution)/shard_map/scatter/pallas_call | solution.py:77
  15.3 0.5 collective-permute-start.2
  15.8 0.1 stack.39.flag
  15.9 1.4 %collective-permute-done.2.theirs = f32[128,512]{1,0:T(8,128)} collective-permute-done((f32[128,512]{1,0:T(8,128)}, f32[128,512]{1,0:T(8,128)}, u32[]{:S(2)}, u32[]{:S(2)}) %collective-permute-start.2) | collective-permute-done | bytes 262176 | tf_op jit(solution)/shard_map/ppermute | solution.py:385
  17.3 0.0 collective-permute-done.om
  17.3 0.0 collective-permute-done.1.os
  17.3 0.0 copy-done
  17.3 0.0 copy-done.1
  17.4 0.0 copy-done.2
  17.4 0.0 copy-start.3
  17.4 0.9 %copy-done.3 = f32[128,512]{1,0:T(8,128)S(1)} copy-done((f32[128,512]{1,0:T(8,128)S(1)}, f32[128,512]{1,0:T(8,128)}, u32[]{:S(2)}) %copy-start.3) | copy-done | bytes 262168
  18.3 0.0 copy-start.4
  18.3 1.1 %rows.1 = (f32[64,512]{1,0:T(8,128)S(1)}, f32[64,512]{1,0:T(8,128)S(1)}) custom-call(s32[5]{0:T(128)S(1)} %stack.39.flag, f32[3,128,512]{2,1,0:T(8,128)S(1)} %copy-done.1, f32[3,128,512]{2,1,0:T(8,128)S(1)} %collective-permute-done.om, f32[3,128,512]{2,1,0:T(8,128)S(1)} %copy-done, f32[3,128,512]{2,1,0:T(8,128)S(1)} %collective-permute-done.1.os, ...), custom_call_target="tpu_custom_call" | custom-call | tf_op jit(solution)/shard_map/rows/pallas_call | solution.py:167
  19.4 1.1 %collective-permute-start.3 = (f32[64,512]{1,0:T(8,128)S(1)}, f32[64,512]{1,0:T(8,128)S(1)}, u32[]{:S(2)}, u32[]{:S(2)}) collective-permute-start(f32[64,512]{1,0:T(8,128)S(1)} %get-tuple-element.12), channel_id=1, source_target_pairs={{0,192},{64,0},{128,64},{192,128},{1,193},{65,1},{129,65},{193,129... | collective-permute-start | bytes 393224 | tf_op jit(solution)/shard_map/ppermute | solution.py:385
  20.5 0.5 collective-permute-start.4
  21.0 3.2 %collective-permute-done.3.after = f32[64,512]{1,0:T(8,128)S(1)} collective-permute-done((f32[64,512]{1,0:T(8,128)S(1)}, f32[64,512]{1,0:T(8,128)S(1)}, u32[]{:S(2)}, u32[]{:S(2)}) %collective-permute-start.3) | collective-permute-done | bytes 131104 | tf_op jit(solution)/shard_map/ppermute | solution.py:385
  24.2 1.9 %collective-permute-done.4.before = f32[64,512]{1,0:T(8,128)S(1)} collective-permute-done((f32[64,512]{1,0:T(8,128)S(1)}, f32[64,512]{1,0:T(8,128)S(1)}, u32[]{:S(2)}, u32[]{:S(2)}) %collective-permute-start.4) | collective-permute-done | bytes 131104 | tf_op jit(solution)/shard_map/ppermute | solution.py:385
  26.1 1.6 %cols.1 = (f32[144,128]{1,0:T(8,128)S(1)}, f32[144,128]{1,0:T(8,128)S(1)}) custom-call(s32[5]{0:T(128)S(1)} %stack.39.flag, f32[3,128,512]{2,1,0:T(8,128)S(1)} %copy-done.1, f32[3,128,512]{2,1,0:T(8,128)S(1)} %collective-permute-done.om, f32[3,128,512]{2,1,0:T(8,128)S(1)} %copy-done, f32[3,128,512]{2,1,0:T(8,128)S(1)} %collective-permute-done.1.os, ...), custom_call_target="tpu_custom_call" | custom-call | tf_op jit(solution)/shard_map/cols/pallas_call | solution.py:167
  27.8 7.8 %collective-permute-start.5 = (f32[144,128]{1,0:T(8,128)S(1)}, f32[144,128]{1,0:T(8,128)S(1)}, u32[]{:S(2)}, u32[]{:S(2)}) collective-permute-start(f32[144,128]{1,0:T(8,128)S(1)} %get-tuple-element.14), channel_id=1, source_target_pairs={{0,62},{2,0},{4,2},{6,4},{8,6},{10,8},{12,10},{14,12},{16,14},{18,... | collective-permute-start | bytes 221192 | tf_op jit(solution)/shard_map/ppermute | solution.py:385
  35.6 0.0 collective-permute-start.6
  35.6 1.4 %collective-permute-done.5.right = f32[144,128]{1,0:T(8,128)S(1)} collective-permute-done((f32[144,128]{1,0:T(8,128)S(1)}, f32[144,128]{1,0:T(8,128)S(1)}, u32[]{:S(2)}, u32[]{:S(2)}) %collective-permute-start.5) | collective-permute-done | bytes 73760 | tf_op jit(solution)/shard_map/ppermute | solution.py:385
  37.0 5.1 %collective-permute-done.6.left = f32[144,128]{1,0:T(8,128)S(1)} collective-permute-done((f32[144,128]{1,0:T(8,128)S(1)}, f32[144,128]{1,0:T(8,128)S(1)}, u32[]{:S(2)}, u32[]{:S(2)}) %collective-permute-start.6) | collective-permute-done | bytes 73760 | tf_op jit(solution)/shard_map/ppermute | solution.py:385
  42.1 0.0 copy-done.4
  42.1 14.3 %basis.1 = (f32[3,128,512]{2,1,0:T(8,128)S(1)}, f32[3,128,512]{2,1,0:T(8,128)S(1)}, f32[3,128,512]{2,1,0:T(8,128)S(1)}, f32[3,128,512]{2,1,0:T(8,128)S(1)}, f32[...) custom-call(s32[5]{0:T(128)S(1)} %stack.39.flag, f32[3,128,512]{2,1,0:T(8,128)S(1)} %copy-done.1, ...), custom_call_target="tpu_custom_call" | custom-call | tf_op jit(solution)/shard_map/basis/pallas_call | solution.py:319
  56.5 20.7 %all_to_all.11 = f32[256,1,128]{2,1,0:T(1,128)S(1)} all-to-all(f32[256,1,128]{2,1,0:T(1,128)S(1)} %bitcast.14), channel_id=1, replica_groups=mesh['gx'=4,'gy_0'=4,'gy_1'=8,'layer'=2] {'gx','gy_0','gy_1','layer'}, dimensions={0} | all-to-all | bytes 262144 | tf_op jit(solution)/shard_map/all_to_all | solution.py:411
  77.2 2.5 %update.1 = (f32[3,128,512]{2,1,0:T(8,128)}, f32[3,128,512]{2,1,0:T(8,128)}) custom-call(s32[5]{0:T(128)S(1)} %stack.39.flag, f32[256,128]{1,0:T(8,128)S(1)} %bitcast.13, f32[3,128,512]{2,1,0:T(8,128)S(1)} %copy-done, f32[3,128,512]{2,1,0:T(8,128)S(1)} %get-tuple-element.17.inv, f32[3,128,512]{2,1,0:T(8,128)S(1)} %get-tuple-element.18.r0_ref, ...), custom_call_target="tpu_custom_call" | custom-call | tf_op jit(solution)/shard_map/update/pallas_call | solution.py:373
Async XLA Ops:
  0.6 16.7 %collective-permute-start = (f32[3,128,512]{2,1,0:T(8,128)}, f32[3,128,512]{2,1,0:T(8,128)S(1)}, u32[]{:S(2)}, u32[]{:S(2)}) collective-permute-start(f32[3,128,512]{2,1,0:T(8,128)} %m.5), channel_id=1, source_target_pairs={{0,1},{1,0},{2,3},{3,2},{4,5},{5,4},{6,7},{7,6},{8,9},{9,8},{10,11... | collective-permute-start | bytes 2359304 | tf_op jit(solution)/shard_map/ppermute | solution.py:385
  4.0 13.4 %collective-permute-start.1 = (f32[3,128,512]{2,1,0:T(8,128)}, f32[3,128,512]{2,1,0:T(8,128)S(1)}, u32[]{:S(2)}, u32[]{:S(2)}) collective-permute-start(f32[3,128,512]{2,1,0:T(8,128)} %start.1), channel_id=1, source_target_pairs={{0,1},{1,0},{2,3},{3,2},{4,5},{5,4},{6,7},{7,6},{8,9},{9,8},{10,11... | collective-permute-start | bytes 2359304 | tf_op jit(solution)/shard_map/ppermute | solution.py:385
  5.4 12.0 %copy-start = (f32[3,128,512]{2,1,0:T(8,128)S(1)}, f32[3,128,512]{2,1,0:T(8,128)}, u32[]{:S(2)}) copy-start(f32[3,128,512]{2,1,0:T(8,128)} %start.1) | copy-start | bytes 2359300
  5.4 12.0 %copy-start.1 = (f32[3,128,512]{2,1,0:T(8,128)S(1)}, f32[3,128,512]{2,1,0:T(8,128)}, u32[]{:S(2)}) copy-start(f32[3,128,512]{2,1,0:T(8,128)} %m.5) | copy-start | bytes 2359300
  5.4 12.0 %copy-start.2 = (f32[128,512]{1,0:T(8,128)S(1)}, f32[128,512]{1,0:T(8,128)}, u32[]{:S(2)}) copy-start(f32[128,512]{1,0:T(8,128)} %via.5) | copy-start | bytes 786436
  15.3 2.0 %collective-permute-start.2 = (f32[128,512]{1,0:T(8,128)}, f32[128,512]{1,0:T(8,128)}, u32[]{:S(2)}, u32[]{:S(2)}) collective-permute-start(f32[128,512]{1,0:T(8,128)} %scatter.1.mine), channel_id=1, source_target_pairs={{0,1},{1,0},{2,3},{3,2},{4,5},{5,4},{6,7},{7,6},{8,9},{9,8},{10,11... | collective-permute-start | bytes 786440 | tf_op jit(solution)/shard_map/ppermute | solution.py:385
  17.4 1.0 %copy-start.3 = (f32[128,512]{1,0:T(8,128)S(1)}, f32[128,512]{1,0:T(8,128)}, u32[]{:S(2)}) copy-start(f32[128,512]{1,0:T(8,128)} %pad.5) | copy-start | bytes 786436
  18.3 23.8 %copy-start.4 = (f32[128,512]{1,0:T(8,128)S(1)}, f32[128,512]{1,0:T(8,128)}, u32[]{:S(2)}) copy-start(f32[128,512]{1,0:T(8,128)} %pad.5) | copy-start | bytes 786436
  19.4 4.8 %collective-permute-start.3 = (f32[64,512]{1,0:T(8,128)S(1)}, f32[64,512]{1,0:T(8,128)S(1)}, u32[]{:S(2)}, u32[]{:S(2)}) collective-permute-start(f32[64,512]{1,0:T(8,128)S(1)} %get-tuple-element.12), channel_id=1, source_target_pairs={{0,192},{64,0},{128,64},{192,128},{1,193},{65,1},{129,65},{193,129... | collective-permute-start | bytes 393224 | tf_op jit(solution)/shard_map/ppermute | solution.py:385
  20.5 5.6 %collective-permute-start.4 = (f32[64,512]{1,0:T(8,128)S(1)}, f32[64,512]{1,0:T(8,128)S(1)}, u32[]{:S(2)}, u32[]{:S(2)}) collective-permute-start(f32[64,512]{1,0:T(8,128)S(1)} %get-tuple-element.13), channel_id=1, source_target_pairs={{0,64},{64,128},{128,192},{192,0},{1,65},{65,129},{129,193},{193,1... | collective-permute-start | bytes 393224 | tf_op jit(solution)/shard_map/ppermute | solution.py:385
  27.8 9.2 %collective-permute-start.5 = (f32[144,128]{1,0:T(8,128)S(1)}, f32[144,128]{1,0:T(8,128)S(1)}, u32[]{:S(2)}, u32[]{:S(2)}) collective-permute-start(f32[144,128]{1,0:T(8,128)S(1)} %get-tuple-element.14), channel_id=1, source_target_pairs={{0,62},{2,0},{4,2},{6,4},{8,6},{10,8},{12,10},{14,12},{16,14},{18,... | collective-permute-start | bytes 221192 | tf_op jit(solution)/shard_map/ppermute | solution.py:385
  35.6 6.5 %collective-permute-start.6 = (f32[144,128]{1,0:T(8,128)S(1)}, f32[144,128]{1,0:T(8,128)S(1)}, u32[]{:S(2)}, u32[]{:S(2)}) collective-permute-start(f32[144,128]{1,0:T(8,128)S(1)} %get-tuple-element.15), channel_id=1, source_target_pairs={{0,2},{2,4},{4,6},{6,8},{8,10},{10,12},{12,14},{14,16},{16,18},{18... | collective-permute-start | bytes 221192 | tf_op jit(solution)/shard_map/ppermute | solution.py:385

commit v3 on v2

v3 whole, which is shorter than its diff:
```python
import jax
import jax.numpy as jnp
from jax import lax
from jax.experimental import pallas as pl
from jax.experimental.pallas import tpu as pltpu
from jax.sharding import Mesh
from jax.sharding import PartitionSpec as P

ALL = ("gx", "gy_0", "gy_1", "layer")
GY = ("gy_0", "gy_1")
HALO = 4
LANES = 128
SIDE = 256
CHUNK = 4096
TINY = 1e-30
MOMENTS = 6

VMEM = pl.BlockSpec(memory_space=pltpu.VMEM)
HBM = pl.BlockSpec(memory_space=pltpu.HBM)
SMEM = pl.BlockSpec(memory_space=pltpu.SMEM)


def params(mebibytes):
    return pltpu.CompilerParams(vmem_limit_bytes=mebibytes << 20)


def scatter_kernel(count_ref, weight_ref, profile_hbm, cell_hbm, out_ref, profile_ref, cell_ref, total_ref, sems):
    half = out_ref.shape[0]
    blocks = profile_ref.shape[0] // CHUNK
    fetches = [pltpu.make_async_copy(cell_hbm, cell_ref, sems.at[blocks])]
    for block in range(blocks):
        span = pl.ds(block * CHUNK, CHUNK)
        fetches.append(
            pltpu.make_async_copy(profile_hbm.at[span], profile_ref.at[span], sems.at[block])
        )
    for fetch in fetches:
        fetch.start()
    total_ref[...] = jnp.zeros_like(total_ref)
    times = weight_ref.shape[0]
    weight = jnp.broadcast_to(weight_ref[...].reshape(1, times), (16, times))
    ids = lax.broadcasted_iota(jnp.int32, (SIDE, CHUNK), 0).astype(jnp.float32).astype(jnp.bfloat16)
    zero, one = jnp.bfloat16(0), jnp.bfloat16(1)
    fetches[0].wait()

    def add_block(block, _):
        first = pl.multiple_of(block * CHUNK, CHUNK)
        span = pl.ds(first, CHUNK)
        pltpu.make_async_copy(profile_hbm.at[span], profile_ref.at[span], sems.at[block]).wait()
        amount = lax.dot_general(
            weight,
            profile_ref[span, :],
            (((1,), (1,)), ((), ())),
            preferred_element_type=jnp.float32,
        )[:1]
        position = first + lax.broadcasted_iota(jnp.int32, (1, CHUNK), 1)
        amount = jnp.where(position < count_ref[0], amount, 0.0)
        high = amount.astype(jnp.bfloat16)
        low = (amount - high.astype(jnp.float32)).astype(jnp.bfloat16)
        cell = cell_ref[:, span]
        row = ((cell >> 9) + ((cell >> 8) & 1) * half).astype(jnp.float32).astype(jnp.bfloat16)
        col = (cell & (SIDE - 1)).astype(jnp.float32).astype(jnp.bfloat16)
        here = ids == row
        left = jnp.concatenate([jnp.where(here, high, zero), jnp.where(here, low, zero)], axis=0)
        right = jnp.where(ids == col, one, zero)
        total_ref[...] += lax.dot_general(
            left, right, (((1,), (1,)), ((), ())), preferred_element_type=jnp.float32
        )
        return 0

    lax.fori_loop(0, blocks, add_block, 0)
    both = total_ref[:SIDE, :] + total_ref[SIDE:, :]
    out_ref[:, :SIDE] = both[:half]
    out_ref[:, SIDE:] = both[half:]


def scatter(profiles, time_weight, slot_cell, inst_count, tile):
    slots, times = profiles.shape[-2:]
    return pl.pallas_call(
        scatter_kernel,
        out_shape=jax.ShapeDtypeStruct(tile, jnp.float32),
        in_specs=[SMEM, VMEM, HBM, HBM],
        out_specs=VMEM,
        scratch_shapes=[
            pltpu.VMEM((slots, times), jnp.bfloat16),
            pltpu.VMEM((1, slots), jnp.int32),
            pltpu.VMEM((2 * SIDE, SIDE), jnp.float32),
            pltpu.SemaphoreType.DMA((slots // CHUNK + 1,)),
        ],
        compiler_params=params(24),
        cost_estimate=pl.CostEstimate(
            flops=6 * slots * SIDE * SIDE, bytes_accessed=2 * slots * times, transcendentals=0
        ),
        name="scatter",
    )(
        inst_count.reshape(1),
        time_weight,
        pltpu.with_memory_space_constraint(profiles.reshape(slots, times), pltpu.HBM),
        pltpu.with_memory_space_constraint(slot_cell.reshape(1, slots), pltpu.HBM),
    )


def plane_readers(metal, other_metal, start, other_start, via, pad, mine, theirs, flip):
    readers = []
    for own, other in ((metal, other_metal), (start, other_start)):
        for ref in (own, other):
            for k in range(3):
                index = jnp.where(flip == 1, 2 - k, k)
                readers.append(lambda rows, cols, ref=ref, index=index: ref[index, rows, cols])
    readers.append(lambda rows, cols: via[rows, cols])
    readers.append(lambda rows, cols: pad[rows, cols])
    readers.append(lambda rows, cols: mine[rows, cols] + theirs[rows, cols])
    return readers


def rows_kernel(flag, m, om, s, os, via, pad, mine, theirs, one_ref, two_ref):
    rows = m.shape[1]
    readers = plane_readers(m, om, s, os, via, pad, mine, theirs, flag[0])
    low = lax.broadcasted_iota(jnp.int32, (8, m.shape[2]), 0) < HALO
    for pair in range(0, len(readers), 2):
        packed = []
        for start in (0, rows - 8):
            span = slice(start, start + 8)
            here = readers[pair](span, slice(None))
            there = here
            if pair + 1 < len(readers):
                there = pltpu.roll(readers[pair + 1](span, slice(None)), HALO, 0)
            packed.append(jnp.where(low, here, there) if start == 0 else jnp.where(low, there, here))
        first, last = packed
        span = slice(pair * HALO, pair * HALO + 8)
        one_ref[span, :] = jnp.where(flag[5] == 1, first, last)
        two_ref[span, :] = jnp.where(flag[5] == 1, last, first)


def row_halos(one, two, plane, cols, flag):
    span = slice(plane // 2 * 8, plane // 2 * 8 + 8)
    one, two = one[span, cols], two[span, cols]
    above = jnp.where(flag[1] == 1, jnp.where(flag[5] == 1, one, two), 0.0)
    below = jnp.where(flag[2] == 1, jnp.where(flag[5] == 1, two, one), 0.0)
    if plane % 2:
        return pltpu.roll(above, HALO, 0), pltpu.roll(below, HALO, 0)
    return above, below


def cols_kernel(flag, m, om, s, os, via, pad, mine, theirs, rows_one, rows_two, one_ref, two_ref):
    rows, cols = m.shape[1], m.shape[2]
    readers = plane_readers(m, om, s, os, via, pad, mine, theirs, flag[0])
    lane = lax.broadcasted_iota(jnp.int32, (rows + 16, LANES), 1)
    sides = []
    for start in (0, cols - LANES):
        span = slice(start, start + LANES)
        packed = jnp.zeros((rows + 16, LANES), jnp.float32)
        for plane, read in enumerate(readers):
            above, below = row_halos(rows_one, rows_two, plane, span, flag)
            values = jnp.concatenate([above, read(slice(None), span), below], axis=0)
            where = HALO * plane if start == 0 else (LANES - HALO + HALO * plane) % LANES
            turned = pltpu.roll(values, HALO * plane, 1) if plane else values
            packed = jnp.where((lane >= where) & (lane < where + HALO), turned, packed)
        sides.append(packed)
    first, last = sides
    one_ref[...] = jnp.where(flag[6] == 1, first, last)
    two_ref[...] = jnp.where(flag[6] == 1, last, first)


def col_halo(one, two, plane, flag):
    after = jnp.where(flag[6] == 1, two[...], one[...])
    before = jnp.where(flag[6] == 1, one[...], two[...])
    lane = lax.broadcasted_iota(jnp.int32, after.shape, 1)
    where = HALO * plane
    back = (LANES - HALO + where) % LANES
    tail = (lane >= where) & (lane < where + HALO) & (flag[4] == 1)
    head = (lane >= back) & (lane < back + HALO) & (flag[3] == 1)
    values = jnp.where(tail, after, jnp.where(head, before, 0.0))
    return pltpu.roll(values, (LANES - where) % LANES, 1) if plane else values


def strip_call(kernel, shape, name, *operands):
    return pl.pallas_call(
        kernel,
        out_shape=(jax.ShapeDtypeStruct(shape, jnp.float32),) * 2,
        in_specs=[SMEM] + [VMEM] * (len(operands) - 1),
        out_specs=(VMEM, VMEM),
        compiler_params=params(24),
        name=name,
    )(*operands)


OWN = 16


def harmonic(values, beside):
    return 2.0 * values * beside / jnp.maximum(values + beside, TINY)


def row_span(i, off=0):
    return pl.ds(OWN + 8 * i + off, 8)


def links_kernel(
    flag, m, om, s, os, via, pad, mine, theirs, rows_one, rows_two,
    row_link, col_link, up_link, total_ref, r_ref, metal_side, start_side,
    metal_ref, start_ref, column_ref,
):
    rows, cols = m.shape[1], m.shape[2]
    tiles, strips = cols // LANES, rows // 8
    readers = plane_readers(m, om, s, os, via, pad, mine, theirs, flag[0])
    places = [(metal_ref, k) for k in range(6)] + [(start_ref, k) for k in range(6)]
    places += [(column_ref, k) for k in range(3)]
    for plane, (read, (ref, k)) in enumerate(zip(readers, places)):
        for j in range(tiles):
            span = slice(j * LANES, j * LANES + LANES)
            above, below = row_halos(rows_one, rows_two, plane, span, flag)
            ref[k, j, OWN - 8 : OWN, :] = above
            ref[k, j, OWN : OWN + rows, :] = read(slice(None), span)
            ref[k, j, OWN + rows : OWN + rows + 8, :] = below

    lane = lax.broadcasted_iota(jnp.int32, (tiles, 8, LANES), 2)
    none = jnp.zeros((1, 8, LANES), jnp.float32)
    weight = jnp.where(flag[0] == 1, 1.0, 0.0)

    def after_col(values):
        turned = pltpu.roll(values, LANES - 1, 2)
        return jnp.where(lane == LANES - 1, jnp.concatenate([turned[1:], none], 0), turned)

    def before_col(values):
        turned = pltpu.roll(values, 1, 2)
        return jnp.where(lane == 0, jnp.concatenate([none, turned[:-1]], 0), turned)

    def body(i, _):
        i = i - 1

        def get(ref, k, off=0):
            return ref[k, :, row_span(i, off), :]

        up, metal, x = None, get(metal_ref, 0), get(start_ref, 0)
        x_before = None
        for k in range(6):
            row = harmonic(metal, get(metal_ref, k, 1))
            row_link[k, :, row_span(i), :] = row
            row_before = get(row_link, k, -1)
            col = harmonic(metal, after_col(metal))
            col_link[k, :, row_span(i), :] = col
            total = row + row_before + col + before_col(col)
            near = row * get(start_ref, k, 1) + row_before * get(start_ref, k, -1)
            near = near + col * after_col(x) + before_col(col * x)
            if k > 0:
                total = total + up
                near = near + up * x_before
            metal_side[k, :, row_span(i), :] = jnp.concatenate([metal[:1], metal[-1:]], 0)
            start_side[k, :, row_span(i), :] = jnp.concatenate([x[:1], x[-1:]], 0)
            x_here = x
            if k < 5:
                metal_after, x = get(metal_ref, k + 1), get(start_ref, k + 1)
                up = get(column_ref, 0) * harmonic(metal, metal_after)
                metal = metal_after
                up_link[k, :, row_span(i), :] = up
                total = total + up
                near = near + up * x
            if k == 0:
                total = total + weight * get(column_ref, 1)
                near = near + (1.0 - weight) * get(column_ref, 2)
            if k == 5:
                total = total + (1.0 - weight) * get(column_ref, 1)
                near = near + weight * get(column_ref, 2)
            total_ref[k, :, row_span(i), :] = total
            r_ref[k, :, row_span(i), :] = near - total * x_here
            x_before = x_here
        return 0

    lax.fori_loop(0, strips + 2, body, 0)


def links(*operands):
    own = operands[1].shape
    counts = [(6, 4), (6, 4), (5, 4), (6, 4), (6, 4), (6, 2), (6, 2)]
    height = own[1] + 2 * OWN
    return pl.pallas_call(
        links_kernel,
        out_shape=[jax.ShapeDtypeStruct(c + (height, LANES), jnp.float32) for c in counts],
        in_specs=[SMEM] + [VMEM] * (len(operands) - 1),
        out_specs=[VMEM] * len(counts),
        scratch_shapes=[pltpu.VMEM((count, 4, height, LANES), jnp.float32) for count in (6, 6, 3)],
        compiler_params=params(24),
        cost_estimate=pl.CostEstimate(flops=80_000_000, bytes_accessed=12_000_000, transcendentals=2_000_000),
        name="links",
    )(*operands)


def basis_kernel(
    flag, cols_one, cols_two, row_link, col_link, up_link, total_ref, r_ref, metal_side, start_side,
    inv_out, r0_out, s1_out, s2_out, s3_out, moments_ref,
    metal_ref, start_ref, column_ref, row_far, col_last, col_far, up_far, inv_ref, z0_ref, z1_ref, z2_ref,
):
    rows, tiles = inv_out.shape[1], col_link.shape[1]
    strips = rows // 8
    inner = slice(OWN - 8, OWN + rows + 8)
    for plane in range(15):
        ref = (metal_ref, start_ref, column_ref)[plane // 6]
        ref[plane % 6, inner, :] = col_halo(cols_one, cols_two, plane, flag)

    weight = jnp.where(flag[0] == 1, 1.0, 0.0)
    lane = lax.broadcasted_iota(jnp.int32, (8, LANES), 1)
    zero = jnp.zeros((8, LANES), jnp.float32)

    def later(values):
        return pltpu.roll(values, LANES - 1, values.ndim - 1)

    def earlier(values):
        return pltpu.roll(values, 1, values.ndim - 1)

    def put_own(ref, k, i, values):
        for j in range(tiles):
            ref[k, pl.ds(8 * i, 8), j * LANES : j * LANES + LANES] = values[j]

    def fold(values):
        return jnp.sum(values[:tiles], axis=0)

    def sweep(body, count):
        body(-1, None)
        sums = lax.fori_loop(0, strips, body, (zero,) * count)
        body(strips, None)
        return sums

    def first(i, sums):
        def get(ref, k, off=0):
            return ref[k, row_span(i, off), :]

        energy = None if sums is None else sums[0]
        up = None
        for k in range(6):
            metal, x = get(metal_ref, k), get(start_ref, k)
            metal_first, metal_last = metal_side[k, 0, row_span(i), :], metal_side[k, 1, row_span(i), :]
            x_first, x_last = start_side[k, 0, row_span(i), :], start_side[k, 1, row_span(i), :]
            row = harmonic(metal, get(metal_ref, k, 1))
            row_far[k, row_span(i), :] = row
            row_before = get(row_far, k, -1)
            metal_later = later(metal)
            last = jnp.where(lane == LANES - 1, harmonic(metal_last, metal_later), 0.0)
            col_last[k, row_span(i), :] = col_link[k, tiles - 1, row_span(i), :] + last
            col = harmonic(metal, jnp.where(lane == LANES - 1, later(metal_first), metal_later))
            col_far[k, row_span(i), :] = col
            col_earlier, x_later = earlier(col), later(x)
            total = row + row_before + col + jnp.where(lane == 0, earlier(last), col_earlier)
            near = row * get(start_ref, k, 1) + row_before * get(start_ref, k, -1)
            near = near + col * jnp.where(lane == LANES - 1, later(x_first), x_later)
            near = near + jnp.where(lane == 0, earlier(last * x_last), earlier(col * x))
            if k > 0:
                total = total + up
                near = near + up * get(start_ref, k - 1)
            if k < 5:
                up = get(column_ref, 0) * harmonic(metal, get(metal_ref, k + 1))
                up_far[k, row_span(i), :] = up
                total = total + up
                near = near + up * get(start_ref, k + 1)
            if k == 0:
                total = total + weight * get(column_ref, 1)
                near = near + (1.0 - weight) * get(column_ref, 2)
            if k == 5:
                total = total + (1.0 - weight) * get(column_ref, 1)
                near = near + weight * get(column_ref, 2)
            before = jnp.where(lane == 0, col_earlier, 0.0)
            totals, r = total_ref[k, :, row_span(i), :], r_ref[k, :, row_span(i), :]
            totals = [totals[0] + before, totals[1], totals[2], totals[3] + last, total]
            r = [
                r[0] + before * (earlier(x) - x_first),
                r[1],
                r[2],
                r[3] + last * (x_later - x_last),
                near - total * x,
            ]
            inv, r = 1.0 / jnp.maximum(jnp.stack(totals), TINY), jnp.stack(r)
            z = r * inv
            inv_ref[k, :, row_span(i), :] = inv
            z0_ref[k, :, row_span(i), :] = z
            if sums is not None and k < 3:
                put_own(inv_out, k, i, inv)
                put_own(r0_out, k, i, r)
                energy = energy + fold(z * r)
        return None if sums is None else (energy,)

    def step(source, target, out, planes):
        width = tiles if target is None else tiles + 1
        ends = lax.broadcasted_iota(jnp.int32, (width, 8, LANES), 2)

        def body(i, sums):
            def get(k, off=0):
                return source[k, :width, row_span(i, off), :]

            def whole(near_ref, far_ref, k, off=0):
                near = near_ref[k, :, row_span(i, off), :]
                if width == tiles:
                    return near
                return jnp.concatenate([near, far_ref[k, row_span(i, off), :][None]], 0)

            totals = sums
            up, z_before = None, None
            z = source[0, :, row_span(i), :]
            for k in range(planes):
                col = jnp.concatenate(
                    [
                        col_link[k, : tiles - 1, row_span(i), :],
                        col_last[k, row_span(i), :][None],
                        col_far[k, row_span(i), :][None],
                    ],
                    0,
                )
                turned = later(z)
                following = jnp.concatenate([turned[1:], turned[:1]], 0)
                z_later = jnp.where(ends == LANES - 1, following[:width], turned[:width])
                turned = earlier(col * z)
                preceding = jnp.concatenate([turned[-1:], turned[:-1]], 0)
                near = col[:width] * z_later + jnp.where(ends == 0, preceding[:width], turned[:width])
                near = near + whole(row_link, row_far, k) * get(k, 1)
                near = near + whole(row_link, row_far, k, -1) * get(k, -1)
                if k > 0:
                    near = near + up * z_before
                z_after = source[k + 1, :, row_span(i), :]
                up = whole(up_link, up_far, k) if k < 5 else None
                if k < 5:
                    near = near + up * z_after[:width]
                z_here = z[:width]
                if target is not None:
                    fresh = near * inv_ref[k, :, row_span(i), :]
                    target[k, :, row_span(i), :] = fresh
                if sums is not None and k < 3:
                    put_own(out, k, i, near)
                    terms = (z_here * near,) if target is None else (z_here * near, fresh * near)
                    totals = tuple(a + fold(b) for a, b in zip(totals, terms))
                z_before, z = z_here, z_after
            return totals

        return body

    sums = sweep(first, 1)
    sums += sweep(step(z0_ref, z1_ref, s1_out, 5), 2)
    sums += sweep(step(z1_ref, z2_ref, s2_out, 4), 2)
    sums += lax.fori_loop(0, strips, step(z2_ref, None, s3_out, 3), (zero,))
    packed = zero
    for k, total in enumerate(sums):
        packed = jnp.where(lane == k, jnp.sum(total, keepdims=True), packed)
    moments_ref[...] = jnp.broadcast_to(packed[:1], moments_ref.shape)


def basis(devices, own, *operands):
    height = own[1] + 2 * OWN
    sides = (6, 6, 3, 6, 6, 6, 5)
    planes = (6, 6, 5, 4)
    return pl.pallas_call(
        basis_kernel,
        out_shape=(jax.ShapeDtypeStruct(own, jnp.float32),) * 5
        + (jax.ShapeDtypeStruct((devices, LANES), jnp.float32),),
        in_specs=[SMEM] + [VMEM] * (len(operands) - 1),
        out_specs=(VMEM,) * 6,
        scratch_shapes=[pltpu.VMEM((count, height, LANES), jnp.float32) for count in sides]
        + [pltpu.VMEM((count, 5, height, LANES), jnp.float32) for count in planes],
        compiler_params=params(20),
        name="basis",
    )(*operands)


def product(one, two, moments):
    total = 0.0
    for i, a in enumerate(one):
        for j, b in enumerate(two):
            total = total + a * b * moments[i + j]
    return total


def coefficients(moments, iterations):
    drops = [moments[i] - moments[i + 1] for i in range(MOMENTS - 1)]
    one = jnp.ones_like(moments[0])
    residual, direction, iterate = [one], [one], [0.0 * one] * iterations
    energy = moments[0]
    for iteration in range(iterations):
        step = energy / product(direction, direction, drops)
        iterate = [x + step * (direction[i] if i < len(direction) else 0.0) for i, x in enumerate(iterate)]
        image = [a - b for a, b in zip(direction + [0.0], [0.0] + direction)]
        residual = [a - step * b for a, b in zip(residual + [0.0], image)]
        if iteration + 1 < iterations:
            after = product(residual, residual, moments)
            ratio = after / energy
            direction = [a + ratio * b for a, b in zip(residual, direction + [0.0])]
            energy = after
    return iterate, residual


def update_kernel(
    flag, sums, start, inv, r0_ref, s1_ref, s2_ref, s3_ref, drop_out, residual_out, drop_ref, residual_ref, sems
):
    sums = jnp.sum(sums[...], axis=0, keepdims=True)
    lane = lax.broadcasted_iota(jnp.int32, sums.shape, 1)
    moments = [
        jnp.sum(jnp.where(lane == k, sums, 0.0), axis=1, keepdims=True) for k in range(MOMENTS)
    ]
    x, r = coefficients(moments, 3)
    copies = []
    for k in range(3):
        index = jnp.where(flag[0] == 1, 2 - k, k)
        r0, s1, s2 = r0_ref[k], s1_ref[k], s2_ref[k]
        drop_ref[k] = start[index] + inv[k] * (x[0] * r0 + x[1] * s1 + x[2] * s2)
        residual_ref[k] = r[0] * r0 + r[1] * s1 + r[2] * s2 + r[3] * s3_ref[k]
        copies.append(pltpu.make_async_copy(drop_ref.at[k], drop_out.at[index], sems.at[2 * k]))
        copies.append(pltpu.make_async_copy(residual_ref.at[k], residual_out.at[index], sems.at[2 * k + 1]))
        for copy in copies[-2:]:
            copy.start()
    for copy in copies:
        copy.wait()


def update(*operands):
    own = operands[2].shape
    shape = jax.ShapeDtypeStruct(own, jnp.float32)
    return pl.pallas_call(
        update_kernel,
        out_shape=(shape, shape),
        in_specs=[SMEM] + [VMEM] * (len(operands) - 1),
        out_specs=(HBM, HBM),
        scratch_shapes=[
            pltpu.VMEM(own, jnp.float32),
            pltpu.VMEM(own, jnp.float32),
            pltpu.SemaphoreType.DMA((6,)),
        ],
        compiler_params=params(24),
        name="update",
    )(*operands)


def trade(one, two, axes):
    count = lax.axis_size(axes)
    pairs = [(i, i ^ 1) for i in range(count)]
    shifted = [((i + 1) % count, (j + 1) % count) for i, j in pairs]
    return lax.ppermute(one, axes, pairs), lax.ppermute(two, axes, shifted)


def swap(value):
    return lax.ppermute(value, "layer", [(0, 1), (1, 0)])


def per_device(profiles, time_weight, slot_cell, inst_count, metal, via_density, pad, start_drop):
    rows, cols = metal.shape[1], metal.shape[2]
    gx, gy, layer = lax.axis_index("gx"), lax.axis_index(GY), lax.axis_index("layer")
    flag = jnp.stack(
        [
            layer,
            gx > 0,
            gx < lax.axis_size("gx") - 1,
            gy > 0,
            gy < lax.axis_size(GY) - 1,
            gx % 2,
            gy % 2,
        ]
    ).astype(jnp.int32)
    other_metal = swap(metal)
    other_start = swap(start_drop)
    mine = scatter(profiles, time_weight, slot_cell, inst_count, (rows, cols))
    theirs = swap(mine)
    planes = (flag, metal, other_metal, start_drop, other_start, via_density, pad, mine, theirs)
    row_strips = trade(*strip_call(rows_kernel, (64, cols), "rows", *planes), "gx")
    col_strips = trade(*strip_call(cols_kernel, (rows + 16, LANES), "cols", *planes, *row_strips), GY)
    prepared = links(*planes, *row_strips)
    devices = lax.axis_size(ALL)
    inv, r0, s1, s2, s3, moments = basis(devices, metal.shape, flag, *col_strips, *prepared)
    sums = lax.all_to_all(moments, ALL, 0, 0, tiled=True)
    return update(flag, sums, start_drop, inv, r0, s1, s2, s3)


def solution(mesh):
    split = Mesh(
        mesh.devices.reshape(mesh.shape["gx"], 4, 8, mesh.shape["layer"]),
        ("gx", "gy_0", "gy_1", "layer"),
    )
    grid = P("layer", "gx", GY)
    return jax.shard_map(
        per_device,
        mesh=split,
        in_specs=(P("layer", "gx", GY, None), P(), grid, grid, grid, P("gx", GY), P("gx", GY), grid),
        out_specs=(grid, grid),
        check_vma=False,
    )
```

time: 79.9 us -> 74.7 us (0.935)
  waiting for transfers between devices: 13.1 us -> 5.99 us
  Pallas kernels: 29.5 us -> 31.7 us
    ppermute x7, waiting for transfers between devices: 13.1 us -> 5.99 us  [the longest x4 4.56 us: trade(): return (lax.ppermute(one, axes, pairs), lax.ppermute(two, axes, shifted))]
    pallas_call x0 -> x1, Pallas kernels: none -> 5.53 us  [links(): pl.pallas_call(links_kernel, out_shape=[jax.ShapeDtypeStruct(c + (height,...]
    pallas_call x1, Pallas kernels: 14.3 us -> 11.3 us  [basis(): pl.pallas_call(basis_kernel, out_shape=(jax.ShapeDtypeStruct(own, jnp.flo...]
  transfers between devices with their start and end apart: 7 -> 7, of which waited for: 5 -> 3; matrix products, arithmetic and copies ran while one was open for 1% -> 0% of each run, Pallas kernels for 12% -> 21%
where the time goes in v3:
time: 74.7 us; the launch traced here: 74.5 us
  Pallas kernels  31.7 us (42%)
  blocking collectives  20.5 us (27%)
  starting transfers between devices  13.2 us (18%)
  waiting for transfers between devices  5.99 us (8%)
  local copies, waits for them, and re-layouts  1.69 us (2%)
  between operations  1.39 us (2%)
    all_to_all x1, blocking collectives, per_device(): sums = lax.all_to_all(moments, ALL, 0, 0, tiled=True)  20.5 us
    pallas_call x1, Pallas kernels, basis(): pl.pallas_call(basis_kernel, out_shape=(jax.ShapeDtypeStruct(own, jnp.flo...  11.3 us
    pallas_call x1, Pallas kernels, scatter(): pl.pallas_call(scatter_kernel, out_shape=jax.ShapeDtypeStruct(tile, jnp.f...  9.95 us
    ppermute x4, starting transfers between devices, trade(): return (lax.ppermute(one, axes, pairs), lax.ppermute(two, axes, shifted))  9.27 us
    pallas_call x1, Pallas kernels, links(): pl.pallas_call(links_kernel, out_shape=[jax.ShapeDtypeStruct(c + (height,...  5.53 us
    ppermute x4, waiting for transfers between devices, trade(): return (lax.ppermute(one, axes, pairs), lax.ppermute(two, axes, shifted))  4.56 us
    ppermute x3, starting transfers between devices, swap(): return lax.ppermute(value, 'layer', [(0, 1), (1, 0)])  3.92 us
    pallas_call x2, Pallas kernels, strip_call(): pl.pallas_call(kernel, out_shape=(jax.ShapeDtypeStruct(shape, jnp.float32...  2.72 us
  transfers between devices with their start and end apart: 7, of which 3 were waited for; matrix products, arithmetic and copies ran while one was open for 0% of the time, Pallas kernels for 21%

profile of v3, /device:TPU:1, one launch (start us, length us, event | category | flops | bytes accessed | tf_op | source)
XLA Modules:
  0.0 74.5 jit_solution(4341859986227716438)
XLA Ops:
  0.6 3.3 %collective-permute-start = (f32[3,128,512]{2,1,0:T(8,128)}, f32[3,128,512]{2,1,0:T(8,128)S(1)}, u32[]{:S(2)}, u32[]{:S(2)}) collective-permute-start(f32[3,128,512]{2,1,0:T(8,128)} %m.5), channel_id=1, source_target_pairs={{0,1},{1,0},{2,3},{3,2},{4,5},{5,4},{6,7},{7,6},{8,9},{9,8},{10,11... | collective-permute-start | bytes 2359304 | tf_op jit(solution)/shard_map/ppermute | solution.py:535
  4.0 0.1 collective-permute-start.1
  4.7 0.0 copy-start.4
  4.7 0.6 copy-done.4
  5.4 0.0 copy-start
  5.4 0.0 copy-start.1
  5.4 0.0 copy-start.2
  5.4 10.0 %scatter.1.mine = f32[128,512]{1,0:T(8,128)} custom-call(s32[1]{0:T(128)} %bitcast.14.count_ref, bf16[256]{0:T(256)(128)(2,1)S(1)} %copy-done.4, bf16[16384,256]{1,0:T(8,128)(2,1)} %bitcast.17, s32[1,16384]{1,0:T(1,128)} %bitcast.18), custom_call_target="tpu_custom_call" | custom-call | flops 6442450944 | bytes 8388608 | tf_op jit(solution)/shard_map/scatter/pallas_call | solution.py:78
  15.3 0.5 collective-permute-start.2
  15.8 0.1 stack.47.flag
  15.9 1.4 %collective-permute-done.2.theirs = f32[128,512]{1,0:T(8,128)} collective-permute-done((f32[128,512]{1,0:T(8,128)}, f32[128,512]{1,0:T(8,128)}, u32[]{:S(2)}, u32[]{:S(2)}) %collective-permute-start.2) | collective-permute-done | bytes 262176 | tf_op jit(solution)/shard_map/ppermute | solution.py:535
  17.3 0.0 collective-permute-done.om
  17.3 0.0 collective-permute-done.1.os
  17.3 0.0 copy-done
  17.3 0.0 copy-done.1
  17.4 0.0 copy-done.2
  17.4 0.0 copy-start.3
  17.4 0.9 %copy-done.3 = f32[128,512]{1,0:T(8,128)S(1)} copy-done((f32[128,512]{1,0:T(8,128)S(1)}, f32[128,512]{1,0:T(8,128)}, u32[]{:S(2)}) %copy-start.3) | copy-done | bytes 262168
  18.3 1.1 %rows.1 = (f32[64,512]{1,0:T(8,128)S(1)}, f32[64,512]{1,0:T(8,128)S(1)}) custom-call(s32[7]{0:T(128)S(1)} %stack.47.flag, f32[3,128,512]{2,1,0:T(8,128)S(1)} %copy-done.1, f32[3,128,512]{2,1,0:T(8,128)S(1)} %collective-permute-done.om, f32[3,128,512]{2,1,0:T(8,128)S(1)} %copy-done, f32[3,128,512]{2,1,0:T(8,128)S(1)} %collective-permute-done.1.os, ...), custom_call_target="tpu_custom_call" | custom-call | tf_op jit(solution)/shard_map/rows/pallas_call | solution.py:177
  19.4 0.1 collective-permute-start.3
  19.5 1.4 %collective-permute-start.4 = (f32[64,512]{1,0:T(8,128)S(1)}, f32[64,512]{1,0:T(8,128)S(1)}, u32[]{:S(2)}, u32[]{:S(2)}) collective-permute-start(f32[64,512]{1,0:T(8,128)S(1)} %get-tuple-element.20), channel_id=1, source_target_pairs={{64,128},{128,64},{192,0},{0,192},{65,129},{129,65},{193,1},{1,193... | collective-permute-start | bytes 393224 | tf_op jit(solution)/shard_map/ppermute | solution.py:531
  20.9 3.2 %collective-permute-done.3.rows_one = f32[64,512]{1,0:T(8,128)S(1)} collective-permute-done((f32[64,512]{1,0:T(8,128)S(1)}, f32[64,512]{1,0:T(8,128)S(1)}, u32[]{:S(2)}, u32[]{:S(2)}) %collective-permute-start.3) | collective-permute-done | bytes 131104 | tf_op jit(solution)/shard_map/ppermute | solution.py:531
  24.2 1.3 %collective-permute-done.4.rows_two = f32[64,512]{1,0:T(8,128)S(1)} collective-permute-done((f32[64,512]{1,0:T(8,128)S(1)}, f32[64,512]{1,0:T(8,128)S(1)}, u32[]{:S(2)}, u32[]{:S(2)}) %collective-permute-start.4) | collective-permute-done | bytes 131104 | tf_op jit(solution)/shard_map/ppermute | solution.py:531
  25.5 1.7 %cols.1 = (f32[144,128]{1,0:T(8,128)S(1)}, f32[144,128]{1,0:T(8,128)S(1)}) custom-call(s32[7]{0:T(128)S(1)} %stack.47.flag, f32[3,128,512]{2,1,0:T(8,128)S(1)} %copy-done.1, f32[3,128,512]{2,1,0:T(8,128)S(1)} %collective-permute-done.om, f32[3,128,512]{2,1,0:T(8,128)S(1)} %copy-done, f32[3,128,512]{2,1,0:T(8,128)S(1)} %collective-permute-done.1.os, ...), custom_call_target="tpu_custom_call" | custom-call | tf_op jit(solution)/shard_map/cols/pallas_call | solution.py:177
  27.2 0.9 %collective-permute-start.5 = (f32[144,128]{1,0:T(8,128)S(1)}, f32[144,128]{1,0:T(8,128)S(1)}, u32[]{:S(2)}, u32[]{:S(2)}) collective-permute-start(f32[144,128]{1,0:T(8,128)S(1)} %get-tuple-element.21), channel_id=1, source_target_pairs={{0,2},{2,0},{4,6},{6,4},{8,10},{10,8},{12,14},{14,12},{16,18},{18,... | collective-permute-start | bytes 221192 | tf_op jit(solution)/shard_map/ppermute | solution.py:531
  28.0 6.9 %collective-permute-start.6 = (f32[144,128]{1,0:T(8,128)S(1)}, f32[144,128]{1,0:T(8,128)S(1)}, u32[]{:S(2)}, u32[]{:S(2)}) collective-permute-start(f32[144,128]{1,0:T(8,128)S(1)} %get-tuple-element.22), channel_id=1, source_target_pairs={{2,4},{4,2},{6,8},{8,6},{10,12},{12,10},{14,16},{16,14},{18,20},{2... | collective-permute-start | bytes 221192 | tf_op jit(solution)/shard_map/ppermute | solution.py:531
  34.9 5.5 %links.1 = (f32[6,4,160,128]{3,2,1,0:T(8,128)S(1)}, f32[6,4,160,128]{3,2,1,0:T(8,128)S(1)}, f32[5,4,160,128]{3,2,1,0:T(8,128)S(1)}, f32[6,4,160,128]{3,2,1,0:T(8...) custom-call(s32[7]{0:T(128)S(1)} %stack.47.flag, ...), custom_call_target="tpu_custom_call" | custom-call | flops 80000000 | bytes 12000000 | tf_op jit(solution)/shard_map/links/pallas_call | solution.py:276
  40.4 0.0 collective-permute-done.5.cols_one
  40.4 0.0 collective-permute-done.6.cols_two
  40.5 11.3 %basis.1 = (f32[3,128,512]{2,1,0:T(8,128)S(1)}, f32[3,128,512]{2,1,0:T(8,128)S(1)}, f32[3,128,512]{2,1,0:T(8,128)S(1)}, f32[3,128,512]{2,1,0:T(8,128)S(1)}, f32[...) custom-call(s32[7]{0:T(128)S(1)} %stack.47.flag, f32[144,128]{1,0:T(8,128)S(1)} %collective-permute-done.5.cols_one, ...), custom_call_target="tpu_custom_call" | custom-call | tf_op jit(solution)/shard_map/basis/pallas_call | solution.py:447
  51.8 20.5 %all_to_all.11 = f32[256,1,128]{2,1,0:T(1,128)S(1)} all-to-all(f32[256,1,128]{2,1,0:T(1,128)S(1)} %bitcast.16), channel_id=1, replica_groups=mesh['gx'=4,'gy_0'=4,'gy_1'=8,'layer'=2] {'gx','gy_0','gy_1','layer'}, dimensions={0} | all-to-all | bytes 262144 | tf_op jit(solution)/shard_map/all_to_all | solution.py:562
  72.2 2.2 %update.1 = (f32[3,128,512]{2,1,0:T(8,128)}, f32[3,128,512]{2,1,0:T(8,128)}) custom-call(s32[7]{0:T(128)S(1)} %stack.47.flag, f32[256,128]{1,0:T(8,128)S(1)} %bitcast.15, f32[3,128,512]{2,1,0:T(8,128)S(1)} %copy-done, f32[3,128,512]{2,1,0:T(8,128)S(1)} %get-tuple-element.31.inv, f32[3,128,512]{2,1,0:T(8,128)S(1)} %get-tuple-element.32.r0_ref, ...), custom_call_target="tpu_custom_call" | custom-call | tf_op jit(solution)/shard_map/update/pallas_call | solution.py:512
Async XLA Ops:
  0.6 16.7 %collective-permute-start = (f32[3,128,512]{2,1,0:T(8,128)}, f32[3,128,512]{2,1,0:T(8,128)S(1)}, u32[]{:S(2)}, u32[]{:S(2)}) collective-permute-start(f32[3,128,512]{2,1,0:T(8,128)} %m.5), channel_id=1, source_target_pairs={{0,1},{1,0},{2,3},{3,2},{4,5},{5,4},{6,7},{7,6},{8,9},{9,8},{10,11... | collective-permute-start | bytes 2359304 | tf_op jit(solution)/shard_map/ppermute | solution.py:535
  4.0 13.4 %collective-permute-start.1 = (f32[3,128,512]{2,1,0:T(8,128)}, f32[3,128,512]{2,1,0:T(8,128)S(1)}, u32[]{:S(2)}, u32[]{:S(2)}) collective-permute-start(f32[3,128,512]{2,1,0:T(8,128)} %start.1), channel_id=1, source_target_pairs={{0,1},{1,0},{2,3},{3,2},{4,5},{5,4},{6,7},{7,6},{8,9},{9,8},{10,11... | collective-permute-start | bytes 2359304 | tf_op jit(solution)/shard_map/ppermute | solution.py:535
  4.7 0.7 copy-start.4
  5.4 12.0 %copy-start = (f32[3,128,512]{2,1,0:T(8,128)S(1)}, f32[3,128,512]{2,1,0:T(8,128)}, u32[]{:S(2)}) copy-start(f32[3,128,512]{2,1,0:T(8,128)} %start.1) | copy-start | bytes 2359300
  5.4 12.0 %copy-start.1 = (f32[3,128,512]{2,1,0:T(8,128)S(1)}, f32[3,128,512]{2,1,0:T(8,128)}, u32[]{:S(2)}) copy-start(f32[3,128,512]{2,1,0:T(8,128)} %m.5) | copy-start | bytes 2359300
  5.4 12.0 %copy-start.2 = (f32[128,512]{1,0:T(8,128)S(1)}, f32[128,512]{1,0:T(8,128)}, u32[]{:S(2)}) copy-start(f32[128,512]{1,0:T(8,128)} %via.5) | copy-start | bytes 786436
  15.3 2.0 %collective-permute-start.2 = (f32[128,512]{1,0:T(8,128)}, f32[128,512]{1,0:T(8,128)}, u32[]{:S(2)}, u32[]{:S(2)}) collective-permute-start(f32[128,512]{1,0:T(8,128)} %scatter.1.mine), channel_id=1, source_target_pairs={{0,1},{1,0},{2,3},{3,2},{4,5},{5,4},{6,7},{7,6},{8,9},{9,8},{10,11... | collective-permute-start | bytes 786440 | tf_op jit(solution)/shard_map/ppermute | solution.py:535
  17.4 1.0 %copy-start.3 = (f32[128,512]{1,0:T(8,128)S(1)}, f32[128,512]{1,0:T(8,128)}, u32[]{:S(2)}) copy-start(f32[128,512]{1,0:T(8,128)} %pad.5) | copy-start | bytes 786436
  19.4 4.8 %collective-permute-start.3 = (f32[64,512]{1,0:T(8,128)S(1)}, f32[64,512]{1,0:T(8,128)S(1)}, u32[]{:S(2)}, u32[]{:S(2)}) collective-permute-start(f32[64,512]{1,0:T(8,128)S(1)} %get-tuple-element.19), channel_id=1, source_target_pairs={{0,64},{64,0},{128,192},{192,128},{1,65},{65,1},{129,193},{193,129... | collective-permute-start | bytes 393224 | tf_op jit(solution)/shard_map/ppermute | solution.py:531
  19.5 6.0 %collective-permute-start.4 = (f32[64,512]{1,0:T(8,128)S(1)}, f32[64,512]{1,0:T(8,128)S(1)}, u32[]{:S(2)}, u32[]{:S(2)}) collective-permute-start(f32[64,512]{1,0:T(8,128)S(1)} %get-tuple-element.20), channel_id=1, source_target_pairs={{64,128},{128,64},{192,0},{0,192},{65,129},{129,65},{193,1},{1,193... | collective-permute-start | bytes 393224 | tf_op jit(solution)/shard_map/ppermute | solution.py:531
  27.2 13.3 %collective-permute-start.5 = (f32[144,128]{1,0:T(8,128)S(1)}, f32[144,128]{1,0:T(8,128)S(1)}, u32[]{:S(2)}, u32[]{:S(2)}) collective-permute-start(f32[144,128]{1,0:T(8,128)S(1)} %get-tuple-element.21), channel_id=1, source_target_pairs={{0,2},{2,0},{4,6},{6,4},{8,10},{10,8},{12,14},{14,12},{16,18},{18,... | collective-permute-start | bytes 221192 | tf_op jit(solution)/shard_map/ppermute | solution.py:531
  28.0 12.4 %collective-permute-start.6 = (f32[144,128]{1,0:T(8,128)S(1)}, f32[144,128]{1,0:T(8,128)S(1)}, u32[]{:S(2)}, u32[]{:S(2)}) collective-permute-start(f32[144,128]{1,0:T(8,128)S(1)} %get-tuple-element.22), channel_id=1, source_target_pairs={{2,4},{4,2},{6,8},{8,6},{10,12},{12,10},{14,16},{16,14},{18,20},{2... | collective-permute-start | bytes 221192 | tf_op jit(solution)/shard_map/ppermute | solution.py:531

commit v4 on v3

--- a/solution.py
+++ b/solution.py
@@ -24,10 +24,16 @@
     return pltpu.CompilerParams(vmem_limit_bytes=mebibytes << 20)
 
 
-def scatter_kernel(count_ref, weight_ref, profile_hbm, cell_hbm, out_ref, profile_ref, cell_ref, total_ref, sems):
+def scatter_kernel(
+    count_ref, weight_hbm, profile_hbm, cell_hbm,
+    out_ref, weight_ref, profile_ref, cell_ref, total_ref, sems,
+):
     half = out_ref.shape[0]
     blocks = profile_ref.shape[0] // CHUNK
-    fetches = [pltpu.make_async_copy(cell_hbm, cell_ref, sems.at[blocks])]
+    fetches = [
+        pltpu.make_async_copy(cell_hbm, cell_ref, sems.at[blocks]),
+        pltpu.make_async_copy(weight_hbm, weight_ref, sems.at[blocks + 1]),
+    ]
     for block in range(blocks):
         span = pl.ds(block * CHUNK, CHUNK)
         fetches.append(
@@ -36,11 +42,12 @@
     for fetch in fetches:
         fetch.start()
     total_ref[...] = jnp.zeros_like(total_ref)
-    times = weight_ref.shape[0]
-    weight = jnp.broadcast_to(weight_ref[...].reshape(1, times), (16, times))
     ids = lax.broadcasted_iota(jnp.int32, (SIDE, CHUNK), 0).astype(jnp.float32).astype(jnp.bfloat16)
     zero, one = jnp.bfloat16(0), jnp.bfloat16(1)
     fetches[0].wait()
+    fetches[1].wait()
+    times = weight_ref.shape[0]
+    weight = jnp.broadcast_to(weight_ref[...].reshape(1, times), (16, times))
 
     def add_block(block, _):
         first = pl.multiple_of(block * CHUNK, CHUNK)
@@ -53,7 +60,7 @@
             preferred_element_type=jnp.float32,
         )[:1]
         position = first + lax.broadcasted_iota(jnp.int32, (1, CHUNK), 1)
-        amount = jnp.where(position < count_ref[0], amount, 0.0)
+        amount = jnp.where(position < count_ref[0, 0, 0], amount, 0.0)
         high = amount.astype(jnp.bfloat16)
         low = (amount - high.astype(jnp.float32)).astype(jnp.bfloat16)
         cell = cell_ref[:, span]
@@ -73,49 +80,65 @@
     out_ref[:, SIDE:] = both[half:]
 
 
+def in_hbm(value):
+    return pltpu.with_memory_space_constraint(value, pltpu.HBM)
+
+
 def scatter(profiles, time_weight, slot_cell, inst_count, tile):
     slots, times = profiles.shape[-2:]
     return pl.pallas_call(
         scatter_kernel,
         out_shape=jax.ShapeDtypeStruct(tile, jnp.float32),
-        in_specs=[SMEM, VMEM, HBM, HBM],
+        in_specs=[SMEM, HBM, HBM, HBM],
         out_specs=VMEM,
         scratch_shapes=[
+            pltpu.VMEM((times,), jnp.bfloat16),
             pltpu.VMEM((slots, times), jnp.bfloat16),
             pltpu.VMEM((1, slots), jnp.int32),
             pltpu.VMEM((2 * SIDE, SIDE), jnp.float32),
-            pltpu.SemaphoreType.DMA((slots // CHUNK + 1,)),
+            pltpu.SemaphoreType.DMA((slots // CHUNK + 2,)),
         ],
-        compiler_params=params(24),
+        compiler_params=params(20),
         cost_estimate=pl.CostEstimate(
             flops=6 * slots * SIDE * SIDE, bytes_accessed=2 * slots * times, transcendentals=0
         ),
         name="scatter",
     )(
-        inst_count.reshape(1),
-        time_weight,
-        pltpu.with_memory_space_constraint(profiles.reshape(slots, times), pltpu.HBM),
-        pltpu.with_memory_space_constraint(slot_cell.reshape(1, slots), pltpu.HBM),
+        inst_count,
+        in_hbm(time_weight),
+        in_hbm(profiles.reshape(slots, times)),
+        in_hbm(slot_cell.reshape(1, slots)),
     )
 
 
+PLANES = 15
+
+
+class Reader:
+    def __init__(self, read, shape):
+        self.read, self.shape = read, shape
+
+    def __call__(self, rows, cols):
+        return self.read(rows, cols)
+
+
 def plane_readers(metal, other_metal, start, other_start, via, pad, mine, theirs, flip):
-    readers = []
+    reads = []
     for own, other in ((metal, other_metal), (start, other_start)):
         for ref in (own, other):
             for k in range(3):
                 index = jnp.where(flip == 1, 2 - k, k)
-                readers.append(lambda rows, cols, ref=ref, index=index: ref[index, rows, cols])
-    readers.append(lambda rows, cols: via[rows, cols])
-    readers.append(lambda rows, cols: pad[rows, cols])
-    readers.append(lambda rows, cols: mine[rows, cols] + theirs[rows, cols])
-    return readers
-
-
-def rows_kernel(flag, m, om, s, os, via, pad, mine, theirs, one_ref, two_ref):
-    rows = m.shape[1]
-    readers = plane_readers(m, om, s, os, via, pad, mine, theirs, flag[0])
-    low = lax.broadcasted_iota(jnp.int32, (8, m.shape[2]), 0) < HALO
+                reads.append(lambda rows, cols, ref=ref, index=index: ref[index, rows, cols])
+    if via is not None:
+        reads.append(lambda rows, cols: via[rows, cols])
+        reads.append(lambda rows, cols: pad[rows, cols])
+        reads.append(lambda rows, cols: mine[rows, cols] + theirs[rows, cols])
+    return [Reader(read, metal.shape[1:]) for read in reads]
+
+
+def row_strips(readers, first_plane, flag, one_ref, two_ref):
+    rows, cols = readers[0].shape
+    low = lax.broadcasted_iota(jnp.int32, (8, cols), 0) < HALO
     for pair in range(0, len(readers), 2):
         packed = []
         for start in (0, rows - 8):
@@ -126,9 +149,35 @@
                 there = pltpu.roll(readers[pair + 1](span, slice(None)), HALO, 0)
             packed.append(jnp.where(low, here, there) if start == 0 else jnp.where(low, there, here))
         first, last = packed
-        span = slice(pair * HALO, pair * HALO + 8)
-        one_ref[span, :] = jnp.where(flag[5] == 1, first, last)
-        two_ref[span, :] = jnp.where(flag[5] == 1, last, first)
+        start = (first_plane + pair) * HALO
+        one_ref[start : start + 8, :] = jnp.where(flag[5] == 1, first, last)
+        two_ref[start : start + 8, :] = jnp.where(flag[5] == 1, last, first)
+
+
+def rows_kernel(flag, via_hbm, pad_hbm, m, om, s, os, one_ref, two_ref, edge_ref, sems):
+    rows = m.shape[1]
+    fetches = []
+    for plane, ref in enumerate((via_hbm, pad_hbm)):
+        for side, start in enumerate((0, rows - 8)):
+            place = edge_ref.at[plane, pl.ds(8 * side, 8)]
+            copy = pltpu.make_async_copy(ref.at[pl.ds(start, 8)], place, sems.at[2 * plane + side])
+            copy.start()
+            fetches.append(copy)
+
+    def edge(plane):
+        return lambda rows, cols: edge_ref[plane, (slice(0, 8) if rows.start == 0 else slice(8, 16)), cols]
+
+    readers = plane_readers(m, om, s, os, None, None, None, None, flag[0])
+    row_strips(readers, 0, flag, one_ref, two_ref)
+    for fetch in fetches:
+        fetch.wait()
+    readers = [Reader(edge(plane), m.shape[1:]) for plane in range(2)]
+    row_strips(readers, PLANES - 3, flag, one_ref, two_ref)
+
+
+def fed_kernel(flag, mine, theirs, one_in, two_in, one_ref, two_ref):
+    reader = Reader(lambda rows, cols: mine[rows, cols] + theirs[rows, cols], mine.shape)
+    row_strips([reader], PLANES - 1, flag, one_ref, two_ref)
 
 
 def row_halos(one, two, plane, cols, flag):
@@ -141,27 +190,44 @@
     return above, below
 
 
-def cols_kernel(flag, m, om, s, os, via, pad, mine, theirs, rows_one, rows_two, one_ref, two_ref):
-    rows, cols = m.shape[1], m.shape[2]
-    readers = plane_readers(m, om, s, os, via, pad, mine, theirs, flag[0])
-    lane = lax.broadcasted_iota(jnp.int32, (rows + 16, LANES), 1)
+def col_strips(values_of, height, cols, flag):
+    lane = lax.broadcasted_iota(jnp.int32, (height, LANES), 1)
     sides = []
     for start in (0, cols - LANES):
         span = slice(start, start + LANES)
-        packed = jnp.zeros((rows + 16, LANES), jnp.float32)
-        for plane, read in enumerate(readers):
-            above, below = row_halos(rows_one, rows_two, plane, span, flag)
-            values = jnp.concatenate([above, read(slice(None), span), below], axis=0)
+        packed = jnp.zeros((height, LANES), jnp.float32)
+        for plane in range(PLANES):
+            values = values_of(plane, span)
             where = HALO * plane if start == 0 else (LANES - HALO + HALO * plane) % LANES
             turned = pltpu.roll(values, HALO * plane, 1) if plane else values
             packed = jnp.where((lane >= where) & (lane < where + HALO), turned, packed)
         sides.append(packed)
     first, last = sides
-    one_ref[...] = jnp.where(flag[6] == 1, first, last)
-    two_ref[...] = jnp.where(flag[6] == 1, last, first)
-
-
-def col_halo(one, two, plane, flag):
+    return jnp.where(flag[6] == 1, first, last), jnp.where(flag[6] == 1, last, first)
+
+
+def cols_kernel(flag, m, om, s, os, via, pad, mine, theirs, one_ref, two_ref):
+    rows, cols = via.shape
+    readers = plane_readers(m, om, s, os, via, pad, mine, theirs, flag[0])
+    inner = slice(8, 8 + rows)
+    one_ref[inner, :], two_ref[inner, :] = col_strips(
+        lambda plane, span: readers[plane](slice(None), span), rows, cols, flag
+    )
+
+
+def corners_kernel(flag, rows_one, rows_two, one_in, two_in, one_ref, two_ref):
+    height, cols = one_ref.shape[0], rows_one.shape[1]
+
+    def halos(plane, span):
+        return jnp.concatenate(row_halos(rows_one, rows_two, plane, span, flag), axis=0)
+
+    one, two = col_strips(halos, 16, cols, flag)
+    for ref, values in ((one_ref, one), (two_ref, two)):
+        ref[:8, :] = values[:8]
+        ref[height - 8 :, :] = values[8:]
+
+
+def col_halo_of(one, two, plane, flag):
     after = jnp.where(flag[6] == 1, two[...], one[...])
     before = jnp.where(flag[6] == 1, one[...], two[...])
     lane = lax.broadcasted_iota(jnp.int32, after.shape, 1)
@@ -173,13 +239,17 @@
     return pltpu.roll(values, (LANES - where) % LANES, 1) if plane else values
 
 
-def strip_call(kernel, shape, name, *operands):
+def strip_call(kernel, shape, name, *operands, in_place=False, far=0, scratch=()):
+    last = len(operands) - 1
     return pl.pallas_call(
         kernel,
         out_shape=(jax.ShapeDtypeStruct(shape, jnp.float32),) * 2,
-        in_specs=[SMEM] + [VMEM] * (len(operands) - 1),
+        in_specs=[SMEM] + [HBM] * far + [VMEM] * (last - far),
         out_specs=(VMEM, VMEM),
-        compiler_params=params(24),
+        scratch_shapes=scratch,
+        input_output_aliases={last - 1: 0, last: 1} if in_place else {},
+        compiler_params=params(8),
+        cost_estimate=pl.CostEstimate(flops=2_000_000, bytes_accessed=1_000_000, transcendentals=0),
         name=name,
     )(*operands)
 
@@ -295,7 +365,7 @@
     inner = slice(OWN - 8, OWN + rows + 8)
     for plane in range(15):
         ref = (metal_ref, start_ref, column_ref)[plane // 6]
-        ref[plane % 6, inner, :] = col_halo(cols_one, cols_two, plane, flag)
+        ref[plane % 6, inner, :] = col_halo_of(cols_one, cols_two, plane, flag)
 
     weight = jnp.where(flag[0] == 1, 1.0, 0.0)
     lane = lax.broadcasted_iota(jnp.int32, (8, LANES), 1)
@@ -554,11 +624,21 @@
     mine = scatter(profiles, time_weight, slot_cell, inst_count, (rows, cols))
     theirs = swap(mine)
     planes = (flag, metal, other_metal, start_drop, other_start, via_density, pad, mine, theirs)
-    row_strips = trade(*strip_call(rows_kernel, (64, cols), "rows", *planes), "gx")
-    col_strips = trade(*strip_call(cols_kernel, (rows + 16, LANES), "cols", *planes, *row_strips), GY)
-    prepared = links(*planes, *row_strips)
+    edges = [pltpu.VMEM((2, 16, cols), jnp.float32), pltpu.SemaphoreType.DMA((4,))]
+    columns = [in_hbm(via_density), in_hbm(pad)]
+    strips = strip_call(
+        rows_kernel, (64, cols), "rows", flag, *columns, *planes[1:5], far=2, scratch=edges
+    )
+    strips = strip_call(fed_kernel, (64, cols), "fed", flag, mine, theirs, *strips, in_place=True)
+    row_halo = trade(*strips, "gx")
+    strips = strip_call(cols_kernel, (rows + 16, LANES), "cols", *planes)
+    strips = strip_call(
+        corners_kernel, (rows + 16, LANES), "corners", flag, *row_halo, *strips, in_place=True
+    )
+    col_halo = trade(*strips, GY)
+    prepared = links(*planes, *row_halo)
     devices = lax.axis_size(ALL)
-    inv, r0, s1, s2, s3, moments = basis(devices, metal.shape, flag, *col_strips, *prepared)
+    inv, r0, s1, s2, s3, moments = basis(devices, metal.shape, flag, *col_halo, *prepared)
     sums = lax.all_to_all(moments, ALL, 0, 0, tiled=True)
     return update(flag, sums, start_drop, inv, r0, s1, s2, s3)
 

time: 74.7 us -> 71.2 us (0.953)
  waiting for transfers between devices: 5.99 us -> 3.28 us
  local copies, waits for them, and re-layouts: 1.69 us -> 0.1 us
  Pallas kernels: 31.7 us -> 32.8 us
    pallas_call x2 -> x4, Pallas kernels: 2.72 us -> 4.5 us  [strip_call(): pl.pallas_call(kernel, out_shape=(jax.ShapeDtypeStruct(shape, jnp.float32...]
    unnamed x10 -> x8, local copies, waits for them, and re-layouts: 1.6 us -> 0.02 us
    ppermute x3, waiting for transfers between devices: 1.42 us -> 0.01 us  [swap(): return lax.ppermute(value, 'layer', [(0, 1), (1, 0)])]
    ppermute x4, waiting for transfers between devices: 4.56 us -> 3.27 us  [trade(): return (lax.ppermute(one, axes, pairs), lax.ppermute(two, axes, shifted))]
  transfers between devices with their start and end apart: 7 -> 7, of which waited for: 3 -> 2; matrix products, arithmetic and copies ran while one was open for 0% -> 0% of each run, Pallas kernels for 21% -> 25%
where the time goes in v4:
time: 71.2 us; the launch traced here: 71 us
  Pallas kernels  32.8 us (46%)
  blocking collectives  20.2 us (28%)
  starting transfers between devices  13.2 us (19%)
  waiting for transfers between devices  3.28 us (5%)
  between operations  1.42 us (2%)
    all_to_all x1, blocking collectives, per_device(): sums = lax.all_to_all(moments, ALL, 0, 0, tiled=True)  20.2 us
    pallas_call x1, Pallas kernels, basis(): pl.pallas_call(basis_kernel, out_shape=(jax.ShapeDtypeStruct(own, jnp.flo...  11.3 us
    ppermute x4, starting transfers between devices, trade(): return (lax.ppermute(one, axes, pairs), lax.ppermute(two, axes, shifted))  9.27 us
    pallas_call x1, Pallas kernels, scatter(): pl.pallas_call(scatter_kernel, out_shape=jax.ShapeDtypeStruct(tile, jnp.f...  9.26 us
    pallas_call x1, Pallas kernels, links(): pl.pallas_call(links_kernel, out_shape=[jax.ShapeDtypeStruct(c + (height,...  5.45 us
    pallas_call x4, Pallas kernels, strip_call(): pl.pallas_call(kernel, out_shape=(jax.ShapeDtypeStruct(shape, jnp.float32...  4.5 us
    ppermute x3, starting transfers between devices, swap(): return lax.ppermute(value, 'layer', [(0, 1), (1, 0)])  3.93 us
    ppermute x4, waiting for transfers between devices, trade(): return (lax.ppermute(one, axes, pairs), lax.ppermute(two, axes, shifted))  3.27 us
  transfers between devices with their start and end apart: 7, of which 2 were waited for; matrix products, arithmetic and copies ran while one was open for 0% of the time, Pallas kernels for 25%

profile of v4, /device:TPU:1, one launch (start us, length us, event | category | flops | bytes accessed | tf_op | source)
XLA Modules:
  0.0 71.0 jit_solution(9329350265335332784)
XLA Ops:
  0.6 3.3 %collective-permute-start.1 = (f32[3,128,512]{2,1,0:T(8,128)}, f32[3,128,512]{2,1,0:T(8,128)S(1)}, u32[]{:S(2)}, u32[]{:S(2)}) collective-permute-start(f32[3,128,512]{2,1,0:T(8,128)} %m.5), channel_id=1, source_target_pairs={{0,1},{1,0},{2,3},{3,2},{4,5},{5,4},{6,7},{7,6},{8,9},{9,8},{10,11... | collective-permute-start | bytes 2359304 | tf_op jit(solution)/shard_map/ppermute | solution.py:605
  4.0 0.1 collective-permute-start.2
  4.7 0.0 copy-start
  4.7 0.0 copy-start.1
  4.7 9.3 %scatter.1.mine = f32[128,512]{1,0:T(8,128)S(1)} custom-call(s32[1,1,1]{2,1,0:T(1,128)S(6)} %copy.19.count_ref, bf16[256]{0:T(256)(128)(2,1)} %weight_hbm.1, bf16[16384,256]{1,0:T(8,128)(2,1)} %bitcast.15, s32[1,16384]{1,0:T(1,128)} %bitcast.16), custom_call_target="tpu_custom_call" | custom-call | flops 6442450944 | bytes 8388608 | tf_op jit(solution)/shard_map/scatter/pallas_call | solution.py:89
  14.0 0.5 collective-permute-start
  14.5 0.1 stack.47.flag
  14.6 0.0 copy-start.2
  14.6 0.0 copy-start.3
  14.6 0.0 collective-permute-done.1.om
  14.6 0.0 collective-permute-done.2.os
  14.6 0.0 copy-done
  14.6 0.0 copy-done.1
  14.6 1.4 %rows.1 = (f32[64,512]{1,0:T(8,128)S(1)}, f32[64,512]{1,0:T(8,128)S(1)}) custom-call(s32[7]{0:T(128)S(1)} %stack.47.flag, f32[128,512]{1,0:T(8,128)} %via.3, f32[128,512]{1,0:T(8,128)} %pad.3, f32[3,128,512]{2,1,0:T(8,128)S(1)} %copy-done.1, f32[3,128,512]{2,1,0:T(8,128)S(1)} %collective-permute-done.1.om, f32[3,128,512]{2,1,0:T(8,128)S(1)} %copy-done, ...), custom_call_target="tpu_custom_call" | custom-call | flops 2000000 | bytes 1000000 | tf_op jit(solution)/shard_map/rows/pallas_call | solution.py:244
  16.0 0.0 collective-permute-done.theirs
  16.0 1.0 %fed.1 = (f32[64,512]{1,0:T(8,128)S(1)}, f32[64,512]{1,0:T(8,128)S(1)}) custom-call(s32[7]{0:T(128)S(1)} %stack.47.flag, f32[128,512]{1,0:T(8,128)S(1)} %scatter.1.mine, f32[128,512]{1,0:T(8,128)} %collective-permute-done.theirs, f32[64,512]{1,0:T(8,128)S(1)} %get-tuple-element.23.one_in, ...), custom_call_target="tpu_custom_call", output_to_operand_aliasing={{0}: (3, {}), {1}: (4, {})} | custom-call | flops 2000000 | bytes 1000000 | tf_op jit(solution)/shard_map/fed/pallas_call | solution.py:244
  17.0 0.1 collective-permute-start.3
  17.1 1.4 %collective-permute-start.4 = (f32[64,512]{1,0:T(8,128)S(1)}, f32[64,512]{1,0:T(8,128)S(1)}, u32[]{:S(2)}, u32[]{:S(2)}) collective-permute-start(f32[64,512]{1,0:T(8,128)S(1)} %get-tuple-element.26), channel_id=1, source_target_pairs={{64,128},{128,64},{192,0},{0,192},{65,129},{129,65},{193,1},{1,193... | collective-permute-start | bytes 393224 | tf_op jit(solution)/shard_map/ppermute | solution.py:601
  18.5 0.0 copy-done.2
  18.5 0.0 copy-done.3
  18.5 1.5 %cols.1 = (f32[144,128]{1,0:T(8,128)S(1)}, f32[144,128]{1,0:T(8,128)S(1)}) custom-call(s32[7]{0:T(128)S(1)} %stack.47.flag, f32[3,128,512]{2,1,0:T(8,128)S(1)} %copy-done.1, f32[3,128,512]{2,1,0:T(8,128)S(1)} %collective-permute-done.1.om, f32[3,128,512]{2,1,0:T(8,128)S(1)} %copy-done, f32[3,128,512]{2,1,0:T(8,128)S(1)} %collective-permute-done.2.os, ...), custom_call_target="tpu_custom_call" | custom-call | flops 2000000 | bytes 1000000 | tf_op jit(solution)/shard_map/cols/pallas_call | solution.py:244
  20.0 2.0 %collective-permute-done.3.rows_one = f32[64,512]{1,0:T(8,128)S(1)} collective-permute-done((f32[64,512]{1,0:T(8,128)S(1)}, f32[64,512]{1,0:T(8,128)S(1)}, u32[]{:S(2)}, u32[]{:S(2)}) %collective-permute-start.3) | collective-permute-done | bytes 131104 | tf_op jit(solution)/shard_map/ppermute | solution.py:601
  22.0 1.3 %collective-permute-done.4.rows_two = f32[64,512]{1,0:T(8,128)S(1)} collective-permute-done((f32[64,512]{1,0:T(8,128)S(1)}, f32[64,512]{1,0:T(8,128)S(1)}, u32[]{:S(2)}, u32[]{:S(2)}) %collective-permute-start.4) | collective-permute-done | bytes 131104 | tf_op jit(solution)/shard_map/ppermute | solution.py:601
  23.3 0.7 corners.1
  24.0 0.9 %collective-permute-start.5 = (f32[144,128]{1,0:T(8,128)S(1)}, f32[144,128]{1,0:T(8,128)S(1)}, u32[]{:S(2)}, u32[]{:S(2)}) collective-permute-start(f32[144,128]{1,0:T(8,128)S(1)} %get-tuple-element.29), channel_id=1, source_target_pairs={{0,2},{2,0},{4,6},{6,4},{8,10},{10,8},{12,14},{14,12},{16,18},{18,... | collective-permute-start | bytes 221192 | tf_op jit(solution)/shard_map/ppermute | solution.py:601
  24.9 6.9 %collective-permute-start.6 = (f32[144,128]{1,0:T(8,128)S(1)}, f32[144,128]{1,0:T(8,128)S(1)}, u32[]{:S(2)}, u32[]{:S(2)}) collective-permute-start(f32[144,128]{1,0:T(8,128)S(1)} %get-tuple-element.30), channel_id=1, source_target_pairs={{2,4},{4,2},{6,8},{8,6},{10,12},{12,10},{14,16},{16,14},{18,20},{2... | collective-permute-start | bytes 221192 | tf_op jit(solution)/shard_map/ppermute | solution.py:601
  31.7 5.5 %links.1 = (f32[6,4,160,128]{3,2,1,0:T(8,128)S(1)}, f32[6,4,160,128]{3,2,1,0:T(8,128)S(1)}, f32[5,4,160,128]{3,2,1,0:T(8,128)S(1)}, f32[6,4,160,128]{3,2,1,0:T(8...) custom-call(s32[7]{0:T(128)S(1)} %stack.47.flag, ...), custom_call_target="tpu_custom_call" | custom-call | flops 80000000 | bytes 12000000 | tf_op jit(solution)/shard_map/links/pallas_call | solution.py:346
  37.2 0.0 collective-permute-done.5.cols_one
  37.2 0.0 collective-permute-done.6.cols_two
  37.2 11.3 %basis.1 = (f32[3,128,512]{2,1,0:T(8,128)S(1)}, f32[3,128,512]{2,1,0:T(8,128)S(1)}, f32[3,128,512]{2,1,0:T(8,128)S(1)}, f32[3,128,512]{2,1,0:T(8,128)S(1)}, f32[...) custom-call(s32[7]{0:T(128)S(1)} %stack.47.flag, f32[144,128]{1,0:T(8,128)S(1)} %collective-permute-done.5.cols_one, ...), custom_call_target="tpu_custom_call" | custom-call | tf_op jit(solution)/shard_map/basis/pallas_call | solution.py:517
  48.5 20.2 %all_to_all.11 = f32[256,1,128]{2,1,0:T(1,128)S(1)} all-to-all(f32[256,1,128]{2,1,0:T(1,128)S(1)} %bitcast.14), channel_id=1, replica_groups=mesh['gx'=4,'gy_0'=4,'gy_1'=8,'layer'=2] {'gx','gy_0','gy_1','layer'}, dimensions={0} | all-to-all | bytes 262144 | tf_op jit(solution)/shard_map/all_to_all | solution.py:642
  68.8 2.2 %update.1 = (f32[3,128,512]{2,1,0:T(8,128)}, f32[3,128,512]{2,1,0:T(8,128)}) custom-call(s32[7]{0:T(128)S(1)} %stack.47.flag, f32[256,128]{1,0:T(8,128)S(1)} %bitcast.13, f32[3,128,512]{2,1,0:T(8,128)S(1)} %copy-done, f32[3,128,512]{2,1,0:T(8,128)S(1)} %get-tuple-element.39.inv, f32[3,128,512]{2,1,0:T(8,128)S(1)} %get-tuple-element.40.r0_ref, ...), custom_call_target="tpu_custom_call" | custom-call | tf_op jit(solution)/shard_map/update/pallas_call | solution.py:582
Async XLA Ops:
  0.6 14.0 %collective-permute-start.1 = (f32[3,128,512]{2,1,0:T(8,128)}, f32[3,128,512]{2,1,0:T(8,128)S(1)}, u32[]{:S(2)}, u32[]{:S(2)}) collective-permute-start(f32[3,128,512]{2,1,0:T(8,128)} %m.5), channel_id=1, source_target_pairs={{0,1},{1,0},{2,3},{3,2},{4,5},{5,4},{6,7},{7,6},{8,9},{9,8},{10,11... | collective-permute-start | bytes 2359304 | tf_op jit(solution)/shard_map/ppermute | solution.py:605
  4.0 10.6 %collective-permute-start.2 = (f32[3,128,512]{2,1,0:T(8,128)}, f32[3,128,512]{2,1,0:T(8,128)S(1)}, u32[]{:S(2)}, u32[]{:S(2)}) collective-permute-start(f32[3,128,512]{2,1,0:T(8,128)} %start.1), channel_id=1, source_target_pairs={{0,1},{1,0},{2,3},{3,2},{4,5},{5,4},{6,7},{7,6},{8,9},{9,8},{10,11... | collective-permute-start | bytes 2359304 | tf_op jit(solution)/shard_map/ppermute | solution.py:605
  4.7 9.9 %copy-start = (f32[3,128,512]{2,1,0:T(8,128)S(1)}, f32[3,128,512]{2,1,0:T(8,128)}, u32[]{:S(2)}) copy-start(f32[3,128,512]{2,1,0:T(8,128)} %start.1) | copy-start | bytes 2359300
  4.7 9.9 %copy-start.1 = (f32[3,128,512]{2,1,0:T(8,128)S(1)}, f32[3,128,512]{2,1,0:T(8,128)}, u32[]{:S(2)}) copy-start(f32[3,128,512]{2,1,0:T(8,128)} %m.5) | copy-start | bytes 2359300
  14.0 2.0 %collective-permute-start = (f32[128,512]{1,0:T(8,128)S(1)}, f32[128,512]{1,0:T(8,128)}, u32[]{:S(2)}, u32[]{:S(2)}) collective-permute-start(f32[128,512]{1,0:T(8,128)S(1)} %scatter.1.mine), channel_id=1, source_target_pairs={{0,1},{1,0},{2,3},{3,2},{4,5},{5,4},{6,7},{7,6},{8,9},{9,8},{10,11... | collective-permute-start | bytes 786440 | tf_op jit(solution)/shard_map/ppermute | solution.py:605
  14.6 3.9 %copy-start.2 = (f32[128,512]{1,0:T(8,128)S(1)}, f32[128,512]{1,0:T(8,128)}, u32[]{:S(2)}) copy-start(f32[128,512]{1,0:T(8,128)} %via.3) | copy-start | bytes 786436
  14.6 3.9 %copy-start.3 = (f32[128,512]{1,0:T(8,128)S(1)}, f32[128,512]{1,0:T(8,128)}, u32[]{:S(2)}) copy-start(f32[128,512]{1,0:T(8,128)} %pad.3) | copy-start | bytes 786436
  17.0 5.0 %collective-permute-start.3 = (f32[64,512]{1,0:T(8,128)S(1)}, f32[64,512]{1,0:T(8,128)S(1)}, u32[]{:S(2)}, u32[]{:S(2)}) collective-permute-start(f32[64,512]{1,0:T(8,128)S(1)} %get-tuple-element.25), channel_id=1, source_target_pairs={{0,64},{64,0},{128,192},{192,128},{1,65},{65,1},{129,193},{193,129... | collective-permute-start | bytes 393224 | tf_op jit(solution)/shard_map/ppermute | solution.py:601
  17.1 6.2 %collective-permute-start.4 = (f32[64,512]{1,0:T(8,128)S(1)}, f32[64,512]{1,0:T(8,128)S(1)}, u32[]{:S(2)}, u32[]{:S(2)}) collective-permute-start(f32[64,512]{1,0:T(8,128)S(1)} %get-tuple-element.26), channel_id=1, source_target_pairs={{64,128},{128,64},{192,0},{0,192},{65,129},{129,65},{193,1},{1,193... | collective-permute-start | bytes 393224 | tf_op jit(solution)/shard_map/ppermute | solution.py:601
  24.0 13.2 %collective-permute-start.5 = (f32[144,128]{1,0:T(8,128)S(1)}, f32[144,128]{1,0:T(8,128)S(1)}, u32[]{:S(2)}, u32[]{:S(2)}) collective-permute-start(f32[144,128]{1,0:T(8,128)S(1)} %get-tuple-element.29), channel_id=1, source_target_pairs={{0,2},{2,0},{4,6},{6,4},{8,10},{10,8},{12,14},{14,12},{16,18},{18,... | collective-permute-start | bytes 221192 | tf_op jit(solution)/shard_map/ppermute | solution.py:601
  24.9 12.3 %collective-permute-start.6 = (f32[144,128]{1,0:T(8,128)S(1)}, f32[144,128]{1,0:T(8,128)S(1)}, u32[]{:S(2)}, u32[]{:S(2)}) collective-permute-start(f32[144,128]{1,0:T(8,128)S(1)} %get-tuple-element.30), channel_id=1, source_target_pairs={{2,4},{4,2},{6,8},{8,6},{10,12},{12,10},{14,16},{16,14},{18,20},{2... | collective-permute-start | bytes 221192 | tf_op jit(solution)/shard_map/ppermute | solution.py:601

commit v5 on v4

--- a/solution.py
+++ b/solution.py
@@ -177,6 +177,9 @@
 
 def fed_kernel(flag, mine, theirs, one_in, two_in, one_ref, two_ref):
     reader = Reader(lambda rows, cols: mine[rows, cols] + theirs[rows, cols], mine.shape)
+    done = (PLANES - 1) * HALO
+    one_ref[:done, :] = one_in[:done, :]
+    two_ref[:done, :] = two_in[:done, :]
     row_strips([reader], PLANES - 1, flag, one_ref, two_ref)
 
 
@@ -222,8 +225,9 @@
         return jnp.concatenate(row_halos(rows_one, rows_two, plane, span, flag), axis=0)
 
     one, two = col_strips(halos, 16, cols, flag)
-    for ref, values in ((one_ref, one), (two_ref, two)):
+    for ref, inner, values in ((one_ref, one_in, one), (two_ref, two_in, two)):
         ref[:8, :] = values[:8]
+        ref[8 : height - 8, :] = inner[8 : height - 8, :]
         ref[height - 8 :, :] = values[8:]
 
 
@@ -239,7 +243,7 @@
     return pltpu.roll(values, (LANES - where) % LANES, 1) if plane else values
 
 
-def strip_call(kernel, shape, name, *operands, in_place=False, far=0, scratch=()):
+def strip_call(kernel, shape, name, *operands, far=0, scratch=()):
     last = len(operands) - 1
     return pl.pallas_call(
         kernel,
@@ -247,8 +251,7 @@
         in_specs=[SMEM] + [HBM] * far + [VMEM] * (last - far),
         out_specs=(VMEM, VMEM),
         scratch_shapes=scratch,
-        input_output_aliases={last - 1: 0, last: 1} if in_place else {},
-        compiler_params=params(8),
+        compiler_params=params(12),
         cost_estimate=pl.CostEstimate(flops=2_000_000, bytes_accessed=1_000_000, transcendentals=0),
         name=name,
     )(*operands)
@@ -349,7 +352,7 @@
         in_specs=[SMEM] + [VMEM] * (len(operands) - 1),
         out_specs=[VMEM] * len(counts),
         scratch_shapes=[pltpu.VMEM((count, 4, height, LANES), jnp.float32) for count in (6, 6, 3)],
-        compiler_params=params(24),
+        compiler_params=params(28),
         cost_estimate=pl.CostEstimate(flops=80_000_000, bytes_accessed=12_000_000, transcendentals=2_000_000),
         name="links",
     )(*operands)
@@ -522,7 +525,7 @@
         out_specs=(VMEM,) * 6,
         scratch_shapes=[pltpu.VMEM((count, height, LANES), jnp.float32) for count in sides]
         + [pltpu.VMEM((count, 5, height, LANES), jnp.float32) for count in planes],
-        compiler_params=params(20),
+        compiler_params=params(36),
         name="basis",
     )(*operands)
 
@@ -629,11 +632,11 @@
     strips = strip_call(
         rows_kernel, (64, cols), "rows", flag, *columns, *planes[1:5], far=2, scratch=edges
     )
-    strips = strip_call(fed_kernel, (64, cols), "fed", flag, mine, theirs, *strips, in_place=True)
+    strips = strip_call(fed_kernel, (64, cols), "fed", flag, mine, theirs, *strips)
     row_halo = trade(*strips, "gx")
     strips = strip_call(cols_kernel, (rows + 16, LANES), "cols", *planes)
     strips = strip_call(
-        corners_kernel, (rows + 16, LANES), "corners", flag, *row_halo, *strips, in_place=True
+        corners_kernel, (rows + 16, LANES), "corners", flag, *row_halo, *strips
     )
     col_halo = trade(*strips, GY)
     prepared = links(*planes, *row_halo)

time: 71.2 us -> 71.2 us (level)
  no operation moved by 1% of the time
where the time goes in v5:
time: 71.2 us; the launch traced here: 71 us
  Pallas kernels  32.8 us (46%)
  blocking collectives  20.2 us (28%)
  starting transfers between devices  13.2 us (19%)
  waiting for transfers between devices  3.28 us (5%)
  between operations  1.42 us (2%)
    all_to_all x1, blocking collectives, per_device(): sums = lax.all_to_all(moments, ALL, 0, 0, tiled=True)  20.2 us
    pallas_call x1, Pallas kernels, basis(): pl.pallas_call(basis_kernel, out_shape=(jax.ShapeDtypeStruct(own, jnp.flo...  11.3 us
    ppermute x4, starting transfers between devices, trade(): return (lax.ppermute(one, axes, pairs), lax.ppermute(two, axes, shifted))  9.27 us
    pallas_call x1, Pallas kernels, scatter(): pl.pallas_call(scatter_kernel, out_shape=jax.ShapeDtypeStruct(tile, jnp.f...  9.26 us
    pallas_call x1, Pallas kernels, links(): pl.pallas_call(links_kernel, out_shape=[jax.ShapeDtypeStruct(c + (height,...  5.45 us
    pallas_call x4, Pallas kernels, strip_call(): pl.pallas_call(kernel, out_shape=(jax.ShapeDtypeStruct(shape, jnp.float32...  4.51 us
    ppermute x3, starting transfers between devices, swap(): return lax.ppermute(value, 'layer', [(0, 1), (1, 0)])  3.93 us
    ppermute x4, waiting for transfers between devices, trade(): return (lax.ppermute(one, axes, pairs), lax.ppermute(two, axes, shifted))  3.27 us
  transfers between devices with their start and end apart: 7, of which 2 were waited for; matrix products, arithmetic and copies ran while one was open for 0% of the time, Pallas kernels for 25%

profile of v5, /device:TPU:1, one launch (start us, length us, event | category | flops | bytes accessed | tf_op | source)
XLA Modules:
  0.0 71.0 jit_solution(11802286740060804595)
XLA Ops:
  0.6 3.3 %collective-permute-start.1 = (f32[3,128,512]{2,1,0:T(8,128)}, f32[3,128,512]{2,1,0:T(8,128)S(1)}, u32[]{:S(2)}, u32[]{:S(2)}) collective-permute-start(f32[3,128,512]{2,1,0:T(8,128)} %m.5), channel_id=1, source_target_pairs={{0,1},{1,0},{2,3},{3,2},{4,5},{5,4},{6,7},{7,6},{8,9},{9,8},{10,11... | collective-permute-start | bytes 2359304 | tf_op jit(solution)/shard_map/ppermute | solution.py:608
  4.0 0.1 collective-permute-start.2
  4.7 0.0 copy-start
  4.7 0.0 copy-start.1
  4.7 9.3 %scatter.1.mine = f32[128,512]{1,0:T(8,128)S(1)} custom-call(s32[1,1,1]{2,1,0:T(1,128)S(6)} %copy.11.count_ref, bf16[256]{0:T(256)(128)(2,1)} %weight_hbm.1, bf16[16384,256]{1,0:T(8,128)(2,1)} %bitcast.15, s32[1,16384]{1,0:T(1,128)} %bitcast.16), custom_call_target="tpu_custom_call" | custom-call | flops 6442450944 | bytes 8388608 | tf_op jit(solution)/shard_map/scatter/pallas_call | solution.py:89
  14.0 0.5 collective-permute-start
  14.5 0.1 stack.47.flag
  14.6 0.0 copy-start.2
  14.6 0.0 copy-start.3
  14.6 0.0 collective-permute-done.1.om
  14.6 0.0 collective-permute-done.2.os
  14.6 0.0 copy-done
  14.6 0.0 copy-done.1
  14.6 1.4 %rows.1 = (f32[64,512]{1,0:T(8,128)S(1)}, f32[64,512]{1,0:T(8,128)S(1)}) custom-call(s32[7]{0:T(128)S(1)} %stack.47.flag, f32[128,512]{1,0:T(8,128)} %via.3, f32[128,512]{1,0:T(8,128)} %pad.3, f32[3,128,512]{2,1,0:T(8,128)S(1)} %copy-done.1, f32[3,128,512]{2,1,0:T(8,128)S(1)} %collective-permute-done.1.om, f32[3,128,512]{2,1,0:T(8,128)S(1)} %copy-done, ...), custom_call_target="tpu_custom_call" | custom-call | flops 2000000 | bytes 1000000 | tf_op jit(solution)/shard_map/rows/pallas_call | solution.py:248
  16.0 0.0 collective-permute-done.theirs
  16.0 1.0 %fed.1 = (f32[64,512]{1,0:T(8,128)S(1)}, f32[64,512]{1,0:T(8,128)S(1)}) custom-call(s32[7]{0:T(128)S(1)} %stack.47.flag, f32[128,512]{1,0:T(8,128)S(1)} %scatter.1.mine, f32[128,512]{1,0:T(8,128)} %collective-permute-done.theirs, f32[64,512]{1,0:T(8,128)S(1)} %get-tuple-element.23.one_in, f32[64,512]{1,0:T(8,128)S(1)} %get-tuple-element.24.two_in), custom_call_target="tpu_custom_call" | custom-call | flops 2000000 | bytes 1000000 | tf_op jit(solution)/shard_map/fed/pallas_call | solution.py:248
  17.0 0.1 collective-permute-start.3
  17.1 1.4 %collective-permute-start.4 = (f32[64,512]{1,0:T(8,128)S(1)}, f32[64,512]{1,0:T(8,128)S(1)}, u32[]{:S(2)}, u32[]{:S(2)}) collective-permute-start(f32[64,512]{1,0:T(8,128)S(1)} %get-tuple-element.26), channel_id=1, source_target_pairs={{64,128},{128,64},{192,0},{0,192},{65,129},{129,65},{193,1},{1,193... | collective-permute-start | bytes 393224 | tf_op jit(solution)/shard_map/ppermute | solution.py:604
  18.5 0.0 copy-done.2
  18.5 0.0 copy-done.3
  18.5 1.5 %cols.1 = (f32[144,128]{1,0:T(8,128)S(1)}, f32[144,128]{1,0:T(8,128)S(1)}) custom-call(s32[7]{0:T(128)S(1)} %stack.47.flag, f32[3,128,512]{2,1,0:T(8,128)S(1)} %copy-done.1, f32[3,128,512]{2,1,0:T(8,128)S(1)} %collective-permute-done.1.om, f32[3,128,512]{2,1,0:T(8,128)S(1)} %copy-done, f32[3,128,512]{2,1,0:T(8,128)S(1)} %collective-permute-done.2.os, ...), custom_call_target="tpu_custom_call" | custom-call | flops 2000000 | bytes 1000000 | tf_op jit(solution)/shard_map/cols/pallas_call | solution.py:248
  20.1 2.0 %collective-permute-done.3.rows_one = f32[64,512]{1,0:T(8,128)S(1)} collective-permute-done((f32[64,512]{1,0:T(8,128)S(1)}, f32[64,512]{1,0:T(8,128)S(1)}, u32[]{:S(2)}, u32[]{:S(2)}) %collective-permute-start.3) | collective-permute-done | bytes 131104 | tf_op jit(solution)/shard_map/ppermute | solution.py:604
  22.0 1.3 %collective-permute-done.4.rows_two = f32[64,512]{1,0:T(8,128)S(1)} collective-permute-done((f32[64,512]{1,0:T(8,128)S(1)}, f32[64,512]{1,0:T(8,128)S(1)}, u32[]{:S(2)}, u32[]{:S(2)}) %collective-permute-start.4) | collective-permute-done | bytes 131104 | tf_op jit(solution)/shard_map/ppermute | solution.py:604
  23.3 0.7 corners.1
  24.0 0.9 %collective-permute-start.5 = (f32[144,128]{1,0:T(8,128)S(1)}, f32[144,128]{1,0:T(8,128)S(1)}, u32[]{:S(2)}, u32[]{:S(2)}) collective-permute-start(f32[144,128]{1,0:T(8,128)S(1)} %get-tuple-element.29), channel_id=1, source_target_pairs={{0,2},{2,0},{4,6},{6,4},{8,10},{10,8},{12,14},{14,12},{16,18},{18,... | collective-permute-start | bytes 221192 | tf_op jit(solution)/shard_map/ppermute | solution.py:604
  24.9 6.9 %collective-permute-start.6 = (f32[144,128]{1,0:T(8,128)S(1)}, f32[144,128]{1,0:T(8,128)S(1)}, u32[]{:S(2)}, u32[]{:S(2)}) collective-permute-start(f32[144,128]{1,0:T(8,128)S(1)} %get-tuple-element.30), channel_id=1, source_target_pairs={{2,4},{4,2},{6,8},{8,6},{10,12},{12,10},{14,16},{16,14},{18,20},{2... | collective-permute-start | bytes 221192 | tf_op jit(solution)/shard_map/ppermute | solution.py:604
  31.7 5.5 %links.1 = (f32[6,4,160,128]{3,2,1,0:T(8,128)S(1)}, f32[6,4,160,128]{3,2,1,0:T(8,128)S(1)}, f32[5,4,160,128]{3,2,1,0:T(8,128)S(1)}, f32[6,4,160,128]{3,2,1,0:T(8...) custom-call(s32[7]{0:T(128)S(1)} %stack.47.flag, ...), custom_call_target="tpu_custom_call" | custom-call | flops 80000000 | bytes 12000000 | tf_op jit(solution)/shard_map/links/pallas_call | solution.py:349
  37.2 0.0 collective-permute-done.5.cols_one
  37.2 0.0 collective-permute-done.6.cols_two
  37.2 11.3 %basis.1 = (f32[3,128,512]{2,1,0:T(8,128)S(1)}, f32[3,128,512]{2,1,0:T(8,128)S(1)}, f32[3,128,512]{2,1,0:T(8,128)S(1)}, f32[3,128,512]{2,1,0:T(8,128)S(1)}, f32[...) custom-call(s32[7]{0:T(128)S(1)} %stack.47.flag, f32[144,128]{1,0:T(8,128)S(1)} %collective-permute-done.5.cols_one, ...), custom_call_target="tpu_custom_call" | custom-call | tf_op jit(solution)/shard_map/basis/pallas_call | solution.py:520
  48.5 20.2 %all_to_all.11 = f32[256,1,128]{2,1,0:T(1,128)S(1)} all-to-all(f32[256,1,128]{2,1,0:T(1,128)S(1)} %bitcast.14), channel_id=1, replica_groups=mesh['gx'=4,'gy_0'=4,'gy_1'=8,'layer'=2] {'gx','gy_0','gy_1','layer'}, dimensions={0} | all-to-all | bytes 262144 | tf_op jit(solution)/shard_map/all_to_all | solution.py:645
  68.8 2.2 %update.1 = (f32[3,128,512]{2,1,0:T(8,128)}, f32[3,128,512]{2,1,0:T(8,128)}) custom-call(s32[7]{0:T(128)S(1)} %stack.47.flag, f32[256,128]{1,0:T(8,128)S(1)} %bitcast.13, f32[3,128,512]{2,1,0:T(8,128)S(1)} %copy-done, f32[3,128,512]{2,1,0:T(8,128)S(1)} %get-tuple-element.39.inv, f32[3,128,512]{2,1,0:T(8,128)S(1)} %get-tuple-element.40.r0_ref, ...), custom_call_target="tpu_custom_call" | custom-call | tf_op jit(solution)/shard_map/update/pallas_call | solution.py:585
Async XLA Ops:
  0.6 14.0 %collective-permute-start.1 = (f32[3,128,512]{2,1,0:T(8,128)}, f32[3,128,512]{2,1,0:T(8,128)S(1)}, u32[]{:S(2)}, u32[]{:S(2)}) collective-permute-start(f32[3,128,512]{2,1,0:T(8,128)} %m.5), channel_id=1, source_target_pairs={{0,1},{1,0},{2,3},{3,2},{4,5},{5,4},{6,7},{7,6},{8,9},{9,8},{10,11... | collective-permute-start | bytes 2359304 | tf_op jit(solution)/shard_map/ppermute | solution.py:608
  4.0 10.6 %collective-permute-start.2 = (f32[3,128,512]{2,1,0:T(8,128)}, f32[3,128,512]{2,1,0:T(8,128)S(1)}, u32[]{:S(2)}, u32[]{:S(2)}) collective-permute-start(f32[3,128,512]{2,1,0:T(8,128)} %start.1), channel_id=1, source_target_pairs={{0,1},{1,0},{2,3},{3,2},{4,5},{5,4},{6,7},{7,6},{8,9},{9,8},{10,11... | collective-permute-start | bytes 2359304 | tf_op jit(solution)/shard_map/ppermute | solution.py:608
  4.7 9.9 %copy-start = (f32[3,128,512]{2,1,0:T(8,128)S(1)}, f32[3,128,512]{2,1,0:T(8,128)}, u32[]{:S(2)}) copy-start(f32[3,128,512]{2,1,0:T(8,128)} %start.1) | copy-start | bytes 2359300
  4.7 9.9 %copy-start.1 = (f32[3,128,512]{2,1,0:T(8,128)S(1)}, f32[3,128,512]{2,1,0:T(8,128)}, u32[]{:S(2)}) copy-start(f32[3,128,512]{2,1,0:T(8,128)} %m.5) | copy-start | bytes 2359300
  14.0 2.0 %collective-permute-start = (f32[128,512]{1,0:T(8,128)S(1)}, f32[128,512]{1,0:T(8,128)}, u32[]{:S(2)}, u32[]{:S(2)}) collective-permute-start(f32[128,512]{1,0:T(8,128)S(1)} %scatter.1.mine), channel_id=1, source_target_pairs={{0,1},{1,0},{2,3},{3,2},{4,5},{5,4},{6,7},{7,6},{8,9},{9,8},{10,11... | collective-permute-start | bytes 786440 | tf_op jit(solution)/shard_map/ppermute | solution.py:608
  14.6 4.0 %copy-start.2 = (f32[128,512]{1,0:T(8,128)S(1)}, f32[128,512]{1,0:T(8,128)}, u32[]{:S(2)}) copy-start(f32[128,512]{1,0:T(8,128)} %via.3) | copy-start | bytes 786436
  14.6 4.0 %copy-start.3 = (f32[128,512]{1,0:T(8,128)S(1)}, f32[128,512]{1,0:T(8,128)}, u32[]{:S(2)}) copy-start(f32[128,512]{1,0:T(8,128)} %pad.3) | copy-start | bytes 786436
  17.0 5.0 %collective-permute-start.3 = (f32[64,512]{1,0:T(8,128)S(1)}, f32[64,512]{1,0:T(8,128)S(1)}, u32[]{:S(2)}, u32[]{:S(2)}) collective-permute-start(f32[64,512]{1,0:T(8,128)S(1)} %get-tuple-element.25), channel_id=1, source_target_pairs={{0,64},{64,0},{128,192},{192,128},{1,65},{65,1},{129,193},{193,129... | collective-permute-start | bytes 393224 | tf_op jit(solution)/shard_map/ppermute | solution.py:604
  17.1 6.2 %collective-permute-start.4 = (f32[64,512]{1,0:T(8,128)S(1)}, f32[64,512]{1,0:T(8,128)S(1)}, u32[]{:S(2)}, u32[]{:S(2)}) collective-permute-start(f32[64,512]{1,0:T(8,128)S(1)} %get-tuple-element.26), channel_id=1, source_target_pairs={{64,128},{128,64},{192,0},{0,192},{65,129},{129,65},{193,1},{1,193... | collective-permute-start | bytes 393224 | tf_op jit(solution)/shard_map/ppermute | solution.py:604
  24.0 13.2 %collective-permute-start.5 = (f32[144,128]{1,0:T(8,128)S(1)}, f32[144,128]{1,0:T(8,128)S(1)}, u32[]{:S(2)}, u32[]{:S(2)}) collective-permute-start(f32[144,128]{1,0:T(8,128)S(1)} %get-tuple-element.29), channel_id=1, source_target_pairs={{0,2},{2,0},{4,6},{6,4},{8,10},{10,8},{12,14},{14,12},{16,18},{18,... | collective-permute-start | bytes 221192 | tf_op jit(solution)/shard_map/ppermute | solution.py:604
  24.9 12.3 %collective-permute-start.6 = (f32[144,128]{1,0:T(8,128)S(1)}, f32[144,128]{1,0:T(8,128)S(1)}, u32[]{:S(2)}, u32[]{:S(2)}) collective-permute-start(f32[144,128]{1,0:T(8,128)S(1)} %get-tuple-element.30), channel_id=1, source_target_pairs={{2,4},{4,2},{6,8},{8,6},{10,12},{12,10},{14,16},{16,14},{18,20},{2... | collective-permute-start | bytes 221192 | tf_op jit(solution)/shard_map/ppermute | solution.py:604
